TPU v7x, 32 devices: a whole 2x2x4 slice. The times are simulated.
32 devices in a mesh: dp: 4 (over y, core), seq: 2 (over x), tensor: 4 (over z).
Axes of the slice: x: 2, y: 2, z: 4, core: 2. Of those that a mesh axis runs over, the one named last changes fastest.
Arguments:
- hidden_in: bfloat16 [4, 1024, 1024], P('dp', ('seq', 'tensor')), may hold values from -6 to 6
- cotangent: bfloat16 [4, 1024, 1024], P('dp', ('seq', 'tensor')), may hold values from -6 to 6
- piece_starts: int32 [4, 2], P('dp'), may hold values from 0 to 768, as said below
- expert_ids: int32 [4, 1024, 8], P('dp', 'seq'), may hold values from 0 to 15, all different within a row
- claim_order: int32 [4, 1024], P('dp', 'seq'), may hold values from 0 to 511, as said below
- first_gain: bfloat16 [1024], P(('dp', 'seq', 'tensor')), may hold values from 0.25 to 1.75
- second_gain: bfloat16 [1024], P(('dp', 'seq', 'tensor')), may hold values from 0.25 to 1.75
- router: bfloat16 [1024, 16], P(('dp', 'seq', 'tensor')), may hold values from -0.09375 to 0.09375
- w_query: bfloat16 [1024, 1024], P(('dp', 'seq'), 'tensor'), may hold values from -0.25 to 0.25
- key_projection: bfloat16 [1024, 512], P(('dp', 'seq'), 'tensor'), may hold values from -0.25 to 0.25
- value_projection: bfloat16 [1024, 512], P(('dp', 'seq'), 'tensor'), may hold values from -0.1875 to 0.1875
- w_out: bfloat16 [1024, 1024], P(('dp', 'seq'), 'tensor'), may hold values from -1.5 to 1.5
- w_gate: bfloat16 [16, 1024, 512], P(None, ('dp', 'seq'), 'tensor'), may hold values from -0.1875 to 0.1875
- w_up: bfloat16 [16, 1024, 512], P(None, ('dp', 'seq'), 'tensor'), may hold values from -0.1875 to 0.1875
- w_down: bfloat16 [16, 1024, 512], P(None, ('dp', 'seq'), 'tensor'), may hold values from -1 to 1
Outputs:
- output: bfloat16 [4, 1024, 1024], P('dp', ('seq', 'tensor'))
- input_grad: bfloat16 [4, 1024, 1024], P('dp', ('seq', 'tensor'))
- query_grad: float32 [1024, 1024], P(('dp', 'seq'), 'tensor')
- key_grad: float32 [1024, 512], P(('dp', 'seq'), 'tensor')
- value_grad: float32 [1024, 512], P(('dp', 'seq'), 'tensor')
- out_grad: float32 [1024, 1024], P(('dp', 'seq'), 'tensor')
- gate_grad: float32 [16, 1024, 512], P(None, ('dp', 'seq'), 'tensor')
- up_grad: float32 [16, 1024, 512], P(None, ('dp', 'seq'), 'tensor')
- down_grad: float32 [16, 1024, 512], P(None, ('dp', 'seq'), 'tensor')
- first_gain_grad: float32 [1024], P(('dp', 'seq', 'tensor'))
- second_gain_grad: float32 [1024], P(('dp', 'seq', 'tensor'))
- router_grad: float32 [1024, 16], P(('dp', 'seq', 'tensor'))
Inputs may be any that keep to these rules, and one draw needn't show every extreme that they name: `piece_starts`: pieces of a sequence come in increasing order and don't intersect. `claim_order`: within each dispatch group the 512 values are a permutation. `expert_ids`: a token names 8 different experts.
All inputs are finite; a program needn't handle non-finite values.
Results may differ from a plain program's by a relative error of at most 0.028.
Values may be sent and summed in bfloat16 or wider, within the bound.
No kernel may reach another device: no remote copies, remote signals or barrier semaphores. Data moves between devices by JAX's collectives and lax.ppermute only.
A program may use at most 320 MiB of HBM per device.

v0:
```python
import math

import jax
import jax.numpy as jnp
from jax import lax
from jax.sharding import PartitionSpec as P

HEAD_SIZE = 64
E = 16
PIECE = 256
CAP = 320


highest = lax.Precision.HIGHEST
norm_eps = 1e-06
masked_fill = -1e30


def rms_scale(value_rows, gain):
    return (
        value_rows
        * lax.rsqrt(jnp.mean(value_rows * value_rows, axis=-1, keepdims=True) + norm_eps)
        * gain
    )


def norm_back(value_rows, gain, upstream):
    inverse = lax.rsqrt(jnp.mean(value_rows * value_rows, axis=-1, keepdims=True) + norm_eps)
    normal = value_rows * inverse
    scaled = upstream * gain
    grad = inverse * (scaled - normal * jnp.mean(scaled * normal, axis=-1, keepdims=True))
    return (grad, jnp.sum(upstream * normal, axis=(0, 1)))


def rotary(value_rows, positions, sign):
    half = HEAD_SIZE // 2
    index = jnp.arange(half).astype(jnp.float32)
    freqs = jnp.exp(index * (-2.0 * math.log(10000.0) / HEAD_SIZE))
    angles = positions.astype(jnp.float32)[:, None] * freqs[None, :]
    cosine = jnp.cos(angles)[:, None, :]
    sine = sign * jnp.sin(angles)[:, None, :]
    shaped = value_rows.reshape(
        value_rows.shape[:-1] + (value_rows.shape[-1] // HEAD_SIZE, HEAD_SIZE)
    )
    leading = shaped[..., :half]
    second = shaped[..., half:]
    turned = jnp.concatenate(
        [leading * cosine - second * sine, second * cosine + leading * sine], axis=-1
    )
    return turned.reshape(value_rows.shape)


def piece_ids(positions, starts):
    inside = (positions[..., :, None] >= starts[..., None, :]) & (
        positions[..., :, None] < starts[..., None, :] + PIECE
    )
    labels = jnp.arange(1, starts.shape[-1] + 1, dtype=jnp.int32)
    return jnp.max(jnp.where(inside, labels, 0), axis=-1) - 1


def allowed_pairs(query_pos, query_ids, key_pos, key_ids):
    causal = key_pos[:, None, :] <= query_pos[:, :, None]
    same_piece = (query_ids[:, :, None] == key_ids[:, None, :]) & (query_ids[:, :, None] >= 0)
    return causal | same_piece


def route_slots(expert_ids, claim, count):
    experts = jnp.arange(E, dtype=jnp.int32)
    chosen = jnp.sum(
        (expert_ids[:, :, None] == experts[None, None, :]).astype(jnp.int32),
        axis=1,
        dtype=jnp.int32,
    )
    order = jnp.zeros((count,), jnp.int32).at[claim].set(jnp.arange(count, dtype=jnp.int32))
    ranked = chosen[order]
    earlier = jnp.cumsum(ranked, axis=0, dtype=jnp.int32) - ranked
    place = jnp.take_along_axis(earlier[claim], expert_ids, axis=1)
    slot = jnp.where(place < CAP, expert_ids * CAP + place, E * CAP)
    owner = jnp.broadcast_to(jnp.arange(count, dtype=jnp.int32)[:, None], expert_ids.shape)
    slot_token = (
        jnp.full((E * CAP,), count, jnp.int32)
        .at[slot.reshape(-1)]
        .set(owner.reshape(-1), mode="drop")
    )
    return (slot, slot_token)


def combine_slots(slot_rows, slot):
    picked = jnp.take(slot_rows, slot, axis=0, mode="fill", fill_value=0.0)
    return jnp.sum(picked, axis=1)


def spread_rows(row_values):
    return lax.all_gather(row_values, "tensor", axis=1, tiled=True)


def collect_rows(terms):
    return lax.psum_scatter(
        terms.astype(jnp.bfloat16), "tensor", scatter_dimension=1, tiled=True
    ).astype(jnp.float32)


def per_device(
    hidden_in,
    cotangent,
    piece_starts,
    expert_ids,
    claim_order,
    first_gain,
    second_gain,
    router,
    w_query,
    key_projection,
    value_projection,
    w_out,
    w_gate,
    w_up,
    w_down,
):
    gain_one, gain_two, router_full = (
        lax.all_gather(first_gain, ("dp", "seq", "tensor"), axis=0, tiled=True),
        lax.all_gather(second_gain, ("dp", "seq", "tensor"), axis=0, tiled=True),
        lax.all_gather(router, ("dp", "seq", "tensor"), axis=0, tiled=True),
    )
    gain_one = gain_one.astype(jnp.float32)
    gain_two = gain_two.astype(jnp.float32)
    seq_count = hidden_in.shape[0]
    width = hidden_in.shape[2]
    tok_seq = expert_ids.shape[1]
    length = tok_seq * lax.axis_size("seq")
    count = seq_count * tok_seq
    scale = HEAD_SIZE ** (-0.5)
    positions = lax.axis_index("seq") * tok_seq + jnp.arange(tok_seq, dtype=jnp.int32)
    query_pos = jnp.broadcast_to(positions, (seq_count, tok_seq))
    query_ids = piece_ids(query_pos, piece_starts)
    inputs = hidden_in.astype(jnp.float32)
    query_matrix, key_matrix, value_matrix, output_matrix = (
        lax.all_gather(w_query, ("dp", "seq"), axis=0, tiled=True),
        lax.all_gather(key_projection, ("dp", "seq"), axis=0, tiled=True),
        lax.all_gather(value_projection, ("dp", "seq"), axis=0, tiled=True),
        lax.all_gather(w_out, ("dp", "seq"), axis=0, tiled=True),
    )
    normed_every_row = spread_rows(rms_scale(inputs, gain_one).astype(jnp.bfloat16))
    query_before_rotary = jnp.einsum(
        "khi,iy->khy", normed_every_row, query_matrix, preferred_element_type=jnp.float32
    )
    key_before_rotary = jnp.einsum(
        "khi,iy->khy", normed_every_row, key_matrix, preferred_element_type=jnp.float32
    )
    value_before_rotary = jnp.einsum(
        "khi,iy->khy", normed_every_row, value_matrix, preferred_element_type=jnp.float32
    )
    query_rows = rotary(query_before_rotary, positions, 1.0).astype(jnp.bfloat16)
    key_rows = rotary(key_before_rotary, positions, 1.0).astype(jnp.bfloat16)
    value_rows = value_before_rotary.astype(jnp.bfloat16)
    heads_of_key = key_matrix.shape[1] // HEAD_SIZE
    group_width = query_matrix.shape[1] // key_matrix.shape[1]
    query_heads = query_rows.reshape(seq_count, tok_seq, heads_of_key, group_width, HEAD_SIZE)

    def score_block(key_blk, first_pos, expert_block):
        key_pos = jnp.broadcast_to(
            first_pos + jnp.arange(expert_block, dtype=jnp.int32), (seq_count, expert_block)
        )
        allowed = allowed_pairs(query_pos, query_ids, key_pos, piece_ids(key_pos, piece_starts))
        scores = (
            jnp.einsum(
                "sqgrd,skgd->sgrqk", query_heads, key_blk, preferred_element_type=jnp.float32
            )
            * scale
        )
        return (scores, allowed[:, None, None])

    stat_shape = (seq_count, heads_of_key, group_width, tok_seq)
    start_state = (
        jnp.full(stat_shape, masked_fill, jnp.float32),
        jnp.zeros(stat_shape, jnp.float32),
        jnp.zeros(stat_shape + (HEAD_SIZE,), jnp.float32),
    )
    key_piece = lax.all_gather(key_rows, "seq", axis=1, tiled=True)
    value_piece = lax.all_gather(value_rows, "seq", axis=1, tiled=True)
    span = key_piece.shape[1]
    attend_expert_block = 256

    def one_block(state, index):
        top, total, accum = state
        leading = index * attend_expert_block
        key_blk = lax.dynamic_slice_in_dim(key_piece, leading, attend_expert_block, 1).reshape(
            seq_count, attend_expert_block, heads_of_key, HEAD_SIZE
        )
        value_blk = lax.dynamic_slice_in_dim(value_piece, leading, attend_expert_block, 1).reshape(
            seq_count, attend_expert_block, heads_of_key, HEAD_SIZE
        )
        scores, allowed = score_block(key_blk, leading, attend_expert_block)
        scores = jnp.where(allowed, scores, masked_fill)
        new_top = jnp.maximum(top, jnp.max(scores, axis=-1))
        weights = jnp.where(allowed, jnp.exp(scores - new_top[..., None]), 0.0)
        shrink = jnp.exp(top - new_top)
        total = total * shrink + jnp.sum(weights, axis=-1)
        accum = accum * shrink[..., None] + jnp.einsum(
            "sgrqk,skgd->sgrqd",
            weights.astype(jnp.bfloat16),
            value_blk,
            preferred_element_type=jnp.float32,
        )
        return ((new_top, total, accum), None)

    final, unused = lax.scan(one_block, start_state, jnp.arange(span // attend_expert_block))
    top, total, accum = final
    log_total = top + jnp.log(total)
    mixed = jnp.transpose(accum / total[..., None], (0, 3, 1, 2, 4))
    mixed_reduced = mixed.reshape(seq_count, tok_seq, -1).astype(jnp.bfloat16)
    branch = collect_rows(
        jnp.einsum("pfy,ry->pfr", mixed_reduced, output_matrix, preferred_element_type=jnp.float32)
    )
    middle = inputs + branch
    second_all = spread_rows(rms_scale(middle, gain_two).astype(jnp.bfloat16))
    flat_second = second_all.reshape(count, width)
    logits = jnp.dot(flat_second, router_full, preferred_element_type=jnp.float32)
    flat_ids = expert_ids.reshape(count, -1)
    gates = jax.nn.softmax(jnp.take_along_axis(logits, flat_ids, axis=1), axis=-1)
    slot, slot_token = route_slots(flat_ids, claim_order.reshape(count), count)
    slot_gate = (
        jnp.zeros((E * CAP,), jnp.float32).at[slot.reshape(-1)].set(gates.reshape(-1), mode="drop")
    )
    shares_all = slot_gate.reshape(E, CAP)
    taken_all = jnp.take(flat_second, slot_token, axis=0, mode="fill", fill_value=0).reshape(
        E, CAP, width
    )
    gate_w, up_w, down_w = (
        lax.all_gather(w_gate, ("dp", "seq"), axis=1, tiled=True),
        lax.all_gather(w_up, ("dp", "seq"), axis=1, tiled=True),
        lax.all_gather(w_down, ("dp", "seq"), axis=1, tiled=True),
    )

    def expert_forward(unused_carry, parts):
        gate_e, up_e, down_e, taken = parts
        gate_pre = jnp.dot(taken, gate_e, preferred_element_type=jnp.float32)
        up_pre = jnp.dot(taken, up_e, preferred_element_type=jnp.float32)
        active = (jax.nn.silu(gate_pre) * up_pre).astype(jnp.bfloat16)
        slot_out = lax.dot_general(
            active, down_e, (((1,), (1,)), ((), ())), preferred_element_type=jnp.float32
        )
        return (unused_carry, (slot_out, gate_pre, up_pre, active))

    unused_final, (slot_outs, gate_pres, up_pres, actives) = lax.scan(
        expert_forward, jnp.zeros((), jnp.float32), (gate_w, up_w, down_w, taken_all)
    )
    weighted_slots = slot_outs.reshape(E * CAP, width) * slot_gate[:, None]
    experts_part = combine_slots(weighted_slots, slot)
    experts_out = collect_rows(experts_part.reshape(seq_count, tok_seq, width))
    output = (middle + experts_out).astype(jnp.bfloat16)
    flat_grad = spread_rows(cotangent).reshape(count, width)
    grad_taken_all = jnp.take(flat_grad, slot_token, axis=0, mode="fill", fill_value=0).reshape(
        E, CAP, width
    )

    def expert_backward(unused_carry, parts):
        gate_e, up_e, down_e, taken, grad_tok, shares, gate_pre, up_pre, active = parts
        scaled = (grad_tok.astype(jnp.float32) * shares[:, None]).astype(jnp.bfloat16)
        active_grad = jnp.dot(scaled, down_e, preferred_element_type=jnp.float32)
        plain = jnp.dot(grad_tok, down_e, preferred_element_type=jnp.float32)
        share_grad = jnp.sum(active.astype(jnp.float32) * plain, axis=-1)
        down_wgrad = lax.dot_general(
            scaled, active, (((0,), (0,)), ((), ())), preferred_element_type=jnp.float32
        )
        sigmoid_gate = jax.nn.sigmoid(gate_pre)
        gate_pre_grad = (
            active_grad * up_pre * sigmoid_gate * (1.0 + gate_pre * (1.0 - sigmoid_gate))
        ).astype(jnp.bfloat16)
        up_pre_grad = (active_grad * gate_pre * sigmoid_gate).astype(jnp.bfloat16)
        taken_grad = lax.dot_general(
            gate_pre_grad, gate_e, (((1,), (1,)), ((), ())), preferred_element_type=jnp.float32
        )
        taken_grad = taken_grad + lax.dot_general(
            up_pre_grad, up_e, (((1,), (1,)), ((), ())), preferred_element_type=jnp.float32
        )
        gate_wgrad = lax.dot_general(
            taken, gate_pre_grad, (((0,), (0,)), ((), ())), preferred_element_type=jnp.float32
        )
        up_wgrad = lax.dot_general(
            taken, up_pre_grad, (((0,), (0,)), ((), ())), preferred_element_type=jnp.float32
        )
        return (unused_carry, (taken_grad, gate_wgrad, up_wgrad, down_wgrad, share_grad))

    unused_back, (taken_grads, gate_wgrads, up_wgrads, down_wgrads, share_grads) = lax.scan(
        expert_backward,
        jnp.zeros((), jnp.float32),
        (gate_w, up_w, down_w, taken_all, grad_taken_all, shares_all, gate_pres, up_pres, actives),
    )
    second_grad = combine_slots(taken_grads.reshape(E * CAP, width), slot)
    pair_grad = jnp.take(share_grads.reshape(-1), slot, axis=0, mode="fill", fill_value=0.0)
    chosen_grad = gates * (pair_grad - jnp.sum(gates * pair_grad, axis=-1, keepdims=True))
    experts = jnp.arange(E, dtype=jnp.int32)
    logit_grad = jnp.sum(
        chosen_grad[:, :, None]
        * (flat_ids[:, :, None] == experts[None, None, :]).astype(jnp.float32),
        axis=1,
    )
    router_f = router_full.astype(jnp.float32)
    second_grad = second_grad + jnp.dot(logit_grad, router_f.T, precision=highest)
    router_wgrad = jnp.dot(flat_second.astype(jnp.float32).T, logit_grad, precision=highest)
    second_rows = collect_rows(second_grad.reshape(seq_count, tok_seq, width))
    middle_norm_grad, gain_two_grad = norm_back(middle, gain_two, second_rows)
    middle_grad = cotangent.astype(jnp.float32) + middle_norm_grad
    branch_gradient = spread_rows(middle_grad.astype(jnp.bfloat16))
    mixed_grad = jnp.einsum(
        "khi,iy->khy", branch_gradient, output_matrix, preferred_element_type=jnp.float32
    ).astype(jnp.bfloat16)
    out_wgrad = jnp.einsum(
        "qvz,qvo->zo", branch_gradient, mixed_reduced, preferred_element_type=jnp.float32
    )
    mixed_heads_grad = mixed_grad.reshape(seq_count, tok_seq, heads_of_key, group_width, HEAD_SIZE)
    delta = jnp.einsum("sqgrd,sqgrd->sgrq", mixed_heads_grad.astype(jnp.float32), mixed)
    keys_all, values_all = (
        lax.all_gather(key_rows, "seq", axis=1, tiled=True),
        lax.all_gather(value_rows, "seq", axis=1, tiled=True),
    )
    expert_block = 256

    def block_terms(index):
        leading = index * expert_block
        key_blk = lax.dynamic_slice_in_dim(keys_all, leading, expert_block, 1).reshape(
            seq_count, expert_block, heads_of_key, HEAD_SIZE
        )
        value_blk = lax.dynamic_slice_in_dim(values_all, leading, expert_block, 1).reshape(
            seq_count, expert_block, heads_of_key, HEAD_SIZE
        )
        scores, allowed = score_block(key_blk, leading, expert_block)
        weights = jnp.where(allowed, jnp.exp(scores - log_total[..., None]), 0.0)
        weight_grad = jnp.einsum(
            "sqgrd,skgd->sgrqk", mixed_heads_grad, value_blk, preferred_element_type=jnp.float32
        )
        score_grad = (weights * (weight_grad - delta[..., None])).astype(jnp.bfloat16)
        query_part = (
            jnp.einsum("sgrqk,skgd->sqgrd", score_grad, key_blk, preferred_element_type=jnp.float32)
            * scale
        )
        return (weights, score_grad, query_part)

    def back_block(query_grad, index):
        weights, score_grad, query_part = block_terms(index)
        value_part = jnp.einsum(
            "sgrqk,sqgrd->skgd",
            weights.astype(jnp.bfloat16),
            mixed_heads_grad,
            preferred_element_type=jnp.float32,
        )
        key_part = (
            jnp.einsum(
                "sgrqk,sqgrd->skgd", score_grad, query_heads, preferred_element_type=jnp.float32
            )
            * scale
        )
        return (
            query_grad + query_part,
            (
                key_part.reshape(seq_count, expert_block, -1),
                value_part.reshape(seq_count, expert_block, -1),
            ),
        )

    query_grad, (key_parts, value_parts) = lax.scan(
        back_block, jnp.zeros(query_heads.shape, jnp.float32), jnp.arange(length // expert_block)
    )
    key_full = jnp.moveaxis(key_parts, 0, 1).reshape(seq_count, length, -1)
    value_full = jnp.moveaxis(value_parts, 0, 1).reshape(seq_count, length, -1)
    key_own, value_own = (
        lax.psum_scatter(
            key_full.astype(jnp.bfloat16), "seq", scatter_dimension=1, tiled=True
        ).astype(jnp.float32),
        lax.psum_scatter(
            value_full.astype(jnp.bfloat16), "seq", scatter_dimension=1, tiled=True
        ).astype(jnp.float32),
    )
    query_before_rotary_gradient = rotary(
        query_grad.reshape(seq_count, tok_seq, -1), positions, -1.0
    ).astype(jnp.bfloat16)
    key_before_rotary_gradient = rotary(key_own, positions, -1.0).astype(jnp.bfloat16)
    value_before_rotary_gradient = value_own.astype(jnp.bfloat16)
    normed_grad = jnp.einsum(
        "pfy,ry->pfr",
        query_before_rotary_gradient,
        query_matrix,
        preferred_element_type=jnp.float32,
    )
    normed_grad = normed_grad + jnp.einsum(
        "pfy,ry->pfr", key_before_rotary_gradient, key_matrix, preferred_element_type=jnp.float32
    )
    normed_grad = normed_grad + jnp.einsum(
        "pfy,ry->pfr",
        value_before_rotary_gradient,
        value_matrix,
        preferred_element_type=jnp.float32,
    )
    query_wgrad = jnp.einsum(
        "qvz,qvo->zo",
        normed_every_row,
        query_before_rotary_gradient,
        preferred_element_type=jnp.float32,
    )
    key_wgrad = jnp.einsum(
        "qvz,qvo->zo",
        normed_every_row,
        key_before_rotary_gradient,
        preferred_element_type=jnp.float32,
    )
    value_wgrad = jnp.einsum(
        "qvz,qvo->zo",
        normed_every_row,
        value_before_rotary_gradient,
        preferred_element_type=jnp.float32,
    )
    normed_rows = collect_rows(normed_grad)
    input_norm_grad, gain_one_grad = norm_back(inputs, gain_one, normed_rows)
    input_grad = (middle_grad + input_norm_grad).astype(jnp.bfloat16)
    query_out, key_out, value_out, out_out = (
        lax.psum_scatter(
            query_wgrad.astype(jnp.bfloat16), ("dp", "seq"), scatter_dimension=0, tiled=True
        ).astype(jnp.float32),
        lax.psum_scatter(
            key_wgrad.astype(jnp.bfloat16), ("dp", "seq"), scatter_dimension=0, tiled=True
        ).astype(jnp.float32),
        lax.psum_scatter(
            value_wgrad.astype(jnp.bfloat16), ("dp", "seq"), scatter_dimension=0, tiled=True
        ).astype(jnp.float32),
        lax.psum_scatter(
            out_wgrad.astype(jnp.bfloat16), ("dp", "seq"), scatter_dimension=0, tiled=True
        ).astype(jnp.float32),
    )
    gate_out, up_out, down_out = (
        lax.psum_scatter(
            gate_wgrads.astype(jnp.bfloat16), ("dp", "seq"), scatter_dimension=1, tiled=True
        ).astype(jnp.float32),
        lax.psum_scatter(
            up_wgrads.astype(jnp.bfloat16), ("dp", "seq"), scatter_dimension=1, tiled=True
        ).astype(jnp.float32),
        lax.psum_scatter(
            down_wgrads.astype(jnp.bfloat16), ("dp", "seq"), scatter_dimension=1, tiled=True
        ).astype(jnp.float32),
    )
    gain_one_out, gain_two_out, router_out = (
        lax.psum_scatter(gain_one_grad, ("dp", "seq", "tensor"), scatter_dimension=0, tiled=True),
        lax.psum_scatter(gain_two_grad, ("dp", "seq", "tensor"), scatter_dimension=0, tiled=True),
        lax.psum_scatter(router_wgrad, ("dp", "seq", "tensor"), scatter_dimension=0, tiled=True),
    )
    return (
        output,
        input_grad,
        query_out,
        key_out,
        value_out,
        out_out,
        gate_out,
        up_out,
        down_out,
        gain_one_out,
        gain_two_out,
        router_out,
    )


def solution(mesh):
    placed = (
        P("dp", ("seq", "tensor"), None),
        P("dp", ("seq", "tensor"), None),
        P("dp", None),
        P("dp", "seq", None),
        P("dp", "seq"),
        P(("dp", "seq", "tensor")),
        P(("dp", "seq", "tensor")),
        P(("dp", "seq", "tensor"), None),
        P(("dp", "seq"), "tensor"),
        P(("dp", "seq"), "tensor"),
        P(("dp", "seq"), "tensor"),
        P(("dp", "seq"), "tensor"),
        P(None, ("dp", "seq"), "tensor"),
        P(None, ("dp", "seq"), "tensor"),
        P(None, ("dp", "seq"), "tensor"),
    )
    return jax.shard_map(
        per_device,
        mesh=mesh,
        in_specs=placed,
        out_specs=(
            P("dp", ("seq", "tensor"), None),
            P("dp", ("seq", "tensor"), None),
            P(("dp", "seq"), "tensor"),
            P(("dp", "seq"), "tensor"),
            P(("dp", "seq"), "tensor"),
            P(("dp", "seq"), "tensor"),
            P(None, ("dp", "seq"), "tensor"),
            P(None, ("dp", "seq"), "tensor"),
            P(None, ("dp", "seq"), "tensor"),
            P(("dp", "seq", "tensor")),
            P(("dp", "seq", "tensor")),
            P(("dp", "seq", "tensor"), None),
        ),
        check_vma=False,
    )
```

profile of v0, /device:TPU:0, one launch (start us, length us, event | category | flops | bytes accessed | tf_op | source)
XLA Modules:
  0.0 1583.4 jit_solution(1462444075174308908)
XLA Ops:
  9.0 42.0 %all-reduce.5 = (bf16[1024]{0:T(1024)(128)(2,1)S(1)}, bf16[1024]{0:T(1024)(128)(2,1)S(1)}) all-reduce(bf16[1024]{0:T(1024)(128)(2,1)S(1)} %dynamic-update-slice, bf16[1024]{0:T(1024)(128)(2,1)S(1)} %dynamic-update-slice.1), channel_id=1, replica_groups=mesh['dp'=4,'seq'=2,'tensor'=4] {'dp','seq','tensor'}, use_global_device_ids=true, to_apply=%add | all-reduce | flops 2048 | bytes 8192
  142.5 39.0 %while.70 = (s32[]{:T(128)}, f32[1,2,2,512]{3,2,1,0:T(2,128)S(1)}, f32[1,2,2,512]{3,2,1,0:T(2,128)}, f32[1,2,2,512,64]{3,4,2,1,0:T(8,128)S(1)}, s32[4]{0:T(128)}...) while((s32[]{:T(128)}, f32[1,2,2,512]{3,2,1,0:T(2,128)S(1)}, ...), condition=%wide.region_6.7_spmd.clone, body=%wide.region_2.6_spmd.clone.sunk | while | flops 141967104 | bytes 8732999 | solution.py:207
  184.6 25.6 %reduce-scatter.17.cloned.1.call-done = bf16[1,128,1024]{2,1,0:T(8,128)(2,1)} async-done(((bf16[1,512,1024]{2,1,0:T(8,128)(2,1)}), bf16[1,128,1024]{2,1,0:T(8,128)(2,1)}) %reduce-scatter.17.cloned.1.call-update) | async-done | bytes 262160 | tf_op jit(solution)/shard_map/reduce_scatter | solution.py:98
  223.1 26.7 %gather_fusion.3 = s32[4096]{0:T(1024)S(1)} fusion(s32[512,16]{1,0:T(8,128)S(1)} %gather_fusion.1, s32[4096]{0:T(1024)S(1)} %reshape.1684), kind=kCustom, calls=%fused_computation.7 | custom fusion | bytes 65536 | tf_op jit(solution)/shard_map/jit(take_along_axis)/gather | solution.py:77
  250.3 67.9 %all-gather.1 = bf16[32,32,16]{1,2,0:T(8,128)(2,1)S(1)} all-gather(bf16[1,32,16]{1,2,0:T(8,128)(2,1)S(1)} %bitcast.586), channel_id=1, replica_groups=mesh['dp'=4,'seq'=2,'tensor'=4] {'dp','seq','tensor'}, dimensions={0}, use_global_device_ids=true | all-gather | bytes 33792 | tf_op jit(solution)/shard_map/all_gather | solution.py:123
  335.7 27.2 %gather_fusion.7 = bf16[5120,1024]{1,0:T(8,128)(2,1)} fusion(bf16[512,1024]{1,0:T(8,128)(2,1)} %bitcast.537, s32[5120]{0:T(1024)S(1)} %fusion.136), kind=kCustom, calls=%fused_computation.2.clone | custom fusion | bytes 20992000 | tf_op jit(solution)/shard_map/jit(_take)/gather | solution.py:253
  362.9 27.3 %gather_fusion.5 = bf16[5120,1024]{1,0:T(8,128)(2,1)} fusion(bf16[512,1024]{1,0:T(8,128)(2,1)} %bitcast.536, s32[5120]{0:T(1024)S(1)} %fusion.136), kind=kCustom, calls=%fused_computation.clone | custom fusion | bytes 20992000 | tf_op jit(solution)/shard_map/jit(_take)/gather | solution.py:226
  390.6 33.0 %gather_fusion.4 = f32[4096]{0:T(1024)S(1)} fusion(f32[512,16]{0,1:T(8,128)S(1)} %fusion.150, s32[4096]{0:T(1024)S(1)} %reshape.1684), kind=kCustom, calls=%fused_computation.8 | custom fusion | bytes 65536 | tf_op jit(solution)/shard_map/jit(take_along_axis)/gather | solution.py:220
  465.8 117.2 %while.68 = (s32[]{:T(128)}, f32[16,320,1024]{2,1,0:T(8,128)}, f32[16,320,128]{2,1,0:T(8,128)}, f32[16,320,128]{2,1,0:T(8,128)}, bf16[16,320,128]{2,1,0:T(8,128)...) while((s32[]{:T(128)}, f32[16,320,1024]{2,1,0:T(8,128)}, ...), condition=%wide.region_15.17_spmd, body=%wide.region_14.16_spmd.sunk | while | flops 251904000 | bytes 4641381 | solution.py:245
  592.6 220.4 %while.69 = (s32[]{:T(128)}, f32[16,320,1024]{2,1,0:T(8,128)}, bf16[16,1024,128]{2,1,0:T(8,128)(2,1)}, bf16[16,1024,128]{2,1,0:T(8,128)(2,1)}, bf16[16,1024,128]...) while((s32[]{:T(128)}, f32[16,320,1024]{2,1,0:T(8,128)}, ...), condition=%wide.region_23.26_spmd, body=%wide.region_21.25_spmd.sunk | while | flops 590151360 | bytes 10833317 | solution.py:285
  852.7 29.4 %gather_fusion.6 = f32[4096,1024]{1,0:T(8,128)} fusion(f32[5120,1024]{1,0:T(8,128)} %bitcast_multiply_fusion.3, s32[4096]{0:T(1024)S(1)} %broadcast_clamp_fusion.1), kind=kCustom, calls=%fused_computation.1.clone | custom fusion | bytes 33570816 | tf_op jit(solution)/shard_map/jit(_take)/gather | solution.py:89
  882.1 29.3 %gather_fusion.8 = f32[4096,1024]{1,0:T(8,128)} fusion(f32[5120,1024]{1,0:T(8,128)} %bitcast.538, s32[4096]{0:T(1024)S(1)} %broadcast_clamp_fusion.1), kind=kCustom, calls=%fused_computation.3.clone | custom fusion | bytes 33570816 | tf_op jit(solution)/shard_map/jit(_take)/gather | solution.py:89
  960.4 25.9 %all-gather.22.cloned.1.call-done = bf16[1,512,1024]{2,1,0:T(8,128)(2,1)} async-done(((bf16[1,128,1024]{2,1,0:T(8,128)(2,1)}), bf16[1,512,1024]{2,1,0:T(8,128)(2,1)}) %all-gather.22.cloned.1.call-update) | async-done | bytes 1048592 | tf_op jit(solution)/shard_map/all_gather | solution.py:94
  988.6 53.7 %while.71 = (s32[]{:T(128)}, f32[1,512,2,2,64]{1,4,3,2,0:T(8,128)S(1)}, bf16[4,1,256,128]{3,2,0,1:T(8,128)(2,1)}, bf16[4,1,256,128]{3,2,0,1:T(8,128)(2,1)}, s32[...) while((s32[]{:T(128)}, ...), condition=%wide.region_31.34_spmd.clone, body=%wide.region_29.33_spmd.clone.sunk | while | flops 340201216 | bytes 21332804 | solution.py:362
  1076.8 129.8 %reduce-scatter.43.cloned.1.call-done = f32[32,16]{1,0:T(8,128)} async-done(((f32[1024,16]{1,0:T(8,128)}), f32[32,16]{1,0:T(8,128)}) %reduce-scatter.43.cloned.1.call-update) | async-done | bytes 2064
  1208.0 32.8 %reduce-scatter.35.cloned.1.call-done = bf16[128,256]{1,0:T(8,128)(2,1)} async-done(((bf16[1024,256]{1,0:T(8,128)(2,1)}), bf16[128,256]{1,0:T(8,128)(2,1)}) %reduce-scatter.35.cloned.1.call-update) | async-done | bytes 65552 | tf_op jit(solution)/shard_map/reduce_scatter | solution.py:426
  1242.3 36.1 %reduce-scatter.29.cloned.1.call-done = bf16[128,256]{1,0:T(8,128)(2,1)} async-done(((bf16[1024,256]{1,0:T(8,128)(2,1)}), bf16[128,256]{1,0:T(8,128)(2,1)}) %reduce-scatter.29.cloned.1.call-update) | async-done | bytes 65552 | tf_op jit(solution)/shard_map/reduce_scatter | solution.py:417
  1280.0 35.7 %reduce-scatter.31.cloned.1.call-done = bf16[128,128]{1,0:T(8,128)(2,1)} async-done(((bf16[1024,128]{1,0:T(8,128)(2,1)}), bf16[128,128]{1,0:T(8,128)(2,1)}) %reduce-scatter.31.cloned.1.call-update) | async-done | bytes 32784 | tf_op jit(solution)/shard_map/reduce_scatter | solution.py:420
  1317.0 35.2 %reduce-scatter.33.cloned.1.call-done = bf16[128,128]{1,0:T(8,128)(2,1)} async-done(((bf16[1024,128]{1,0:T(8,128)(2,1)}), bf16[128,128]{1,0:T(8,128)(2,1)}) %reduce-scatter.33.cloned.1.call-update) | async-done | bytes 32784 | tf_op jit(solution)/shard_map/reduce_scatter | solution.py:423
  1353.7 28.6 %reduce-scatter.27.cloned.1.call-done = bf16[1,128,1024]{2,1,0:T(8,128)(2,1)} async-done(((bf16[1,512,1024]{2,1,0:T(8,128)(2,1)}), bf16[1,128,1024]{2,1,0:T(8,128)(2,1)}) %reduce-scatter.27.cloned.1.call-update) | async-done | bytes 262160 | tf_op jit(solution)/shard_map/reduce_scatter | solution.py:98
  1383.6 39.1 %all-reduce.4 = (f32[1024]{0:T(1024)S(1)}, f32[1024]{0:T(1024)S(1)}) all-reduce(f32[1024]{0:T(1024)S(1)} %get-tuple-element.688, f32[1024]{0:T(1024)S(1)} %copy-done.52), channel_id=16, replica_groups=mesh['dp'=4,'seq'=2,'tensor'=4] {'dp','seq','tensor'}, use_global_device_ids=true, to_apply=%region_44.47.clone | all-reduce | flops 2048 | bytes 16384
  1437.7 52.4 %reduce-scatter.39.cloned.1.call-done = bf16[16,128,128]{2,1,0:T(8,128)(2,1)} async-done(((bf16[16,1024,128]{2,1,0:T(8,128)(2,1)}), bf16[16,128,128]{2,1,0:T(8,128)(2,1)}) %reduce-scatter.39.cloned.1.call-update) | async-done | bytes 524304 | tf_op jit(solution)/shard_map/reduce_scatter | solution.py:434
  1492.3 52.3 %reduce-scatter.41.cloned.1.call-done = bf16[16,128,128]{2,1,0:T(8,128)(2,1)} async-done(((bf16[16,1024,128]{2,1,0:T(8,128)(2,1)}), bf16[16,128,128]{2,1,0:T(8,128)(2,1)}) %reduce-scatter.41.cloned.1.call-update) | async-done | bytes 524304 | tf_op jit(solution)/shard_map/reduce_scatter | solution.py:437
  1546.7 27.5 %reduce-scatter.19.cloned.1.call-done = bf16[1,128,1024]{2,1,0:T(8,128)(2,1)} async-done(((bf16[1,512,1024]{2,1,0:T(8,128)(2,1)}), bf16[1,128,1024]{2,1,0:T(8,128)(2,1)}) %reduce-scatter.19.cloned.1.call-update) | async-done | bytes 262160 | tf_op jit(solution)/shard_map/reduce_scatter | solution.py:98
  (702 shorter events, 757.2 us)
Async XLA Ops:
  7.2 118.6 %all-gather.10.cloned.1.call-start = ((), (), s32[]{:S(2)}) async-start(), calls=%async_computation.14 | async-start | bytes 1310720 | tf_op jit(solution)/shard_map/all_gather | solution.py:94
  53.9 156.3 %reduce-scatter.17.cloned.1.call-start = ((), (), s32[]{:S(2)}) async-start(), calls=%async_computation.15 | async-start | bytes 1310720 | tf_op jit(solution)/shard_map/reduce_scatter | solution.py:98
  183.8 151.8 %all-gather.20.cloned.1.call-start = ((), (), s32[]{:S(2)}) async-start(), calls=%async_computation.21 | async-start | bytes 1310720 | tf_op jit(solution)/shard_map/all_gather | solution.py:94
  184.6 178.3 %all-gather.12.cloned.1.call-start = ((), (), s32[]{:S(2)}) async-start(), calls=%async_computation.16 | async-start | bytes 1310720 | tf_op jit(solution)/shard_map/all_gather | solution.py:94
  213.2 242.9 %all-gather.14.cloned.1.call-start = ((), (), s32[]{:S(2)}) async-start(), calls=%async_computation.17 | async-start | bytes 4718592 | tf_op jit(solution)/shard_map/all_gather | solution.py:230
  213.8 242.3 %all-gather.16.cloned.1.call-start = ((), (), s32[]{:S(2)}) async-start(), calls=%async_computation.18 | async-start | bytes 4718592 | tf_op jit(solution)/shard_map/all_gather | solution.py:231
  214.4 241.7 %all-gather.18.cloned.1.call-start = ((), (), s32[]{:S(2)}) async-start(), calls=%async_computation.19 | async-start | bytes 4718592 | tf_op jit(solution)/shard_map/all_gather | solution.py:232
  215.1 740.7 %reduce-scatter.21.cloned.1.call-start = ((), (), s32[]{:S(2)}) async-start(), calls=%async_computation.22 | async-start | bytes 1310720 | tf_op jit(solution)/shard_map/reduce_scatter | solution.py:98
  931.3 55.0 %all-gather.22.cloned.1.call-start = ((), (), s32[]{:S(2)}) async-start(), calls=%async_computation.23 | async-start | bytes 1310720 | tf_op jit(solution)/shard_map/all_gather | solution.py:94
  959.7 94.0 %reduce-scatter.23.cloned.1.call-start = ((), (), s32[]{:S(2)}) async-start(), calls=%async_computation.24 | async-start | bytes 393216 | tf_op jit(solution)/shard_map/reduce_scatter | solution.py:368
  1042.4 25.9 %reduce-scatter.25.cloned.1.call-start = ((), (), s32[]{:S(2)}) async-start(), calls=%async_computation.25 | async-start | bytes 393216 | tf_op jit(solution)/shard_map/reduce_scatter | solution.py:371
  1043.1 163.5 %reduce-scatter.43.cloned.1.call-start = ((), (), s32[]{:S(2)}) async-start(), calls=%async_computation.34 | async-start | bytes 540672
  1046.0 194.8 %reduce-scatter.35.cloned.1.call-start = ((), (), s32[]{:S(2)}) async-start(), calls=%async_computation.30 | async-start | bytes 589824 | tf_op jit(solution)/shard_map/reduce_scatter | solution.py:426
  1048.6 229.8 %reduce-scatter.29.cloned.1.call-start = ((), (), s32[]{:S(2)}) async-start(), calls=%async_computation.27 | async-start | bytes 589824 | tf_op jit(solution)/shard_map/reduce_scatter | solution.py:417
  1050.1 265.5 %reduce-scatter.31.cloned.1.call-start = ((), (), s32[]{:S(2)}) async-start(), calls=%async_computation.28 | async-start | bytes 294912 | tf_op jit(solution)/shard_map/reduce_scatter | solution.py:420
  1055.9 296.3 %reduce-scatter.33.cloned.1.call-start = ((), (), s32[]{:S(2)}) async-start(), calls=%async_computation.29 | async-start | bytes 294912 | tf_op jit(solution)/shard_map/reduce_scatter | solution.py:423
  1070.8 311.5 %reduce-scatter.27.cloned.1.call-start = ((), (), s32[]{:S(2)}) async-start(), calls=%async_computation.26 | async-start | bytes 1310720 | tf_op jit(solution)/shard_map/reduce_scatter | solution.py:98
  1074.1 361.5 %reduce-scatter.37.cloned.1.call-start = ((), (), s32[]{:S(2)}) async-start(), calls=%async_computation.31 | async-start | bytes 4718592 | tf_op jit(solution)/shard_map/reduce_scatter | solution.py:431
  1074.7 415.4 %reduce-scatter.39.cloned.1.call-start = ((), (), s32[]{:S(2)}) async-start(), calls=%async_computation.32 | async-start | bytes 4718592 | tf_op jit(solution)/shard_map/reduce_scatter | solution.py:434
  1075.4 469.1 %reduce-scatter.41.cloned.1.call-start = ((), (), s32[]{:S(2)}) async-start(), calls=%async_computation.33 | async-start | bytes 4718592 | tf_op jit(solution)/shard_map/reduce_scatter | solution.py:437
  1075.5 306.8 %copy-start.45 = (f32[1024]{0:T(1024)S(1)}, f32[1024]{0:T(1024)}, u32[]{:S(2)}) copy-start(f32[1024]{0:T(1024)} %copy-done.44) | copy-start | bytes 12292
  1075.5 306.8 %copy-start.57 = (f32[128]{0:T(128)S(1)}, f32[128]{0:T(128)}, u32[]{:S(2)}) copy-start(f32[128]{0:T(128)} %copy-done.56) | copy-start | bytes 1540
  1075.5 308.1 %copy-start.52 = (f32[1024]{0:T(1024)S(1)}, f32[1024]{0:T(1024)}, u32[]{:S(2)}) copy-start(f32[1024]{0:T(1024)} %get-tuple-element.686) | copy-start | bytes 12292
  1076.0 498.1 %reduce-scatter.19.cloned.1.call-start = ((), (), s32[]{:S(2)}) async-start(), calls=%async_computation.20 | async-start | bytes 1310720 | tf_op jit(solution)/shard_map/reduce_scatter | solution.py:98
  (68 other events, 3164.2 us)
Sparse Core Ops, SparseCore 0:
  54.0 27.7 all-gather.9
  184.0 26.2 reduce-scatter.16
  211.8 26.5 all-gather.19
  240.4 28.0 all-gather.11
  270.2 36.1 all-gather.13
  308.2 36.6 all-gather.15
  346.7 36.5 all-gather.17
  931.4 24.3 reduce-scatter.20
  959.8 26.4 all-gather.21
  1042.5 11.1 reduce-scatter.22
  1056.4 11.7 reduce-scatter.24
  1070.3 136.2 reduce-scatter.42
  1210.2 30.5 reduce-scatter.34
  1244.3 34.0 reduce-scatter.28
  1281.9 33.6 reduce-scatter.30
  1318.5 33.6 reduce-scatter.32
  1355.0 27.2 reduce-scatter.26
  1385.5 50.0 reduce-scatter.36
  1439.0 51.1 reduce-scatter.38
  1493.3 51.1 reduce-scatter.40
  1546.8 27.2 reduce-scatter.18
where the time goes:
time: 1600 us; the launch traced here: 1580 us
  waiting for transfers between devices  540 us (34%)
  matrix products  376 us (24%)
  local copies, waits for them, and re-layouts  316 us (20%)
  blocking collectives  229 us (14%)
  other arithmetic  99.1 us (6%)
    unnamed x22, waiting for transfers between devices  136 us
    reduce_scatter x4, waiting for transfers between devices, collect_rows(): lax.psum_scatter(terms.astype(jnp.bfloat16), 'tensor', scatter_dimension=...  106 us
    unnamed x2, blocking collectives  81.1 us
    all_gather x1, blocking collectives, per_device(): lax.all_gather(router, ('dp', 'seq', 'tensor'), axis=0, tiled=True)  67.9 us
    gather x2, local copies, waits for them, and re-layouts, combine_slots(): picked = jnp.take(slot_rows, slot, axis=0, mode='fill', fill_value=0.0)  58.7 us
    reduce_scatter x1, waiting for transfers between devices, per_device(): lax.psum_scatter(up_wgrads.astype(jnp.bfloat16), ('dp', 'seq'), scatter_d...  52.4 us
    reduce_scatter x1, waiting for transfers between devices, per_device(): lax.psum_scatter(down_wgrads.astype(jnp.bfloat16), ('dp', 'seq'), scatter...  52.3 us
    dot_general x16, matrix products, expert_forward(): lax.dot_general(active, down_e, (((1,), (1,)), ((), ())), preferred_eleme...  38 us
  transfers between devices with their start and end apart: 21, of which 15 were waited for; matrix products, arithmetic and copies ran while one was open for 13% of the time, Pallas kernels for 0%

commit v1 on v0

v1 whole, which is shorter than its diff:
```python
import functools
import math

import jax
import jax.numpy as jnp
from jax import lax
from jax.experimental import pallas as pl
from jax.experimental.pallas import tpu as pltpu
from jax.sharding import PartitionSpec as P

HEAD = 64
E = 16
PIECE = 256
CAP = 320
EPS = 1e-06
FILL = -1e30
EXPERTS_PER_STEP = 2
ROW_TILE = 256
f32 = jnp.float32
bf16 = jnp.bfloat16

NT = (((1,), (1,)), ((), ()))
NN = (((1,), (0,)), ((), ()))


def dot(a, b, dims=NN):
    return lax.dot_general(a, b, dims, preferred_element_type=f32)


def full(shape):
    rank = len(shape)
    return pl.BlockSpec(shape, lambda *_: (0,) * rank)


def whole_call(body, outs, args, scratch=(), flops=0, prefetch=0):
    moved = sum(math.prod(a.shape) * a.dtype.itemsize for a in (*args, *outs))
    return pl.pallas_call(
        body,
        out_shape=outs,
        grid_spec=pltpu.PrefetchScalarGridSpec(
            num_scalar_prefetch=prefetch,
            grid=(1,),
            in_specs=[full(a.shape) for a in args[prefetch:]],
            out_specs=[full(o.shape) for o in outs],
            scratch_shapes=list(scratch),
        ),
        cost_estimate=pl.CostEstimate(flops=int(flops), bytes_accessed=int(moved), transcendentals=0),
    )(*args)


def sds(shape, dtype):
    return jax.ShapeDtypeStruct(shape, dtype)


def reorder_kernel(where, a_ref, b_ref, a_out, b_out):
    wide = a_ref.shape[1] // where.shape[0]
    for i in range(where.shape[0]):
        source = pl.ds(pl.multiple_of(where[i] * wide, wide), wide)
        a_out[:, i * wide : (i + 1) * wide] = a_ref[:, source]
        b_out[:, i * wide : (i + 1) * wide] = b_ref[:, source]


def turn(v, cos, sin):
    lane = lax.broadcasted_iota(jnp.int32, v.shape, 1) % HEAD
    other = jnp.where(lane < HEAD // 2, pltpu.roll(v, 128 - HEAD // 2, 1), pltpu.roll(v, HEAD // 2, 1))
    return v * cos + other * sin


def rows_of(refs, rows):
    parts = []
    for r in refs:
        parts += [r[i, 0:rows, :] for i in range(r.shape[0])]
    return jnp.concatenate(parts, axis=0)


def qkv_kernel(n, rows, *refs):
    xs, (gain, cos, sin, wa, wb), (x1, q, kv) = refs[:n], refs[n : n + 5], refs[n + 5 :]
    m = xs[0].shape[0]
    for j in range(n):
        v = xs[j][...].astype(f32)
        r = lax.rsqrt(jnp.mean(v * v, axis=-1, keepdims=True) + EPS)
        x1[j * m : (j + 1) * m, :] = (v * r * gain[...]).astype(bf16)
    out = dot(x1[...], rows_of((wa, wb), rows))
    c, s = cos[...], sin[...]
    q[:, 0:128] = turn(out[:, 0:128], c, s).astype(bf16)
    q[:, 128:256] = turn(out[:, 128:256], c, s).astype(bf16)
    kv[:, 0:128] = turn(out[:, 256:384], c, s).astype(bf16)
    kv[:, 128:256] = out[:, 384:512].astype(bf16)


SCORE = HEAD ** (-0.5) * math.log2(math.e)


def attend_kernel(parts, n, q, lim, *refs):
    kvs, poss = refs[:parts], refs[parts : 2 * parts]
    mixed, (ot, lse) = refs[2 * parts : 2 * parts + n], refs[2 * parts + n : 2 * parts + n + 2]
    qs, ks, vt, kp = refs[2 * parts + n + 2 :]
    count = q.shape[0]
    heads = q.shape[1] // HEAD
    first = 0
    for kvr, pr in zip(kvs, poss):
        span = slice(first, first + kvr.shape[0])
        first += kvr.shape[0]
        v = kvr[:, 128:256].astype(f32).T.astype(bf16)
        for g in range(2):
            ks[g, span, :] = kvr[:, g * HEAD : (g + 1) * HEAD]
            vt[g, :, span] = v[g * HEAD : (g + 1) * HEAD, :]
        kp[span, :] = pr[...]
    for h in range(heads):
        qs[h] = q[:, h * HEAD : (h + 1) * HEAD]
    tiles = count // ROW_TILE

    def body(i, carry):
        h, t = i // tiles, i % tiles
        at = pl.ds(pl.multiple_of(t * ROW_TILE, ROW_TILE), ROW_TILE)
        g = h // 2
        s = dot(ks[g], qs[h, at, :], NT)
        s = jnp.where(kp[...] <= lim[:, at], s, FILL)
        top = jnp.max(s, axis=0, keepdims=True)
        p = jnp.exp2((s - top) * SCORE)
        total = jnp.sum(p, axis=0, keepdims=True)
        o = dot(vt[g], p.astype(bf16))
        ot[h, :, at] = o / total
        lse[h, :, at] = top * SCORE + jnp.log2(total)
        return carry

    lax.fori_loop(0, heads * tiles, body, 0)
    out = ot[...].reshape(heads * HEAD, count).T.astype(bf16)
    m = count // n
    for j in range(n):
        mixed[j][...] = out[j * m : (j + 1) * m, :]


def attend_back_kernel(n, last, q, lim, kv, kpos, lse, ot, *refs):
    dos_in, refs = refs[:n], refs[n:]
    if last:
        (dq_in, cos, sin), refs = refs[:3], refs[3:]
    dkv, dq_out = refs[:2]
    qs, dos, ks, vs, kt, delta, dk, dv, dqt = refs[2:]
    count = q.shape[0]
    heads = q.shape[1] // HEAD
    m = count // n
    for j in range(n):
        block = dos_in[j][...]
        turned = block.astype(f32).T
        for h in range(heads):
            span = slice(h * HEAD, (h + 1) * HEAD)
            dos[h, j * m : (j + 1) * m, :] = block[:, span]
            delta[h, :, j * m : (j + 1) * m] = jnp.sum(
                turned[span, :] * ot[h, :, j * m : (j + 1) * m], axis=0, keepdims=True
            )
    k_turned = kv[:, 0:128].astype(f32).T.astype(bf16)
    for g in range(2):
        ks[g] = kv[:, g * HEAD : (g + 1) * HEAD]
        vs[g] = kv[:, 128 + g * HEAD : 128 + (g + 1) * HEAD]
        kt[g] = k_turned[g * HEAD : (g + 1) * HEAD, :]
    for h in range(heads):
        qs[h] = q[:, h * HEAD : (h + 1) * HEAD]
    dk[...] = jnp.zeros_like(dk)
    dv[...] = jnp.zeros_like(dv)
    tiles = count // ROW_TILE

    def body(i, carry):
        h, t = i // tiles, i % tiles
        at = pl.ds(pl.multiple_of(t * ROW_TILE, ROW_TILE), ROW_TILE)
        g = h // 2
        q_h, do_h = qs[h, at, :], dos[h, at, :]
        s = dot(ks[g], q_h, NT)
        p = jnp.where(kpos[...] <= lim[:, at], jnp.exp2(s * SCORE - lse[h, :, at]), 0.0)
        dp = dot(vs[g], do_h, NT)
        ds = (p * (dp - delta[h, :, at])).astype(bf16)
        dv[g] += dot(p.astype(bf16), do_h)
        dk[g] += dot(ds, q_h)
        dqt[h, :, at] = dot(kt[g], ds)
        return carry

    lax.fori_loop(0, heads * tiles, body, 0)
    scale = HEAD ** (-0.5)
    dkv[...] = jnp.concatenate([dk[0] * scale, dk[1] * scale, dv[0], dv[1]], axis=1).astype(dkv.dtype)
    if last:
        whole = ((dqt[...] + dq_in[...]).reshape(heads * HEAD, count) * scale).T
        for half in range(2):
            lanes = slice(half * 128, (half + 1) * 128)
            dq_out[:, lanes] = turn(whole[:, lanes], cos[...], -sin[...]).astype(bf16)
    else:
        dq_out[...] = dqt[...]


def middle_kernel(n, x, gain, wa, wb, *refs):
    mixed, (middle, second) = refs[:n], refs[n:]
    rows = wa.shape[1]
    both = jnp.concatenate([r[...] for r in mixed], axis=1)
    value = x[...].astype(f32) + dot(both, rows_of((wa, wb), rows), NT)
    middle[...] = value
    r = lax.rsqrt(jnp.mean(value * value, axis=-1, keepdims=True) + EPS)
    second[...] = (value * r * gain[...]).astype(bf16)


def middle_back_kernel(n, middle, gain, cot, wa, wb, *refs):
    parts, refs = refs[:n], refs[n:]
    middle_grad, branch, gain_grad = refs[:3]
    pieces = refs[3:]
    u = parts[0][...].astype(f32)
    for r in parts[1:]:
        u = u + r[...].astype(f32)
    value = middle[...]
    r = lax.rsqrt(jnp.mean(value * value, axis=-1, keepdims=True) + EPS)
    normal = value * r
    gain_grad[...] = jnp.sum(u * normal, axis=0, keepdims=True)
    scaled = u * gain[...]
    grad = cot[...].astype(f32) + r * (scaled - normal * jnp.mean(scaled * normal, axis=-1, keepdims=True))
    middle_grad[...] = grad
    low = grad.astype(bf16)
    branch[...] = low
    rows = wa.shape[1]
    out = dot(low, rows_of((wa, wb), rows)).astype(bf16)
    wide = out.shape[1] // n
    for j in range(n):
        pieces[j][...] = out[:, j * wide : (j + 1) * wide]


def pick(table, index):
    lane = lax.broadcasted_iota(jnp.int32, table.shape, 1)
    return jnp.sum(jnp.where(lane == index, table, 0.0), axis=1, keepdims=True)


def expert_kernel(n, pieces, chosen, kept, router, *refs):
    xs, cs, ws, refs = refs[:n], refs[n : 2 * n], refs[2 * n : 2 * n + pieces], refs[2 * n + pieces :]
    outs, (active_out, gate_out, up_out, router_grad) = refs[:n], refs[n : n + 4]
    x, c, w, total, soft, share = refs[n + 4 :]
    step, steps = pl.program_id(0), pl.num_programs(0)
    m = xs[0].shape[0]
    eb = EXPERTS_PER_STEP
    fe = ws[0].shape[3]
    wide = eb * fe

    @pl.when(step == 0)
    def _():
        for j in range(n):
            x[j * m : (j + 1) * m, :] = xs[j][...]
            c[j * m : (j + 1) * m, :] = cs[j][...]
        logits = jnp.where(chosen[...] > 0.0, dot(x[...], router[...]), FILL)
        top = jnp.max(logits, axis=1, keepdims=True)
        e = jnp.where(chosen[...] > 0.0, jnp.exp(logits - top), 0.0)
        soft[...] = e / jnp.sum(e, axis=1, keepdims=True)
        total[...] = jnp.zeros_like(total)
        share[...] = jnp.zeros_like(share)

    first = 0
    for r in ws:
        span = slice(first, first + r.shape[2])
        first += r.shape[2]
        for kind in range(3):
            for i in range(eb):
                w[span, kind * wide + i * fe : kind * wide + (i + 1) * fe] = r[kind, i]
    gu = dot(x[...], w[:, : 2 * wide])
    down = dot(c[...], w[:, 2 * wide :])
    table = soft[...] * kept[...]
    lane = lax.broadcasted_iota(jnp.int32, share.shape, 1)
    sums = jnp.zeros(share.shape, f32)
    gate_parts, up_parts = [], []
    for i in range(eb):
        span = slice(i * fe, (i + 1) * fe)
        gate, up, d = gu[:, span], gu[:, wide + i * fe : wide + (i + 1) * fe], down[:, span]
        index = step * eb + i
        weight = pick(table, index)
        sig = jax.nn.sigmoid(gate)
        silu = gate * sig
        active = silu * up
        active_out[:, span] = (active * weight).astype(bf16)
        sums = sums + jnp.where(lane == index, jnp.sum(active * d, axis=1, keepdims=True), 0.0)
        ag = d * weight
        gp = (ag * up * (sig * (1.0 + gate * (1.0 - sig)))).astype(bf16)
        ug = (ag * silu).astype(bf16)
        gate_out[:, span] = gp
        up_out[:, span] = ug
        gate_parts.append(gp)
        up_parts.append(ug)
    share[...] += sums
    total[...] += dot(jnp.concatenate(gate_parts + up_parts, axis=1), w[:, : 2 * wide], NT)

    @pl.when(step == steps - 1)
    def _():
        pair = share[...] * kept[...]
        mine = soft[...]
        logit = mine * (pair - jnp.sum(mine * pair, axis=1, keepdims=True))
        high = logit.astype(bf16)
        low = (logit - high.astype(f32)).astype(bf16)
        value = total[...] + (dot(high, router[...], NT) + dot(low, router[...], NT))
        for j in range(n):
            outs[j][...] = value[j * m : (j + 1) * m, :].astype(bf16)
        across = (((0,), (0,)), ((), ()))
        router_grad[...] = dot(high, x[...], across) + dot(low, x[...], across)


def expert_back_kernel(n, pieces, rows, active, gate, up, *refs):
    xs, cs, ws, refs = refs[:n], refs[n : 2 * n], refs[2 * n : 2 * n + pieces], refs[2 * n + pieces :]
    outs, (keep, send) = refs[:n], refs[n : n + 2]
    xt, ct, w, total = refs[n + 2 :]
    step, steps = pl.program_id(0), pl.num_programs(0)
    m = xs[0].shape[0]
    eb = EXPERTS_PER_STEP
    fe = ws[0].shape[3]

    @pl.when(step == 0)
    def _():
        for j in range(n):
            xt[:, j * m : (j + 1) * m] = xs[j][...].T
            ct[:, j * m : (j + 1) * m] = cs[j][...].T
        total[...] = jnp.zeros_like(total)

    first = 0
    for r in ws:
        span = slice(first, first + r.shape[2])
        first += r.shape[2]
        for i in range(eb):
            w[span, i * fe : (i + 1) * fe] = r[0, i]
    total[...] += dot(active[...], w[...], NT)
    half = keep.shape[0]
    for kind, (left, right) in enumerate(((xt, gate), (xt, up), (ct, active))):
        value = dot(left[...], right[...]).astype(bf16)
        for b in range(2 * half):
            target = keep if b < half else send
            for i in range(eb):
                target[b % half, kind, i] = value[b * rows : (b + 1) * rows, i * fe : (i + 1) * fe]

    @pl.when(step == steps - 1)
    def _():
        for j in range(n):
            outs[j][...] = total[j * m : (j + 1) * m, :].astype(bf16)


def qkv_back_kernel(n, rows, dq, dkv, got, cos, sin, wa, wb, *refs):
    xs, refs = refs[:n], refs[n:]
    outs, (grads, gain_grad) = refs[:n], refs[n:]
    m = xs[0].shape[0]
    both = dkv[...].astype(f32)
    if got is not None:
        both = both + got[...].astype(f32)
    grads[:, 0:256] = dq[...]
    grads[:, 256:384] = turn(both[:, 0:128], cos[...], -sin[...]).astype(bf16)
    grads[:, 384:512] = both[:, 128:256].astype(bf16)
    u = dot(grads[...], rows_of((wa, wb), rows), NT)
    sums = jnp.zeros(gain_grad.shape, f32)
    for j in range(n):
        v = xs[j][...].astype(f32)
        r = lax.rsqrt(jnp.mean(v * v, axis=-1, keepdims=True) + EPS)
        part = u[j * m : (j + 1) * m, :]
        sums = sums + jnp.sum(part * (v * r), axis=0, keepdims=True)
        outs[j][...] = part.astype(bf16)
    gain_grad[...] = sums


def weight_back_kernel(n, rows, x1, grads, *refs):
    bs, ms, (keep, send) = refs[:n], refs[n : 2 * n], refs[2 * n :]
    first = dot(x1[...].T, grads[...]).astype(bf16)
    branch = jnp.concatenate([r[...] for r in bs], axis=0)
    mixed = jnp.concatenate([r[...] for r in ms], axis=0)
    second = dot(branch.T, mixed).astype(bf16)
    half = keep.shape[0]
    wide = first.shape[1]
    for b in range(2 * half):
        target = keep if b < half else send
        target[b % half, :, 0:wide] = first[b * rows : (b + 1) * rows, :]
        target[b % half, :, wide:] = second[b * rows : (b + 1) * rows, :]


def put(out, value, where):
    wide = out.shape[1] // where.shape[0]
    if wide % 128:
        out[...] = value
        return
    for i in range(where.shape[0]):
        out[:, pl.ds(pl.multiple_of(where[i] * wide, wide), wide)] = value[:, i * wide : (i + 1) * wide]


def input_kernel(n, where, x, gain, middle_grad, *refs):
    parts, out = refs[:n], refs[n]
    u = parts[0][...].astype(f32)
    for r in parts[1:]:
        u = u + r[...].astype(f32)
    v = x[...].astype(f32)
    r = lax.rsqrt(jnp.mean(v * v, axis=-1, keepdims=True) + EPS)
    normal = v * r
    scaled = u * gain[...]
    grad = r * (scaled - normal * jnp.mean(scaled * normal, axis=-1, keepdims=True))
    put(out, (middle_grad[...] + grad).astype(bf16), where)


def output_kernel(n, where, middle, *refs):
    parts, out = refs[:n], refs[n]
    u = middle[...]
    for r in parts:
        u = u + r[...].astype(f32)
    put(out, u.astype(bf16), where)


def tensor_shift(v, s):
    n = lax.axis_size("tensor")
    return lax.ppermute(v, "tensor", [(i, (i + s) % n) for i in range(n)])


def swap_x(v):
    return lax.ppermute(v, "seq", [(0, 1), (1, 0)])


def swap_core(v):
    return lax.ppermute(v, "dp", [(i, i ^ 1) for i in range(4)])


def swap_y(v):
    return lax.ppermute(v, "dp", [(i, i ^ 2) for i in range(4)])


def swap_xy(v):
    return lax.ppermute(v, ("dp", "seq"), [(i, i ^ 5) for i in range(8)])


def plane_gather(v, fancy):
    if fancy:
        near = jnp.stack([v, swap_x(v), swap_y(v), swap_xy(v)])
        return near, swap_core(near)
    every = lax.all_gather(v, ("dp", "seq"), axis=0, tiled=False)
    half = every.shape[0] // 2
    return every[:half], every[half:]


def plane_scatter(keep, send, fancy):
    if not fancy:
        both = jnp.concatenate([keep, send], axis=0)
        return lax.psum_scatter(both, ("dp", "seq"), scatter_dimension=0, tiled=False).astype(f32)
    near = keep.astype(f32) + swap_core(send).astype(f32)
    low = near[1:].astype(bf16)
    return (
        near[0]
        + swap_x(low[0]).astype(f32)
        + swap_y(low[1]).astype(f32)
        + swap_xy(low[2]).astype(f32)
    )


def plane_scatter_large(keep, send, fancy):
    if not fancy:
        return plane_scatter(keep, send, fancy)
    near = keep.astype(f32) + swap_core(send).astype(f32)
    half = near.shape[-2] // 2
    far = near[3].astype(bf16)
    got_x, got_y = swap_x(far[..., :half, :]), swap_y(far[..., half:, :])
    to_y = jnp.concatenate([near[2][..., :half, :] + got_x.astype(f32), near[2][..., half:, :]], axis=-2)
    to_x = jnp.concatenate([near[1][..., :half, :], near[1][..., half:, :] + got_y.astype(f32)], axis=-2)
    return near[0] + swap_x(to_x.astype(bf16)).astype(f32) + swap_y(to_y.astype(bf16)).astype(f32)


def gather_experts(packed, fancy):
    if not fancy:
        every = lax.all_gather(packed, ("dp", "seq"), axis=2, tiled=True)
        return [every]
    half = packed.shape[2] // 2
    on_x, on_y = swap_x(packed), swap_y(packed)
    far_a = swap_x(on_y[:, :, :half])
    far_b = swap_y(on_x[:, :, half:])
    near = [packed, on_x, on_y, far_a, far_b]
    return near + [swap_core(v) for v in near]


def per_device(
    hidden_in,
    cotangent,
    piece_starts,
    expert_ids,
    claim_order,
    first_gain,
    second_gain,
    router,
    w_query,
    key_projection,
    value_projection,
    w_out,
    w_gate,
    w_up,
    w_down,
):
    n_dp, n_seq, n = lax.axis_size("dp"), lax.axis_size("seq"), lax.axis_size("tensor")
    fancy = n_dp == 4 and n_seq == 2
    n_p = n_dp * n_seq
    me = lax.axis_index("tensor")
    seq_at = lax.axis_index("seq")
    place = lax.axis_index("dp") * n_seq + seq_at
    m, d = hidden_in.shape[1:]
    count = m * n
    rows = d // n_p
    if hidden_in.shape[0] != 1 or expert_ids.shape[1] != count:
        raise ValueError("shapes")
    wide = w_query.shape[1]
    order = (0, 1, 4, 5, 2, 3, 6, 7) if fancy else tuple(range(n_p))
    where = (place ^ jnp.array(order, jnp.int32)) if fancy else jnp.arange(n_p, dtype=jnp.int32)

    own, cot = hidden_in[0], cotangent[0]
    if fancy:
        own, cot = whole_call(
            reorder_kernel, (sds(own.shape, bf16), sds(cot.shape, bf16)), (where, own, cot), prefetch=1
        )
    xs = [own] + [tensor_shift(own, j) for j in range(1, n)]

    qkv_w = jnp.concatenate([w_query, key_projection, value_projection], axis=1)
    cols = qkv_w.shape[1]
    small = jnp.concatenate([router.reshape(-1), first_gain, second_gain])
    size = small.shape[0]
    small = jnp.pad(small, (0, 16 * cols - size)).reshape(16, cols)
    wa, wb = plane_gather(jnp.concatenate([qkv_w, small], axis=0), fancy)
    tail = jnp.concatenate([wa[:, rows:], wb[:, rows:]], axis=0).reshape(n_p, -1)[:, :size]
    tails = [tail] + [tensor_shift(tail, j) for j in range(1, n)]
    stacked = jnp.stack(tails).astype(f32)
    which = (me - jnp.arange(n)) % n
    pick_rows = (which[:, None] == jnp.arange(n)[None, :]).astype(f32)
    natural = jnp.sum(pick_rows[:, :, None, None] * stacked[None], axis=1)
    shard = first_gain.shape[0]
    gain_one = jnp.transpose(natural[:, :, size - 2 * shard : size - shard], (1, 0, 2)).reshape(1, d)
    gain_two = jnp.transpose(natural[:, :, size - shard :], (1, 0, 2)).reshape(1, d)
    router_all = (
        jnp.transpose(natural[:, :, : size - 2 * shard].reshape(n, n_p, shard, E), (1, 0, 2, 3))
        .reshape(d, E)
        .astype(bf16)
    )

    blocks = (me - jnp.arange(n, dtype=jnp.int32)) % n
    positions = (seq_at * count + blocks[:, None] * m + jnp.arange(m, dtype=jnp.int32)[None, :]).reshape(count)
    starts = piece_starts[0]
    inside = (positions[:, None] >= starts[None, :]) & (positions[:, None] < starts[None, :] + PIECE)
    limit = jnp.maximum(
        positions, jnp.max(jnp.where(inside, starts[None, :] + PIECE - 1, -1), axis=1)
    ).reshape(1, count)
    half = HEAD // 2
    freqs = jnp.exp(jnp.arange(half).astype(f32) * (-2.0 * math.log(10000.0) / HEAD))
    angles = positions.astype(f32)[:, None] * freqs[None, :]
    cosine, sine = jnp.cos(angles), jnp.sin(angles)
    cos = jnp.concatenate([cosine] * 4, axis=1)
    sin = jnp.concatenate([-sine, sine] * 2, axis=1)

    ids, claim = expert_ids[0], claim_order[0]
    experts = jnp.arange(E, dtype=jnp.int32)
    chosen = jnp.max((ids[:, :, None] == experts[None, None, :]).astype(f32), axis=1)
    before = (claim[None, :] < claim[:, None]).astype(bf16)
    taken = dot(before, chosen.astype(bf16))
    kept = jnp.where(taken < CAP, chosen, 0.0)
    tables = jnp.concatenate([chosen, kept], axis=1).reshape(n, m, 2 * E)
    tables = jnp.sum(
        (blocks[:, None] == jnp.arange(n)[None, :]).astype(f32)[:, :, None, None] * tables[None], axis=1
    ).reshape(count, 2 * E)
    chosen, kept = tables[:, :E], tables[:, E:]

    x1, q, kv = whole_call(
        functools.partial(qkv_kernel, n, rows),
        (sds((count, d), bf16), sds((count, wide), bf16), sds((count, 256), bf16)),
        (*xs, gain_one, cos, sin, wa, wb),
        flops=2 * count * d * cols,
    )
    key_pos = positions.reshape(count, 1)
    if fancy:
        kvs = [kv, swap_x(kv)]
        poss = [key_pos, key_pos + (1 - 2 * seq_at) * count]
    else:
        kvs = [lax.all_gather(kv, "seq", axis=0, tiled=True)]
        poss = [lax.all_gather(key_pos.astype(f32), "seq", axis=0, tiled=True).astype(jnp.int32)]
    span = sum(v.shape[0] for v in kvs)
    heads = wide // HEAD
    got = whole_call(
        functools.partial(attend_kernel, len(kvs), n),
        tuple([sds((m, wide), bf16)] * n) + (sds((heads, HEAD, count), f32), sds((heads, 1, count), f32)),
        (q, limit, *kvs, *poss),
        scratch=(
            pltpu.VMEM((heads, count, HEAD), bf16),
            pltpu.VMEM((2, span, HEAD), bf16),
            pltpu.VMEM((2, HEAD, span), bf16),
            pltpu.VMEM((span, 1), jnp.int32),
        ),
        flops=4 * count * span * wide * 4,
    )
    mixed, (mixed_t, lse) = got[:n], got[n:]

    out_w = jnp.concatenate([w_out] + [tensor_shift(w_out, -j) for j in range(1, n)], axis=1)
    oa, ob = plane_gather(out_w, fancy)
    mine = [mixed[0]] + [tensor_shift(mixed[j], -j) for j in range(1, n)]
    middle, second = whole_call(
        functools.partial(middle_kernel, n),
        (sds((m, d), f32), sds((m, d), bf16)),
        (own, gain_two, oa, ob, *mine),
        flops=2 * m * d * d,
    )

    seconds = [second] + [tensor_shift(second, j) for j in range(1, n)]
    cots = [cot] + [tensor_shift(cot, j) for j in range(1, n)]
    ws = gather_experts(jnp.stack([w_gate, w_up, w_down]), fancy)
    eb, fe = EXPERTS_PER_STEP, w_gate.shape[2]
    steps = E // eb
    block = pl.BlockSpec((count, eb * fe), lambda s: (0, s))
    wide_out = sds((count, E * fe), bf16)
    got = pl.pallas_call(
        functools.partial(expert_kernel, n, len(ws)),
        out_shape=tuple([sds((m, d), bf16)] * n) + (wide_out, wide_out, wide_out, sds((E, d), f32)),
        grid=(steps,),
        in_specs=[full((count, E)), full((count, E)), full((d, E))]
        + [full((m, d))] * (2 * n)
        + [pl.BlockSpec((3, eb, w.shape[2], fe), lambda s: (0, s, 0, 0)) for w in ws],
        out_specs=[full((m, d))] * n + [block] * 3 + [full((E, d))],
        scratch_shapes=[
            pltpu.VMEM((count, d), bf16),
            pltpu.VMEM((count, d), bf16),
            pltpu.VMEM((d, 3 * eb * fe), bf16),
            pltpu.VMEM((count, d), f32),
            pltpu.VMEM((count, E), f32),
            pltpu.VMEM((count, E), f32),
        ],
        cost_estimate=pl.CostEstimate(
            flops=10 * count * d * E * fe, bytes_accessed=3 * d * E * fe * 2, transcendentals=count * E * fe
        ),
    )(chosen, kept, router_all, *seconds, *cots, *ws)
    second_parts, (active, gate_g, up_g, router_part) = got[:n], got[n:]
    half_p = n_p // 2
    grad_shape = sds((half_p, 3, E, rows, fe), bf16)
    grad_block = pl.BlockSpec((half_p, 3, eb, rows, fe), lambda s: (0, 0, s, 0, 0))
    got = pl.pallas_call(
        functools.partial(expert_back_kernel, n, len(ws), rows),
        out_shape=tuple([sds((m, d), bf16)] * n) + (grad_shape, grad_shape),
        grid=(steps,),
        in_specs=[block] * 3
        + [full((m, d))] * (2 * n)
        + [pl.BlockSpec((1, eb, w.shape[2], fe), lambda s: (2, s, 0, 0)) for w in ws],
        out_specs=[full((m, d))] * n + [grad_block] * 2,
        scratch_shapes=[
            pltpu.VMEM((d, count), bf16),
            pltpu.VMEM((d, count), bf16),
            pltpu.VMEM((d, eb * fe), bf16),
            pltpu.VMEM((count, d), f32),
        ],
        cost_estimate=pl.CostEstimate(
            flops=8 * count * d * E * fe, bytes_accessed=4 * d * E * fe * 2, transcendentals=0
        ),
    )(active, gate_g, up_g, *seconds, *cots, *ws)
    out_parts, (keep, send) = got[:n], got[n:]

    sums = [second_parts[0]] + [tensor_shift(second_parts[j], -j) for j in range(1, n)]
    got = whole_call(
        functools.partial(middle_back_kernel, n),
        (sds((m, d), f32), sds((m, d), bf16), sds((1, d), f32)) + tuple([sds((m, wide), bf16)] * n),
        (middle, gain_two, cot, oa, ob, *sums),
        flops=2 * m * d * d,
    )
    (middle_grad, branch, gain_two_part), pieces = got[:3], got[3:]
    mixed_grads = [pieces[0]] + [tensor_shift(pieces[j], j) for j in range(1, n)]
    branches = [branch] + [tensor_shift(branch, j) for j in range(1, n)]

    def attend_back(kv_one, pos_one, dtype, extra):
        one = kv_one.shape[0]
        last = bool(extra)
        return whole_call(
            functools.partial(attend_back_kernel, n, last),
            (
                sds((one, 256), dtype),
                sds((count, wide), bf16) if last else sds((heads, HEAD, count), f32),
            ),
            (q, limit, kv_one, pos_one, lse, mixed_t, *mixed_grads, *extra),
            scratch=(
                pltpu.VMEM((heads, count, HEAD), bf16),
                pltpu.VMEM((heads, count, HEAD), bf16),
                pltpu.VMEM((2, one, HEAD), bf16),
                pltpu.VMEM((2, one, HEAD), bf16),
                pltpu.VMEM((2, HEAD, one), bf16),
                pltpu.VMEM((heads, 1, count), f32),
                pltpu.VMEM((2, one, HEAD), f32),
                pltpu.VMEM((2, one, HEAD), f32),
                pltpu.VMEM((heads, HEAD, count), f32),
            ),
            flops=10 * count * one * wide * 4,
        )

    if fancy:
        far, dq_far = attend_back(kvs[1], poss[1], bf16, ())
        got_kv = (swap_x(far),)
        dkv, dq = attend_back(kvs[0], poss[0], f32, (dq_far, cos, sin))
    else:
        zero = jnp.zeros((heads, HEAD, count), f32)
        dkv, dq = attend_back(kvs[0], poss[0], bf16, (zero, cos, sin))
        dkv = lax.psum_scatter(dkv, "seq", scatter_dimension=0, tiled=True)
        got_kv = (jnp.zeros((count, 256), bf16),)

    got = whole_call(
        functools.partial(qkv_back_kernel, n, rows),
        tuple([sds((m, d), bf16)] * n) + (sds((count, cols), bf16), sds((1, d), f32)),
        (dq, dkv, *got_kv, cos, sin, wa, wb, *xs),
        flops=2 * count * d * cols,
    )
    first_parts, (grads, gain_one_part) = got[:n], got[n:]
    sums = [first_parts[0]] + [tensor_shift(first_parts[j], -j) for j in range(1, n)]
    weight_shape = sds((half_p, rows, cols + wide), bf16)
    weight_keep, weight_send = whole_call(
        functools.partial(weight_back_kernel, n, rows),
        (weight_shape, weight_shape),
        (x1, grads, *branches, *mixed),
        flops=2 * count * d * (cols + wide),
    )

    (input_grad,) = whole_call(
        functools.partial(input_kernel, n), (sds((m, d), bf16),), (where, own, gain_one, middle_grad, *sums), prefetch=1
    )
    out_sums = [out_parts[0]] + [tensor_shift(out_parts[j], -j) for j in range(1, n)]
    (output,) = whole_call(
        functools.partial(output_kernel, n), (sds((m, d), bf16),), (where, middle, *out_sums), prefetch=1
    )
    weights = plane_scatter(weight_keep, weight_send, fancy)
    expert_grads = plane_scatter_large(keep, send, fancy)

    vectors = jnp.concatenate([router_part, gain_one_part, gain_two_part], axis=0)
    lines = vectors.shape[0]
    vectors = jnp.transpose(vectors.reshape(lines, n_p, rows), (1, 0, 2))
    if fancy:
        vectors = vectors[:4] + swap_core(vectors[4:])
        vectors = vectors[:2] + swap_y(vectors[2:])
        vectors = vectors[0] + swap_x(vectors[1])
    else:
        vectors = lax.psum_scatter(vectors, ("dp", "seq"), scatter_dimension=0, tiled=False)
    total = vectors
    for j in range(1, n):
        total = total + tensor_shift(vectors, j)
    total = lax.dynamic_slice_in_dim(total, me * shard, shard, axis=1)
    kv_wide = key_projection.shape[1]
    return (
        output[None],
        input_grad[None],
        weights[:, :wide],
        weights[:, wide : wide + kv_wide],
        weights[:, wide + kv_wide : cols],
        weights[:, cols:],
        expert_grads[0],
        expert_grads[1],
        expert_grads[2],
        total[E],
        total[E + 1],
        total[:E].T,
    )


def solution(mesh):
    placed = (
        P("dp", ("seq", "tensor"), None),
        P("dp", ("seq", "tensor"), None),
        P("dp", None),
        P("dp", "seq", None),
        P("dp", "seq"),
        P(("dp", "seq", "tensor")),
        P(("dp", "seq", "tensor")),
        P(("dp", "seq", "tensor"), None),
        P(("dp", "seq"), "tensor"),
        P(("dp", "seq"), "tensor"),
        P(("dp", "seq"), "tensor"),
        P(("dp", "seq"), "tensor"),
        P(None, ("dp", "seq"), "tensor"),
        P(None, ("dp", "seq"), "tensor"),
        P(None, ("dp", "seq"), "tensor"),
    )
    return jax.shard_map(
        per_device,
        mesh=mesh,
        in_specs=placed,
        out_specs=(
            P("dp", ("seq", "tensor"), None),
            P("dp", ("seq", "tensor"), None),
            P(("dp", "seq"), "tensor"),
            P(("dp", "seq"), "tensor"),
            P(("dp", "seq"), "tensor"),
            P(("dp", "seq"), "tensor"),
            P(None, ("dp", "seq"), "tensor"),
            P(None, ("dp", "seq"), "tensor"),
            P(None, ("dp", "seq"), "tensor"),
            P(("dp", "seq", "tensor")),
            P(("dp", "seq", "tensor")),
            P(("dp", "seq", "tensor"), None),
        ),
        check_vma=False,
    )
```

time: 1600 us -> 426 us (0.27)
  matrix products: 376 us -> 0.36 us
  waiting for transfers between devices: 540 us -> 200 us
  local copies, waits for them, and re-layouts: 316 us -> 23.8 us
  blocking collectives: 229 us -> 0 us
  Pallas kernels: 0 us -> 91.5 us
  starting transfers between devices: 1.05 us -> 78.8 us
  other arithmetic: 99.1 us -> 29.1 us
    reduce_scatter x13 -> x0, waiting for transfers between devices: 378 us -> none  [the longest x4 106 us: collect_rows(): lax.psum_scatter(terms.astype(jnp.bfloat16), 'tensor', scatter_dimension=...]
    dot_general x202 -> x1, matrix products: 373 us -> 0.36 us  [dot(): return lax.dot_general(a, b, dims, preferred_element_type=f32)]
    ppermute x0 -> x67, waiting for transfers between devices: none -> 200 us  [the longest x36 103 us: tensor_shift(): return lax.ppermute(v, 'tensor', [(i, (i + s) % n) for i in range(n)])]
    gather x17 -> x0, local copies, waits for them, and re-layouts: 200 us -> none  [the longest x2 58.7 us: combine_slots(): picked = jnp.take(slot_rows, slot, axis=0, mode='fill', fill_value=0.0)]
    all_gather x7 -> x0, blocking collectives: 148 us -> none  [the longest x1 67.9 us: per_device(): lax.all_gather(router, ('dp', 'seq', 'tensor'), axis=0, tiled=True)]
    unnamed x22 -> x0, waiting for transfers between devices: 136 us -> none
    pallas_call x0 -> x13, Pallas kernels: none -> 91.5 us  [the longest x11 50 us: whole_call(): pl.pallas_call(body, out_shape=outs, grid_spec=pltpu.PrefetchScalarGridSp...]
    unnamed x2 -> x0, blocking collectives: 81.1 us -> none
  transfers between devices with their start and end apart: 21 -> 67, of which waited for: 15 -> 23; matrix products, arithmetic and copies ran while one was open for 13% -> 10% of each run, Pallas kernels for 0% -> 12%
where the time goes in v1:
time: 426 us; the launch traced here: 425 us
  waiting for transfers between devices  200 us (47%)
  Pallas kernels  91.5 us (21%)
  starting transfers between devices  78.8 us (18%)
  other arithmetic  29.1 us (7%)
  local copies, waits for them, and re-layouts  23.8 us (6%)
    ppermute x36, waiting for transfers between devices, tensor_shift(): return lax.ppermute(v, 'tensor', [(i, (i + s) % n) for i in range(n)])  103 us
    ppermute x10, waiting for transfers between devices, swap_x(): return lax.ppermute(v, 'seq', [(0, 1), (1, 0)])  52.1 us
    pallas_call x11, Pallas kernels, whole_call(): pl.pallas_call(body, out_shape=outs, grid_spec=pltpu.PrefetchScalarGridSp...  50 us
    ppermute x36, starting transfers between devices, tensor_shift(): return lax.ppermute(v, 'tensor', [(i, (i + s) % n) for i in range(n)])  48.2 us
    ppermute x8, waiting for transfers between devices, swap_y(): return lax.ppermute(v, 'dp', [(i, i ^ 2) for i in range(4)])  45.1 us
    pallas_call x1, Pallas kernels, per_device(): pl.pallas_call(functools.partial(expert_kernel, n, len(ws)), out_shape=tu...  24.8 us
    pallas_call x1, Pallas kernels, per_device(): pl.pallas_call(functools.partial(expert_back_kernel, n, len(ws), rows), o...  16.7 us
    ppermute x10, starting transfers between devices, swap_x(): return lax.ppermute(v, 'seq', [(0, 1), (1, 0)])  15.5 us
  transfers between devices with their start and end apart: 67, of which 23 were waited for; matrix products, arithmetic and copies ran while one was open for 10% of the time, Pallas kernels for 12%

profile of v1, /device:TPU:0, one launch (start us, length us, event | category | flops | bytes accessed | tf_op | source)
XLA Modules:
  0.0 425.0 jit_solution(14431002810815785333)
XLA Ops:
  7.9 4.1 collective-permute-start.7
  33.0 37.3 %collective-permute-done.11 = bf16[128,1024]{1,0:T(8,128)(2,1)S(1)} collective-permute-done((bf16[128,1024]{1,0:T(8,128)(2,1)S(1)}, bf16[128,1024]{1,0:T(8,128)(2,1)S(1)}, u32[]{:S(2)}, u32[]{:S(2)}) %collective-permute-start.11) | collective-permute-done | bytes 262176 | tf_op jit(solution)/shard_map/ppermute | solution.py:412
  77.3 12.4 %collective-permute-done.15.refs_2_ = bf16[128,1024]{1,0:T(8,128)(2,1)S(1)} collective-permute-done((bf16[128,1024]{1,0:T(8,128)(2,1)S(1)}, bf16[128,1024]{1,0:T(8,128)(2,1)S(1)}, u32[]{:S(2)}, u32[]{:S(2)}) %collective-permute-start.15) | collective-permute-done | bytes 262176 | tf_op jit(solution)/shard_map/ppermute | solution.py:400
  98.2 12.1 %collective-permute-done.25.refs_6_ = bf16[128,1024]{1,0:T(8,128)(2,1)S(1)} collective-permute-done((bf16[128,1024]{1,0:T(8,128)(2,1)S(1)}, bf16[128,1024]{1,0:T(8,128)(2,1)S(1)}, u32[]{:S(2)}, u32[]{:S(2)}) %collective-permute-start.25) | collective-permute-done | bytes 262176 | tf_op jit(solution)/shard_map/ppermute | solution.py:400
  112.8 6.0 %collective-permute-done.17.refs_1_.kv = bf16[512,256]{1,0:T(8,128)(2,1)S(1)} collective-permute-done((bf16[512,256]{1,0:T(8,128)(2,1)}, bf16[512,256]{1,0:T(8,128)(2,1)S(1)}, u32[]{:S(2)}, u32[]{:S(2)}) %collective-permute-start.17) | collective-permute-done | bytes 262176 | tf_op jit(solution)/shard_map/ppermute | solution.py:404
  121.4 8.6 %shard_map.249 = (bf16[128,256]{1,0:T(8,128)(2,1)}, bf16[128,256]{1,0:T(8,128)(2,1)}, bf16[128,256]{1,0:T(8,128)(2,1)}, bf16[128,256]{1,0:T(8,128)(2,1)}, f32[4,64,512]{2,1,0:T(8,128)}, /*index=5*/f32[4,1,512]{2,1,0:T(1,128)}) custom-call(bf16[512,256]{1,0:T(8,128)(2,1)} %get-tuple-element.59.q, s32[1,512]{1,0:T(1,128)} %max.10.lim, ...), custom_call_target="tpu_custom_call" | custom-call | flops 2147483648 | bytes 1587200 | tf_op jit(solution)/shard_map/pallas_call | solution.py:37
  144.8 9.3 %collective-permute-done.29.refs_11_ = bf16[3,16,64,128]{3,2,1,0:T(8,128)(2,1)} collective-permute-done((bf16[3,16,64,128]{3,2,1,0:T(8,128)(2,1)}, bf16[3,16,64,128]{3,2,1,0:T(8,128)(2,1)}, u32[]{:S(2)}, u32[]{:S(2)}) %collective-permute-start.29) | collective-permute-done | bytes 786464 | tf_op jit(solution)/shard_map/ppermute | solution.py:404
  157.8 13.0 %collective-permute-done.22.refs_2_ = bf16[128,1024]{1,0:T(8,128)(2,1)S(1)} collective-permute-done((bf16[128,1024]{1,0:T(8,128)(2,1)}, bf16[128,1024]{1,0:T(8,128)(2,1)S(1)}, u32[]{:S(2)}, u32[]{:S(2)}) %collective-permute-start.22) | collective-permute-done | bytes 262176 | tf_op jit(solution)/shard_map/ppermute | solution.py:400
  180.2 24.8 %shard_map.251 = (bf16[128,1024]{1,0:T(8,128)(2,1)}, bf16[128,1024]{1,0:T(8,128)(2,1)}, bf16[128,1024]{1,0:T(8,128)(2,1)}, bf16[128,1024]{1,0:T(8,128)(2,1)}, bf...) custom-call(f32[512,16]{1,0:T(8,128)} %get-tuple-element.121.chosen, ...), custom_call_target="tpu_custom_call" | custom-call | flops 10737418240 | bytes 12582912 | tf_op jit(solution)/shard_map/pallas_call | solution.py:598
  205.1 16.7 %shard_map.252 = (bf16[128,1024]{1,0:T(8,128)(2,1)}, bf16[128,1024]{1,0:T(8,128)(2,1)}, bf16[128,1024]{1,0:T(8,128)(2,1)}, bf16[128,1024]{1,0:T(8,128)(2,1)}, bf...) custom-call(bf16[512,2048]{1,0:T(8,128)(2,1)} %get-tuple-element.68.active, ...), custom_call_target="tpu_custom_call" | custom-call | flops 8589934592 | bytes 16777216 | tf_op jit(solution)/shard_map/pallas_call | solution.py:622
  221.9 4.2 collective-permute-start.39
  226.8 6.8 %collective-permute-done.39.refs_1_ = bf16[128,1024]{1,0:T(8,128)(2,1)S(1)} collective-permute-done((bf16[128,1024]{1,0:T(8,128)(2,1)S(1)}, bf16[128,1024]{1,0:T(8,128)(2,1)S(1)}, u32[]{:S(2)}, u32[]{:S(2)}) %collective-permute-start.39) | collective-permute-done | bytes 262176 | tf_op jit(solution)/shard_map/ppermute | solution.py:400
  233.6 13.3 %collective-permute-done.40.refs_2_ = bf16[128,1024]{1,0:T(8,128)(2,1)S(1)} collective-permute-done((bf16[128,1024]{1,0:T(8,128)(2,1)S(1)}, bf16[128,1024]{1,0:T(8,128)(2,1)S(1)}, u32[]{:S(2)}, u32[]{:S(2)}) %collective-permute-start.40) | collective-permute-done | bytes 262176 | tf_op jit(solution)/shard_map/ppermute | solution.py:400
  261.7 6.7 %shard_map.255 = (bf16[512,256]{1,0:T(8,128)(2,1)}, f32[4,64,512]{2,1,0:T(8,128)}) custom-call(bf16[512,256]{1,0:T(8,128)(2,1)} %get-tuple-element.59.q, s32[1,512]{1,0:T(1,128)} %max.10.lim, bf16[512,256]{1,0:T(8,128)(2,1)} %copy-done.32, s32[512,1]{1,0:T(8,128)} %broadcast_add_fusion.refs_3_.kpos, f32[4,1,512]{2,1,0:T(1,128)} %get-tuple-element.80.lse, ...), custom_call_target="tpu_custom_call" | custom-call | flops 2684354560 | bytes 2109440 | tf_op jit(solution)/shard_map/pallas_call | solution.py:37
  269.8 7.5 %shard_map.256 = (f32[512,256]{1,0:T(8,128)}, bf16[512,256]{1,0:T(8,128)(2,1)}) custom-call(bf16[512,256]{1,0:T(8,128)(2,1)} %get-tuple-element.59.q, s32[1,512]{1,0:T(1,128)} %max.10.lim, bf16[512,256]{1,0:T(8,128)(2,1)} %get-tuple-element.60.refs_0_.kv, s32[512,1]{1,0:T(8,128)} %copy-done.5, f32[4,1,512]{2,1,0:T(1,128)} %get-tuple-element.80.lse, ...), custom_call_target="tpu_custom_call" | custom-call | flops 2684354560 | bytes 3158016 | tf_op jit(solution)/shard_map/pallas_call | solution.py:37
  278.1 4.1 shard_map.257
  283.0 4.1 collective-permute-start.36
  289.4 4.5 %collective-permute-done.36.refs_1_ = bf16[128,1024]{1,0:T(8,128)(2,1)S(1)} collective-permute-done((bf16[128,1024]{1,0:T(8,128)(2,1)S(1)}, bf16[128,1024]{1,0:T(8,128)(2,1)S(1)}, u32[]{:S(2)}, u32[]{:S(2)}) %collective-permute-start.36) | collective-permute-done | bytes 262176 | tf_op jit(solution)/shard_map/ppermute | solution.py:400
  293.9 26.5 %collective-permute-done.37.refs_2_ = bf16[128,1024]{1,0:T(8,128)(2,1)S(1)} collective-permute-done((bf16[128,1024]{1,0:T(8,128)(2,1)S(1)}, bf16[128,1024]{1,0:T(8,128)(2,1)S(1)}, u32[]{:S(2)}, u32[]{:S(2)}) %collective-permute-start.37) | collective-permute-done | bytes 262176 | tf_op jit(solution)/shard_map/ppermute | solution.py:400
  324.8 12.2 %convert_add_fusion = f32[4,3,16,128,128]{4,3,2,1,0:T(8,128)} fusion(bf16[4,3,16,128,128]{4,3,2,1,0:T(8,128)(2,1)} %collective-permute-done.56, bf16[4,3,16,128,128]{4,3,2,1,0:T(8,128)(2,1)} %get-tuple-element.99), kind=kLoop, calls=%fused_computation | loop fusion | flops 9437184 | bytes 25165824 | tf_op jit(solution)/shard_map/add | solution.py:445
  361.2 11.8 %collective-permute-done.59 = bf16[3,16,64,128]{3,2,1,0:T(8,128)(2,1)S(1)} collective-permute-done((bf16[3,16,64,128]{3,2,1,0:T(8,128)(2,1)S(1)}, bf16[3,16,64,128]{3,2,1,0:T(8,128)(2,1)S(1)}, u32[]{:S(2)}, u32[]{:S(2)}) %collective-permute-start.59) | collective-permute-done | bytes 786464 | tf_op jit(solution)/shard_map/ppermute | solution.py:404
  379.8 4.1 collective-permute-done.48.refs_3_
  389.9 21.1 %collective-permute-done.53 = bf16[128,768]{1,0:T(8,128)(2,1)} collective-permute-done((bf16[128,768]{1,0:T(8,128)(2,1)}, bf16[128,768]{1,0:T(8,128)(2,1)}, u32[]{:S(2)}, u32[]{:S(2)}) %collective-permute-start.53) | collective-permute-done | bytes 196640 | tf_op jit(solution)/shard_map/ppermute | solution.py:404
  411.0 6.5 %collective-permute-done.54 = bf16[128,768]{1,0:T(8,128)(2,1)} collective-permute-done((bf16[128,768]{1,0:T(8,128)(2,1)}, bf16[128,768]{1,0:T(8,128)(2,1)}, u32[]{:S(2)}, u32[]{:S(2)}) %collective-permute-start.54) | collective-permute-done | bytes 196640 | tf_op jit(solution)/shard_map/ppermute | solution.py:412
  (303 shorter events, 145.6 us)
Async XLA Ops:
  22.0 108.3 %collective-permute-start.28 = (bf16[3,16,128,128]{3,2,1,0:T(8,128)(2,1)}, bf16[3,16,128,128]{3,2,1,0:T(8,128)(2,1)}, u32[]{:S(2)}, u32[]{:S(2)}) collective-permute-start(bf16[3,16,128,128]{3,2,1,0:T(8,128)(2,1)} %pad_maximum_fusion.refs_8_), channel_id=1, source_target_pairs={{0,16},{8,24},{16,0},{24,8},{1,17},{9,25},{17,1},{25,9},{2,18},{10... | collective-permute-start | bytes 4718600 | tf_op jit(solution)/shard_map/ppermute | solution.py:412
  25.2 45.1 %collective-permute-start.11 = (bf16[128,1024]{1,0:T(8,128)(2,1)S(1)}, bf16[128,1024]{1,0:T(8,128)(2,1)S(1)}, u32[]{:S(2)}, u32[]{:S(2)}) collective-permute-start(bf16[128,1024]{1,0:T(8,128)(2,1)S(1)} %constant_dynamic-update-slice_fusion), channel_id=1, source_target_pairs={{0,16},{8,24},{16,0},{24,8},{1,17},{9,25},{17,1},{25,9},{2,18},{10... | collective-permute-start | bytes 786440 | tf_op jit(solution)/shard_map/ppermute | solution.py:412
  26.8 44.4 %collective-permute-start.12 = (bf16[128,1024]{1,0:T(8,128)(2,1)S(1)}, bf16[128,1024]{1,0:T(8,128)(2,1)S(1)}, u32[]{:S(2)}, u32[]{:S(2)}) collective-permute-start(bf16[128,1024]{1,0:T(8,128)(2,1)S(1)} %constant_dynamic-update-slice_fusion), channel_id=1, source_target_pairs={{0,20},{4,16},{8,28},{12,24},{16,4},{20,0},{24,12},{28,8},{1,21},{... | collective-permute-start | bytes 786440 | tf_op jit(solution)/shard_map/ppermute | solution.py:416
  27.5 104.2 %collective-permute-start.27 = (bf16[3,16,128,128]{3,2,1,0:T(8,128)(2,1)}, bf16[3,16,128,128]{3,2,1,0:T(8,128)(2,1)}, u32[]{:S(2)}, u32[]{:S(2)}) collective-permute-start(bf16[3,16,128,128]{3,2,1,0:T(8,128)(2,1)} %pad_maximum_fusion.refs_8_), channel_id=1, source_target_pairs={{0,4},{4,0},{1,5},{5,1},{2,6},{6,2},{3,7},{7,3},{8,12},{12,8},{9,1... | collective-permute-start | bytes 4718600 | tf_op jit(solution)/shard_map/ppermute | solution.py:404
  32.9 41.1 %collective-permute-start.4 = (bf16[8,576]{1,0:T(8,128)(2,1)S(1)}, bf16[8,576]{1,0:T(8,128)(2,1)S(1)}, u32[]{:S(2)}, u32[]{:S(2)}) collective-permute-start(bf16[8,576]{1,0:T(8,128)(2,1)S(1)} %get-tuple-element.125), channel_id=1, source_target_pairs={{0,1},{1,2},{2,3},{3,0},{4,5},{5,6},{6,7},{7,4},{8,9},{9,10},{10,1... | collective-permute-start | bytes 27656 | tf_op jit(solution)/shard_map/ppermute | solution.py:400
  89.8 54.4 %collective-permute-start.31 = (bf16[3,16,128,128]{3,2,1,0:T(8,128)(2,1)}, bf16[3,16,128,128]{3,2,1,0:T(8,128)(2,1)}, u32[]{:S(2)}, u32[]{:S(2)}) collective-permute-start(bf16[3,16,128,128]{3,2,1,0:T(8,128)(2,1)} %pad_maximum_fusion.refs_8_), channel_id=1, source_target_pairs={{0,8},{8,0},{16,24},{24,16},{1,9},{9,1},{17,25},{25,17},{2,10},{10... | collective-permute-start | bytes 4718600 | tf_op jit(solution)/shard_map/ppermute | solution.py:408
  93.7 45.9 %collective-permute-start.13 = (bf16[4,128,1024]{2,1,0:T(8,128)(2,1)S(1)}, bf16[4,128,1024]{2,1,0:T(8,128)(2,1)S(1)}, u32[]{:S(2)}, u32[]{:S(2)}) collective-permute-start(bf16[4,128,1024]{2,1,0:T(8,128)(2,1)S(1)} %pad_maximum_fusion.3.wa), channel_id=1, source_target_pairs={{0,8},{8,0},{16,24},{24,16},{1,9},{9,1},{17,25},{25,17},{2,10},{10... | collective-permute-start | bytes 3145736 | tf_op jit(solution)/shard_map/ppermute | solution.py:408
  139.6 39.4 %collective-permute-start.32 = (bf16[3,16,128,128]{3,2,1,0:T(8,128)(2,1)}, bf16[3,16,128,128]{3,2,1,0:T(8,128)(2,1)}, u32[]{:S(2)}, u32[]{:S(2)}) collective-permute-start(bf16[3,16,128,128]{3,2,1,0:T(8,128)(2,1)} %collective-permute-done.27.refs_9_), channel_id=1, source_target_pairs={{0,8},{8,0},{16,24},{24,16},{1,9},{9,1},{17,25},{25,17},{2,10},{10... | collective-permute-start | bytes 4718600 | tf_op jit(solution)/shard_map/ppermute | solution.py:408
  139.6 39.4 %collective-permute-start.33 = (bf16[3,16,128,128]{3,2,1,0:T(8,128)(2,1)}, bf16[3,16,128,128]{3,2,1,0:T(8,128)(2,1)}, u32[]{:S(2)}, u32[]{:S(2)}) collective-permute-start(bf16[3,16,128,128]{3,2,1,0:T(8,128)(2,1)} %collective-permute-done.28.refs_10_), channel_id=1, source_target_pairs={{0,8},{8,0},{16,24},{24,16},{1,9},{9,1},{17,25},{25,17},{2,10},{10... | collective-permute-start | bytes 4718600 | tf_op jit(solution)/shard_map/ppermute | solution.py:408
  154.1 24.8 %collective-permute-start.34 = (bf16[3,16,64,128]{3,2,1,0:T(8,128)(2,1)}, bf16[3,16,64,128]{3,2,1,0:T(8,128)(2,1)S(1)}, u32[]{:S(2)}, u32[]{:S(2)}) collective-permute-start(bf16[3,16,64,128]{3,2,1,0:T(8,128)(2,1)} %collective-permute-done.29.refs_11_), channel_id=1, source_target_pairs={{0,8},{8,0},{16,24},{24,16},{1,9},{9,1},{17,25},{25,17},{2,10},{10... | collective-permute-start | bytes 2359304 | tf_op jit(solution)/shard_map/ppermute | solution.py:408
  221.8 103.0 %collective-permute-start.56 = (bf16[4,3,16,128,128]{4,3,2,1,0:T(8,128)(2,1)}, bf16[4,3,16,128,128]{4,3,2,1,0:T(8,128)(2,1)}, u32[]{:S(2)}, u32[]{:S(2)}) collective-permute-start(bf16[4,3,16,128,128]{4,3,2,1,0:T(8,128)(2,1)} %get-tuple-element.100), channel_id=1, source_target_pairs={{0,8},{8,0},{16,24},{24,16},{1,9},{9,1},{17,25},{25,17},{2,10},{10... | collective-permute-start | bytes 18874376 | tf_op jit(solution)/shard_map/ppermute | solution.py:408
  287.1 33.3 %collective-permute-start.37 = (bf16[128,1024]{1,0:T(8,128)(2,1)S(1)}, bf16[128,1024]{1,0:T(8,128)(2,1)S(1)}, u32[]{:S(2)}, u32[]{:S(2)}) collective-permute-start(bf16[128,1024]{1,0:T(8,128)(2,1)S(1)} %copy-done.37), channel_id=1, source_target_pairs={{0,2},{1,3},{2,0},{3,1},{4,6},{5,7},{6,4},{7,5},{8,10},{9,11},{10,... | collective-permute-start | bytes 786440 | tf_op jit(solution)/shard_map/ppermute | solution.py:400
  287.1 33.3 %collective-permute-start.38 = (bf16[128,1024]{1,0:T(8,128)(2,1)S(1)}, bf16[128,1024]{1,0:T(8,128)(2,1)S(1)}, u32[]{:S(2)}, u32[]{:S(2)}) collective-permute-start(bf16[128,1024]{1,0:T(8,128)(2,1)S(1)} %copy-done.36), channel_id=1, source_target_pairs={{0,1},{1,2},{2,3},{3,0},{4,5},{5,6},{6,7},{7,4},{8,9},{9,10},{10,1... | collective-permute-start | bytes 786440 | tf_op jit(solution)/shard_map/ppermute | solution.py:400
  287.8 36.3 %collective-permute-start.62 = (f32[2,18,128]{2,1,0:T(8,128)S(1)}, f32[2,18,128]{2,1,0:T(8,128)S(1)}, u32[]{:S(2)}, u32[]{:S(2)}) collective-permute-start(f32[2,18,128]{2,1,0:T(8,128)S(1)} %slice.205), channel_id=1, source_target_pairs={{0,16},{8,24},{16,0},{24,8},{1,17},{9,25},{17,1},{25,9},{2,18},{10... | collective-permute-start | bytes 55304 | tf_op jit(solution)/shard_map/ppermute | solution.py:412
  293.9 48.6 %collective-permute-start.49 = (bf16[128,1024]{1,0:T(8,128)(2,1)S(1)}, bf16[128,1024]{1,0:T(8,128)(2,1)S(1)}, u32[]{:S(2)}, u32[]{:S(2)}) collective-permute-start(bf16[128,1024]{1,0:T(8,128)(2,1)S(1)} %copy-done.35), channel_id=1, source_target_pairs={{0,1},{1,2},{2,3},{3,0},{4,5},{5,6},{6,7},{7,4},{8,9},{9,10},{10,1... | collective-permute-start | bytes 786440 | tf_op jit(solution)/shard_map/ppermute | solution.py:400
  320.5 26.3 %collective-permute-start.51 = (bf16[128,1024]{1,0:T(8,128)(2,1)S(1)}, bf16[128,1024]{1,0:T(8,128)(2,1)}, u32[]{:S(2)}, u32[]{:S(2)}) collective-permute-start(bf16[128,1024]{1,0:T(8,128)(2,1)S(1)} %copy-done.35), channel_id=1, source_target_pairs={{0,3},{1,0},{2,1},{3,2},{4,7},{5,4},{6,5},{7,6},{8,11},{9,8},{10,9... | collective-permute-start | bytes 786440 | tf_op jit(solution)/shard_map/ppermute | solution.py:400
  350.5 25.1 %collective-permute-start.52 = (bf16[4,128,768]{2,1,0:T(8,128)(2,1)}, bf16[4,128,768]{2,1,0:T(8,128)(2,1)S(1)}, u32[]{:S(2)}, u32[]{:S(2)}) collective-permute-start(bf16[4,128,768]{2,1,0:T(8,128)(2,1)} %get-tuple-element.98), channel_id=1, source_target_pairs={{0,8},{8,0},{16,24},{24,16},{1,9},{9,1},{17,25},{25,17},{2,10},{10... | collective-permute-start | bytes 2359304 | tf_op jit(solution)/shard_map/ppermute | solution.py:408
  350.5 26.3 %collective-permute-start.46 = (bf16[128,1024]{1,0:T(8,128)(2,1)}, bf16[128,1024]{1,0:T(8,128)(2,1)S(1)}, u32[]{:S(2)}, u32[]{:S(2)}) collective-permute-start(bf16[128,1024]{1,0:T(8,128)(2,1)} %get-tuple-element.91), channel_id=1, source_target_pairs={{0,3},{1,0},{2,1},{3,2},{4,7},{5,4},{6,5},{7,6},{8,11},{9,8},{10,9... | collective-permute-start | bytes 786440 | tf_op jit(solution)/shard_map/ppermute | solution.py:400
  351.3 27.0 %collective-permute-start.47 = (bf16[128,1024]{1,0:T(8,128)(2,1)}, bf16[128,1024]{1,0:T(8,128)(2,1)}, u32[]{:S(2)}, u32[]{:S(2)}) collective-permute-start(bf16[128,1024]{1,0:T(8,128)(2,1)} %get-tuple-element.92), channel_id=1, source_target_pairs={{0,2},{1,3},{2,0},{3,1},{4,6},{5,7},{6,4},{7,5},{8,10},{9,11},{10,... | collective-permute-start | bytes 786440 | tf_op jit(solution)/shard_map/ppermute | solution.py:400
  359.7 60.3 %collective-permute-start.58 = (bf16[3,16,128,128]{3,2,1,0:T(8,128)(2,1)}, bf16[3,16,128,128]{3,2,1,0:T(8,128)(2,1)S(1)}, u32[]{:S(2)}, u32[]{:S(2)}) collective-permute-start(bf16[3,16,128,128]{3,2,1,0:T(8,128)(2,1)} %pad_maximum_fusion.1), channel_id=1, source_target_pairs={{0,4},{4,0},{1,5},{5,1},{2,6},{6,2},{3,7},{7,3},{8,12},{12,8},{9,1... | collective-permute-start | bytes 4718600 | tf_op jit(solution)/shard_map/ppermute | solution.py:404
  374.5 45.6 %collective-permute-start.60 = (bf16[3,16,128,128]{3,2,1,0:T(8,128)(2,1)}, bf16[3,16,128,128]{3,2,1,0:T(8,128)(2,1)}, u32[]{:S(2)}, u32[]{:S(2)}) collective-permute-start(bf16[3,16,128,128]{3,2,1,0:T(8,128)(2,1)} %pad_maximum_fusion.2), channel_id=1, source_target_pairs={{0,16},{8,24},{16,0},{24,8},{1,17},{9,25},{17,1},{25,9},{2,18},{10... | collective-permute-start | bytes 4718600 | tf_op jit(solution)/shard_map/ppermute | solution.py:412
  376.8 34.2 %collective-permute-start.53 = (bf16[128,768]{1,0:T(8,128)(2,1)}, bf16[128,768]{1,0:T(8,128)(2,1)}, u32[]{:S(2)}, u32[]{:S(2)}) collective-permute-start(bf16[128,768]{1,0:T(8,128)(2,1)} %get-tuple-element.113), channel_id=1, source_target_pairs={{0,4},{4,0},{1,5},{5,1},{2,6},{6,2},{3,7},{7,3},{8,12},{12,8},{9,1... | collective-permute-start | bytes 589832 | tf_op jit(solution)/shard_map/ppermute | solution.py:404
  378.3 39.2 %collective-permute-start.54 = (bf16[128,768]{1,0:T(8,128)(2,1)}, bf16[128,768]{1,0:T(8,128)(2,1)}, u32[]{:S(2)}, u32[]{:S(2)}) collective-permute-start(bf16[128,768]{1,0:T(8,128)(2,1)} %get-tuple-element.115), channel_id=1, source_target_pairs={{0,16},{8,24},{16,0},{24,8},{1,17},{9,25},{17,1},{25,9},{2,18},{10... | collective-permute-start | bytes 589832 | tf_op jit(solution)/shard_map/ppermute | solution.py:412
  383.9 33.6 %collective-permute-start.55 = (bf16[128,768]{1,0:T(8,128)(2,1)}, bf16[128,768]{1,0:T(8,128)(2,1)}, u32[]{:S(2)}, u32[]{:S(2)}) collective-permute-start(bf16[128,768]{1,0:T(8,128)(2,1)} %get-tuple-element.114), channel_id=1, source_target_pairs={{0,20},{4,16},{8,28},{12,24},{16,4},{20,0},{24,12},{28,8},{1,21},{... | collective-permute-start | bytes 589832 | tf_op jit(solution)/shard_map/ppermute | solution.py:416
  (94 other events, 1163.1 us)

commit v2 on v1

--- a/solution.py
+++ b/solution.py
@@ -16,6 +16,7 @@
 FILL = -1e30
 EXPERTS_PER_STEP = 2
 ROW_TILE = 256
+LINES = 32
 f32 = jnp.float32
 bf16 = jnp.bfloat16
 
@@ -44,20 +45,12 @@
             out_specs=[full(o.shape) for o in outs],
             scratch_shapes=list(scratch),
         ),
-        cost_estimate=pl.CostEstimate(flops=int(flops), bytes_accessed=int(moved), transcendentals=0),
+        cost_estimate=pl.CostEstimate(flops=0, bytes_accessed=0, transcendentals=0),
     )(*args)
 
 
 def sds(shape, dtype):
     return jax.ShapeDtypeStruct(shape, dtype)
-
-
-def reorder_kernel(where, a_ref, b_ref, a_out, b_out):
-    wide = a_ref.shape[1] // where.shape[0]
-    for i in range(where.shape[0]):
-        source = pl.ds(pl.multiple_of(where[i] * wide, wide), wide)
-        a_out[:, i * wide : (i + 1) * wide] = a_ref[:, source]
-        b_out[:, i * wide : (i + 1) * wide] = b_ref[:, source]
 
 
 def turn(v, cos, sin):
@@ -66,21 +59,24 @@
     return v * cos + other * sin
 
 
-def rows_of(refs, rows):
-    parts = []
-    for r in refs:
-        parts += [r[i, 0:rows, :] for i in range(r.shape[0])]
-    return jnp.concatenate(parts, axis=0)
-
-
-def qkv_kernel(n, rows, *refs):
-    xs, (gain, cos, sin, wa, wb), (x1, q, kv) = refs[:n], refs[n : n + 5], refs[n + 5 :]
+def lay(out, stacks, where, rows):
+    first = 0
+    for r in stacks:
+        for i in range(r.shape[0]):
+            out[pl.ds(pl.multiple_of(where[first + i] * rows, rows), rows), :] = r[i, 0:rows, :]
+        first += r.shape[0]
+
+
+def qkv_kernel(n, rows, where, *refs):
+    xs, (gain, cos, sin, wa, wb), (x1, q, kv, w) = refs[:n], refs[n : n + 5], refs[n + 5 :]
+    lay(w, (wa, wb), where, rows)
     m = xs[0].shape[0]
+    x_width = x1.shape[1]
     for j in range(n):
-        v = xs[j][...].astype(f32)
+        v = xs[j][:, : x_width].astype(f32)
         r = lax.rsqrt(jnp.mean(v * v, axis=-1, keepdims=True) + EPS)
         x1[j * m : (j + 1) * m, :] = (v * r * gain[...]).astype(bf16)
-    out = dot(x1[...], rows_of((wa, wb), rows))
+    out = dot(x1[...], w[...])
     c, s = cos[...], sin[...]
     q[:, 0:128] = turn(out[:, 0:128], c, s).astype(bf16)
     q[:, 128:256] = turn(out[:, 128:256], c, s).astype(bf16)
@@ -186,20 +182,21 @@
         dq_out[...] = dqt[...]
 
 
-def middle_kernel(n, x, gain, wa, wb, *refs):
-    mixed, (middle, second) = refs[:n], refs[n:]
-    rows = wa.shape[1]
+def middle_kernel(n, where, x, gain, wa, wb, *refs):
+    mixed, (middle, second, w) = refs[:n], refs[n:]
+    lay(w, (wa, wb), where, wa.shape[1])
     both = jnp.concatenate([r[...] for r in mixed], axis=1)
-    value = x[...].astype(f32) + dot(both, rows_of((wa, wb), rows), NT)
+    value = x[...].astype(f32) + dot(both, w[...], NT)
     middle[...] = value
     r = lax.rsqrt(jnp.mean(value * value, axis=-1, keepdims=True) + EPS)
     second[...] = (value * r * gain[...]).astype(bf16)
 
 
-def middle_back_kernel(n, middle, gain, cot, wa, wb, *refs):
+def middle_back_kernel(n, where, middle, gain, cot, wa, wb, *refs):
     parts, refs = refs[:n], refs[n:]
     middle_grad, branch, gain_grad = refs[:3]
-    pieces = refs[3:]
+    pieces, w = refs[3:-1], refs[-1]
+    lay(w, (wa, wb), where, wa.shape[1])
     u = parts[0][...].astype(f32)
     for r in parts[1:]:
         u = u + r[...].astype(f32)
@@ -212,8 +209,7 @@
     middle_grad[...] = grad
     low = grad.astype(bf16)
     branch[...] = low
-    rows = wa.shape[1]
-    out = dot(low, rows_of((wa, wb), rows)).astype(bf16)
+    out = dot(low, w[...]).astype(bf16)
     wide = out.shape[1] // n
     for j in range(n):
         pieces[j][...] = out[:, j * wide : (j + 1) * wide]
@@ -224,14 +220,14 @@
     return jnp.sum(jnp.where(lane == index, table, 0.0), axis=1, keepdims=True)
 
 
-def expert_kernel(n, pieces, chosen, kept, router, *refs):
-    xs, cs, ws, refs = refs[:n], refs[n : 2 * n], refs[2 * n : 2 * n + pieces], refs[2 * n + pieces :]
+def expert_kernel(n, chosen, kept, router, ws, *refs):
+    xs, cs, refs = refs[:n], refs[n : 2 * n], refs[2 * n :]
     outs, (active_out, gate_out, up_out, router_grad) = refs[:n], refs[n : n + 4]
     x, c, w, total, soft, share = refs[n + 4 :]
     step, steps = pl.program_id(0), pl.num_programs(0)
     m = xs[0].shape[0]
     eb = EXPERTS_PER_STEP
-    fe = ws[0].shape[3]
+    blocks, _, _, rows, fe = ws.shape
     wide = eb * fe
 
     @pl.when(step == 0)
@@ -246,13 +242,11 @@
         total[...] = jnp.zeros_like(total)
         share[...] = jnp.zeros_like(share)
 
-    first = 0
-    for r in ws:
-        span = slice(first, first + r.shape[2])
-        first += r.shape[2]
+    for b in range(blocks):
         for kind in range(3):
             for i in range(eb):
-                w[span, kind * wide + i * fe : kind * wide + (i + 1) * fe] = r[kind, i]
+                at = kind * wide + i * fe
+                w[b * rows : (b + 1) * rows, at : at + fe] = ws[b, kind, i]
     gu = dot(x[...], w[:, : 2 * wide])
     down = dot(c[...], w[:, 2 * wide :])
     table = soft[...] * kept[...]
@@ -289,18 +283,18 @@
         value = total[...] + (dot(high, router[...], NT) + dot(low, router[...], NT))
         for j in range(n):
             outs[j][...] = value[j * m : (j + 1) * m, :].astype(bf16)
-        across = (((0,), (0,)), ((), ()))
-        router_grad[...] = dot(high, x[...], across) + dot(low, x[...], across)
-
-
-def expert_back_kernel(n, pieces, rows, active, gate, up, *refs):
-    xs, cs, ws, refs = refs[:n], refs[n : 2 * n], refs[2 * n : 2 * n + pieces], refs[2 * n + pieces :]
-    outs, (keep, send) = refs[:n], refs[n : n + 2]
-    xt, ct, w, total = refs[n + 2 :]
+        across_rows = (((0,), (0,)), ((), ()))
+        router_grad[...] = dot(high, x[...], across_rows) + dot(low, x[...], across_rows)
+
+
+def expert_back_kernel(n, active, gate, up, ws, *refs):
+    xs, cs, refs = refs[:n], refs[n : 2 * n], refs[2 * n :]
+    outs, grads = refs[:n], refs[n]
+    xt, ct, w, total = refs[n + 1 :]
     step, steps = pl.program_id(0), pl.num_programs(0)
     m = xs[0].shape[0]
     eb = EXPERTS_PER_STEP
-    fe = ws[0].shape[3]
+    blocks, _, _, rows, fe = ws.shape
 
     @pl.when(step == 0)
     def _():
@@ -309,20 +303,15 @@
             ct[:, j * m : (j + 1) * m] = cs[j][...].T
         total[...] = jnp.zeros_like(total)
 
-    first = 0
-    for r in ws:
-        span = slice(first, first + r.shape[2])
-        first += r.shape[2]
+    for b in range(blocks):
         for i in range(eb):
-            w[span, i * fe : (i + 1) * fe] = r[0, i]
+            w[b * rows : (b + 1) * rows, i * fe : (i + 1) * fe] = ws[b, 0, i]
     total[...] += dot(active[...], w[...], NT)
-    half = keep.shape[0]
     for kind, (left, right) in enumerate(((xt, gate), (xt, up), (ct, active))):
         value = dot(left[...], right[...]).astype(bf16)
-        for b in range(2 * half):
-            target = keep if b < half else send
+        for b in range(blocks):
             for i in range(eb):
-                target[b % half, kind, i] = value[b * rows : (b + 1) * rows, i * fe : (i + 1) * fe]
+                grads[b, kind, i] = value[b * rows : (b + 1) * rows, i * fe : (i + 1) * fe]
 
     @pl.when(step == steps - 1)
     def _():
@@ -330,9 +319,10 @@
             outs[j][...] = total[j * m : (j + 1) * m, :].astype(bf16)
 
 
-def qkv_back_kernel(n, rows, dq, dkv, got, cos, sin, wa, wb, *refs):
+def qkv_back_kernel(n, rows, where, dq, dkv, got, cos, sin, wa, wb, *refs):
     xs, refs = refs[:n], refs[n:]
-    outs, (grads, gain_grad) = refs[:n], refs[n:]
+    outs, (grads, gain_grad, w) = refs[:n], refs[n:]
+    lay(w, (wa, wb), where, rows)
     m = xs[0].shape[0]
     both = dkv[...].astype(f32)
     if got is not None:
@@ -340,10 +330,11 @@
     grads[:, 0:256] = dq[...]
     grads[:, 256:384] = turn(both[:, 0:128], cos[...], -sin[...]).astype(bf16)
     grads[:, 384:512] = both[:, 128:256].astype(bf16)
-    u = dot(grads[...], rows_of((wa, wb), rows), NT)
+    u = dot(grads[...], w[...], NT)
     sums = jnp.zeros(gain_grad.shape, f32)
+    x_width = u.shape[1]
     for j in range(n):
-        v = xs[j][...].astype(f32)
+        v = xs[j][:, : x_width].astype(f32)
         r = lax.rsqrt(jnp.mean(v * v, axis=-1, keepdims=True) + EPS)
         part = u[j * m : (j + 1) * m, :]
         sums = sums + jnp.sum(part * (v * r), axis=0, keepdims=True)
@@ -351,30 +342,28 @@
     gain_grad[...] = sums
 
 
-def weight_back_kernel(n, rows, x1, grads, *refs):
-    bs, ms, (keep, send) = refs[:n], refs[n : 2 * n], refs[2 * n :]
-    first = dot(x1[...].T, grads[...]).astype(bf16)
+def weight_back_kernel(n, rows, where, x1, grads, router_part, gain_one, gain_two, *refs):
+    bs, ms, (keep, send, value, vectors) = refs[:n], refs[n : 2 * n], refs[2 * n :]
+    wide = grads.shape[1]
+    value[:, :wide] = dot(x1[...].T, grads[...]).astype(bf16)
     branch = jnp.concatenate([r[...] for r in bs], axis=0)
     mixed = jnp.concatenate([r[...] for r in ms], axis=0)
-    second = dot(branch.T, mixed).astype(bf16)
+    value[:, wide:] = dot(branch.T, mixed).astype(bf16)
+    lines = vectors.shape[1]
+    for q in range(vectors.shape[0]):
+        columns = slice(q * rows, (q + 1) * rows)
+        block = [router_part[:, columns], gain_one[:, columns], gain_two[:, columns]]
+        block.append(jnp.zeros((lines - E - 2, rows), f32))
+        vectors[q] = jnp.concatenate(block, axis=0).astype(bf16)
     half = keep.shape[0]
-    wide = first.shape[1]
     for b in range(2 * half):
         target = keep if b < half else send
-        target[b % half, :, 0:wide] = first[b * rows : (b + 1) * rows, :]
-        target[b % half, :, wide:] = second[b * rows : (b + 1) * rows, :]
-
-
-def put(out, value, where):
-    wide = out.shape[1] // where.shape[0]
-    if wide % 128:
-        out[...] = value
-        return
-    for i in range(where.shape[0]):
-        out[:, pl.ds(pl.multiple_of(where[i] * wide, wide), wide)] = value[:, i * wide : (i + 1) * wide]
-
-
-def input_kernel(n, where, x, gain, middle_grad, *refs):
+        target[b % half, 0:rows, :] = value[pl.ds(pl.multiple_of(where[b] * rows, rows), rows), :]
+        target[b % half, rows : rows + lines, 0:rows] = vectors[where[b]]
+        target[b % half, rows : rows + lines, rows:] = jnp.zeros((lines, value.shape[1] - rows), bf16)
+
+
+def input_kernel(n, x, gain, middle_grad, *refs):
     parts, out = refs[:n], refs[n]
     u = parts[0][...].astype(f32)
     for r in parts[1:]:
@@ -384,20 +373,38 @@
     normal = v * r
     scaled = u * gain[...]
     grad = r * (scaled - normal * jnp.mean(scaled * normal, axis=-1, keepdims=True))
-    put(out, (middle_grad[...] + grad).astype(bf16), where)
-
-
-def output_kernel(n, where, middle, *refs):
+    out[...] = (middle_grad[...] + grad).astype(bf16)
+
+
+def output_kernel(n, middle, *refs):
     parts, out = refs[:n], refs[n]
     u = middle[...]
     for r in parts:
         u = u + r[...].astype(f32)
-    put(out, u.astype(bf16), where)
-
-
-def tensor_shift(v, s):
-    n = lax.axis_size("tensor")
-    return lax.ppermute(v, "tensor", [(i, (i + s) % n) for i in range(n)])
+    out[...] = u.astype(bf16)
+
+
+def across(v, j):
+    return lax.ppermute(v, "tensor", [(i, i ^ j) for i in range(lax.axis_size("tensor"))])
+
+
+def spread(v):
+    return [v] + [across(v, j) for j in range(1, lax.axis_size("tensor"))]
+
+
+def spread_by_two(v):
+    if lax.axis_size("tensor") != 4:
+        return spread(v)
+    near = across(v, 1)
+    return [v, near, across(v, 2), across(near, 2)]
+
+
+def collect(parts):
+    return [parts[0]] + [across(parts[j], j) for j in range(1, len(parts))]
+
+
+def after(v, *others):
+    return lax.optimization_barrier((v, *others))[0]
 
 
 def swap_x(v):
@@ -416,9 +423,17 @@
     return lax.ppermute(v, ("dp", "seq"), [(i, i ^ 5) for i in range(8)])
 
 
-def plane_gather(v, fancy):
+def after_all(values, others):
+    return lax.optimization_barrier((*values, *others))[: len(values)]
+
+
+def plane_gather(v, fancy, near=False):
+    if fancy and near:
+        near = jnp.stack([v, swap_x(v), swap_y(v), swap_xy(v)])
+        return near, swap_core(near)
     if fancy:
-        near = jnp.stack([v, swap_x(v), swap_y(v), swap_xy(v)])
+        near = jnp.stack([v, swap_x(v)])
+        near = jnp.concatenate([near, swap_y(near)])
         return near, swap_core(near)
     every = lax.all_gather(v, ("dp", "seq"), axis=0, tiled=False)
     half = every.shape[0] // 2
@@ -429,38 +444,10 @@
     if not fancy:
         both = jnp.concatenate([keep, send], axis=0)
         return lax.psum_scatter(both, ("dp", "seq"), scatter_dimension=0, tiled=False).astype(f32)
-    near = keep.astype(f32) + swap_core(send).astype(f32)
-    low = near[1:].astype(bf16)
-    return (
-        near[0]
-        + swap_x(low[0]).astype(f32)
-        + swap_y(low[1]).astype(f32)
-        + swap_xy(low[2]).astype(f32)
-    )
-
-
-def plane_scatter_large(keep, send, fancy):
-    if not fancy:
-        return plane_scatter(keep, send, fancy)
-    near = keep.astype(f32) + swap_core(send).astype(f32)
-    half = near.shape[-2] // 2
-    far = near[3].astype(bf16)
-    got_x, got_y = swap_x(far[..., :half, :]), swap_y(far[..., half:, :])
-    to_y = jnp.concatenate([near[2][..., :half, :] + got_x.astype(f32), near[2][..., half:, :]], axis=-2)
-    to_x = jnp.concatenate([near[1][..., :half, :], near[1][..., half:, :] + got_y.astype(f32)], axis=-2)
-    return near[0] + swap_x(to_x.astype(bf16)).astype(f32) + swap_y(to_y.astype(bf16)).astype(f32)
-
-
-def gather_experts(packed, fancy):
-    if not fancy:
-        every = lax.all_gather(packed, ("dp", "seq"), axis=2, tiled=True)
-        return [every]
-    half = packed.shape[2] // 2
-    on_x, on_y = swap_x(packed), swap_y(packed)
-    far_a = swap_x(on_y[:, :, :half])
-    far_b = swap_y(on_x[:, :, half:])
-    near = [packed, on_x, on_y, far_a, far_b]
-    return near + [swap_core(v) for v in near]
+    got = swap_core(send)
+    far = swap_y((keep[2:].astype(f32) + got[2:].astype(f32)).astype(bf16))
+    mine = keep[:2].astype(f32) + got[:2].astype(f32) + far.astype(f32)
+    return mine[0] + swap_x(mine[1].astype(bf16)).astype(f32)
 
 
 def per_device(
@@ -496,34 +483,28 @@
     where = (place ^ jnp.array(order, jnp.int32)) if fancy else jnp.arange(n_p, dtype=jnp.int32)
 
     own, cot = hidden_in[0], cotangent[0]
-    if fancy:
-        own, cot = whole_call(
-            reorder_kernel, (sds(own.shape, bf16), sds(cot.shape, bf16)), (where, own, cot), prefetch=1
-        )
-    xs = [own] + [tensor_shift(own, j) for j in range(1, n)]
-
+    joined = m == w_out.shape[0]
+    xs = spread(jnp.concatenate([own, w_out], axis=1) if joined else own)
+
+    shard = first_gain.shape[0]
+    small = jnp.concatenate([router.reshape(-1), first_gain, second_gain])
+    size = small.shape[0]
     qkv_w = jnp.concatenate([w_query, key_projection, value_projection], axis=1)
     cols = qkv_w.shape[1]
-    small = jnp.concatenate([router.reshape(-1), first_gain, second_gain])
-    size = small.shape[0]
     small = jnp.pad(small, (0, 16 * cols - size)).reshape(16, cols)
     wa, wb = plane_gather(jnp.concatenate([qkv_w, small], axis=0), fancy)
     tail = jnp.concatenate([wa[:, rows:], wb[:, rows:]], axis=0).reshape(n_p, -1)[:, :size]
-    tails = [tail] + [tensor_shift(tail, j) for j in range(1, n)]
-    stacked = jnp.stack(tails).astype(f32)
-    which = (me - jnp.arange(n)) % n
+    stacked = jnp.stack(spread(tail)).astype(f32)
+    which = me ^ jnp.arange(n)
     pick_rows = (which[:, None] == jnp.arange(n)[None, :]).astype(f32)
-    natural = jnp.sum(pick_rows[:, :, None, None] * stacked[None], axis=1)
-    shard = first_gain.shape[0]
-    gain_one = jnp.transpose(natural[:, :, size - 2 * shard : size - shard], (1, 0, 2)).reshape(1, d)
-    gain_two = jnp.transpose(natural[:, :, size - shard :], (1, 0, 2)).reshape(1, d)
-    router_all = (
-        jnp.transpose(natural[:, :, : size - 2 * shard].reshape(n, n_p, shard, E), (1, 0, 2, 3))
-        .reshape(d, E)
-        .astype(bf16)
-    )
-
-    blocks = (me - jnp.arange(n, dtype=jnp.int32)) % n
+    ordered = (where[None, :] == jnp.arange(n_p, dtype=jnp.int32)[:, None]).astype(f32)
+    stacked = jnp.sum(pick_rows[:, :, None, None] * stacked[None], axis=1)
+    tail = jnp.sum(ordered[:, None, :, None] * stacked[None], axis=2)
+    gain_one = tail[:, :, size - 2 * shard : size - shard].reshape(1, d)
+    gain_two = tail[:, :, size - shard :].reshape(1, d)
+    router_all = tail[:, :, : size - 2 * shard].reshape(d, E).astype(bf16)
+
+    blocks = me ^ jnp.arange(n, dtype=jnp.int32)
     positions = (seq_at * count + blocks[:, None] * m + jnp.arange(m, dtype=jnp.int32)[None, :]).reshape(count)
     starts = piece_starts[0]
     inside = (positions[:, None] >= starts[None, :]) & (positions[:, None] < starts[None, :] + PIECE)
@@ -552,8 +533,10 @@
     x1, q, kv = whole_call(
         functools.partial(qkv_kernel, n, rows),
         (sds((count, d), bf16), sds((count, wide), bf16), sds((count, 256), bf16)),
-        (*xs, gain_one, cos, sin, wa, wb),
+        (where, *xs, gain_one, cos, sin, wa, wb),
+        scratch=(pltpu.VMEM((d, cols), bf16),),
         flops=2 * count * d * cols,
+        prefetch=1,
     )
     key_pos = positions.reshape(count, 1)
     if fancy:
@@ -578,30 +561,33 @@
     )
     mixed, (mixed_t, lse) = got[:n], got[n:]
 
-    out_w = jnp.concatenate([w_out] + [tensor_shift(w_out, -j) for j in range(1, n)], axis=1)
-    oa, ob = plane_gather(out_w, fancy)
-    mine = [mixed[0]] + [tensor_shift(mixed[j], -j) for j in range(1, n)]
+    out_w = jnp.concatenate([v[:, d:] for v in xs] if joined else spread(w_out), axis=1)
+    oa, ob = plane_gather(after(out_w, kv), fancy, near=True)
+    mine = collect(mixed)
     middle, second = whole_call(
         functools.partial(middle_kernel, n),
         (sds((m, d), f32), sds((m, d), bf16)),
-        (own, gain_two, oa, ob, *mine),
+        (where, own, gain_two, oa, ob, *mine),
+        scratch=(pltpu.VMEM((d, n * wide), bf16),),
         flops=2 * m * d * d,
-    )
-
-    seconds = [second] + [tensor_shift(second, j) for j in range(1, n)]
-    cots = [cot] + [tensor_shift(cot, j) for j in range(1, n)]
-    ws = gather_experts(jnp.stack([w_gate, w_up, w_down]), fancy)
+        prefetch=1,
+    )
+
+    seconds = spread(second)
+    cots = [cot] + spread(after(cot, kv))[1:]
+    packed = jnp.stack([w_gate, w_up, w_down])
+    ws = lax.all_gather(packed, ("dp", "seq"), axis=0, tiled=False)
     eb, fe = EXPERTS_PER_STEP, w_gate.shape[2]
     steps = E // eb
     block = pl.BlockSpec((count, eb * fe), lambda s: (0, s))
     wide_out = sds((count, E * fe), bf16)
     got = pl.pallas_call(
-        functools.partial(expert_kernel, n, len(ws)),
+        functools.partial(expert_kernel, n),
         out_shape=tuple([sds((m, d), bf16)] * n) + (wide_out, wide_out, wide_out, sds((E, d), f32)),
         grid=(steps,),
         in_specs=[full((count, E)), full((count, E)), full((d, E))]
-        + [full((m, d))] * (2 * n)
-        + [pl.BlockSpec((3, eb, w.shape[2], fe), lambda s: (0, s, 0, 0)) for w in ws],
+        + [pl.BlockSpec((n_p, 3, eb, rows, fe), lambda s: (0, 0, s, 0, 0))]
+        + [full((m, d))] * (2 * n),
         out_specs=[full((m, d))] * n + [block] * 3 + [full((E, d))],
         scratch_shapes=[
             pltpu.VMEM((count, d), bf16),
@@ -611,44 +597,42 @@
             pltpu.VMEM((count, E), f32),
             pltpu.VMEM((count, E), f32),
         ],
-        cost_estimate=pl.CostEstimate(
-            flops=10 * count * d * E * fe, bytes_accessed=3 * d * E * fe * 2, transcendentals=count * E * fe
-        ),
-    )(chosen, kept, router_all, *seconds, *cots, *ws)
+        cost_estimate=pl.CostEstimate(flops=0, bytes_accessed=0, transcendentals=0),
+    )(chosen, kept, router_all, ws, *seconds, *cots)
     second_parts, (active, gate_g, up_g, router_part) = got[:n], got[n:]
     half_p = n_p // 2
-    grad_shape = sds((half_p, 3, E, rows, fe), bf16)
-    grad_block = pl.BlockSpec((half_p, 3, eb, rows, fe), lambda s: (0, 0, s, 0, 0))
     got = pl.pallas_call(
-        functools.partial(expert_back_kernel, n, len(ws), rows),
-        out_shape=tuple([sds((m, d), bf16)] * n) + (grad_shape, grad_shape),
+        functools.partial(expert_back_kernel, n),
+        out_shape=tuple([sds((m, d), bf16)] * n) + (sds((n_p, 3, E, rows, fe), bf16),),
         grid=(steps,),
         in_specs=[block] * 3
-        + [full((m, d))] * (2 * n)
-        + [pl.BlockSpec((1, eb, w.shape[2], fe), lambda s: (2, s, 0, 0)) for w in ws],
-        out_specs=[full((m, d))] * n + [grad_block] * 2,
+        + [pl.BlockSpec((n_p, 1, eb, rows, fe), lambda s: (0, 2, s, 0, 0))]
+        + [full((m, d))] * (2 * n),
+        out_specs=[full((m, d))] * n + [pl.BlockSpec((n_p, 3, eb, rows, fe), lambda s: (0, 0, s, 0, 0))],
         scratch_shapes=[
             pltpu.VMEM((d, count), bf16),
             pltpu.VMEM((d, count), bf16),
             pltpu.VMEM((d, eb * fe), bf16),
             pltpu.VMEM((count, d), f32),
         ],
-        cost_estimate=pl.CostEstimate(
-            flops=8 * count * d * E * fe, bytes_accessed=4 * d * E * fe * 2, transcendentals=0
-        ),
-    )(active, gate_g, up_g, *seconds, *cots, *ws)
-    out_parts, (keep, send) = got[:n], got[n:]
-
-    sums = [second_parts[0]] + [tensor_shift(second_parts[j], -j) for j in range(1, n)]
+        cost_estimate=pl.CostEstimate(flops=0, bytes_accessed=0, transcendentals=0),
+    )(active, gate_g, up_g, ws, *seconds, *cots)
+    out_parts, expert_parts = got[:n], got[n]
+
+    sums = collect(second_parts)
+    expert_parts = after(expert_parts, *sums)
+    expert_grads = lax.psum_scatter(expert_parts, ("dp", "seq"), scatter_dimension=0, tiled=False).astype(f32)
     got = whole_call(
         functools.partial(middle_back_kernel, n),
         (sds((m, d), f32), sds((m, d), bf16), sds((1, d), f32)) + tuple([sds((m, wide), bf16)] * n),
-        (middle, gain_two, cot, oa, ob, *sums),
+        (where, middle, gain_two, cot, oa, ob, *sums),
+        scratch=(pltpu.VMEM((d, n * wide), bf16),),
         flops=2 * m * d * d,
+        prefetch=1,
     )
     (middle_grad, branch, gain_two_part), pieces = got[:3], got[3:]
-    mixed_grads = [pieces[0]] + [tensor_shift(pieces[j], j) for j in range(1, n)]
-    branches = [branch] + [tensor_shift(branch, j) for j in range(1, n)]
+    mixed_grads = collect(pieces)
+    branches = [branch] + spread_by_two(after(branch, *mixed_grads))[1:]
 
     def attend_back(kv_one, pos_one, dtype, extra):
         one = kv_one.shape[0]
@@ -684,45 +668,40 @@
         dkv = lax.psum_scatter(dkv, "seq", scatter_dimension=0, tiled=True)
         got_kv = (jnp.zeros((count, 256), bf16),)
 
+    dq_ready = after(dq, *branches[1:3])
     got = whole_call(
         functools.partial(qkv_back_kernel, n, rows),
         tuple([sds((m, d), bf16)] * n) + (sds((count, cols), bf16), sds((1, d), f32)),
-        (dq, dkv, *got_kv, cos, sin, wa, wb, *xs),
+        (where, dq_ready, dkv, *got_kv, cos, sin, wa, wb, *xs),
+        scratch=(pltpu.VMEM((d, cols), bf16),),
         flops=2 * count * d * cols,
+        prefetch=1,
     )
     first_parts, (grads, gain_one_part) = got[:n], got[n:]
-    sums = [first_parts[0]] + [tensor_shift(first_parts[j], -j) for j in range(1, n)]
-    weight_shape = sds((half_p, rows, cols + wide), bf16)
+    sums = collect(first_parts)
+    weight_shape = sds((half_p, rows + LINES, cols + wide), bf16)
     weight_keep, weight_send = whole_call(
         functools.partial(weight_back_kernel, n, rows),
         (weight_shape, weight_shape),
-        (x1, grads, *branches, *mixed),
+        (where, x1, grads, router_part, gain_one_part, gain_two_part, *branches, *mixed),
+        scratch=(pltpu.VMEM((d, cols + wide), bf16), pltpu.VMEM((n_p, LINES, rows), bf16)),
         flops=2 * count * d * (cols + wide),
+        prefetch=1,
     )
 
     (input_grad,) = whole_call(
-        functools.partial(input_kernel, n), (sds((m, d), bf16),), (where, own, gain_one, middle_grad, *sums), prefetch=1
-    )
-    out_sums = [out_parts[0]] + [tensor_shift(out_parts[j], -j) for j in range(1, n)]
+        functools.partial(input_kernel, n), (sds((m, d), bf16),), (own, gain_one, middle_grad, *sums)
+    )
+    out_sums = [out_parts[0]] + collect([sums[0], *after_all(out_parts[1:], sums)])[1:]
     (output,) = whole_call(
-        functools.partial(output_kernel, n), (sds((m, d), bf16),), (where, middle, *out_sums), prefetch=1
+        functools.partial(output_kernel, n), (sds((m, d), bf16),), (middle, *out_sums)
     )
     weights = plane_scatter(weight_keep, weight_send, fancy)
-    expert_grads = plane_scatter_large(keep, send, fancy)
-
-    vectors = jnp.concatenate([router_part, gain_one_part, gain_two_part], axis=0)
-    lines = vectors.shape[0]
-    vectors = jnp.transpose(vectors.reshape(lines, n_p, rows), (1, 0, 2))
-    if fancy:
-        vectors = vectors[:4] + swap_core(vectors[4:])
-        vectors = vectors[:2] + swap_y(vectors[2:])
-        vectors = vectors[0] + swap_x(vectors[1])
-    else:
-        vectors = lax.psum_scatter(vectors, ("dp", "seq"), scatter_dimension=0, tiled=False)
-    total = vectors
-    for j in range(1, n):
-        total = total + tensor_shift(vectors, j)
+    total = weights[rows : rows + E + 2, :rows]
+    for bit in range(n.bit_length() - 1):
+        total = total + across(total, 1 << bit)
     total = lax.dynamic_slice_in_dim(total, me * shard, shard, axis=1)
+    weights = weights[:rows]
     kv_wide = key_projection.shape[1]
     return (
         output[None],

time: 426 us -> 339 us (0.80)
  waiting for transfers between devices: 200 us -> 132 us
  other arithmetic: 29.1 us -> 11.8 us
  between operations: 1.47 us -> 14.7 us
  local copies, waits for them, and re-layouts: 23.8 us -> 13.6 us
  starting transfers between devices: 78.8 us -> 73.2 us
    ppermute x10 -> x5, waiting for transfers between devices: 52.1 us -> 22.2 us  [swap_x(): return lax.ppermute(v, 'seq', [(0, 1), (1, 0)])]
    ppermute x36 -> x32, waiting for transfers between devices: 103 us -> 79.2 us  [across(): lax.ppermute(v, 'tensor', [(i, i ^ j) for i in range(lax.axis_size('tenso...]
    ppermute x8 -> x3, waiting for transfers between devices: 45.1 us -> 27.9 us  [swap_y(): return lax.ppermute(v, 'dp', [(i, i ^ 2) for i in range(4)])]
    add x7 -> x4, other arithmetic: 16.7 us -> 1.31 us  [the longest x1 1.19 us: plane_scatter(): mine = keep[:2].astype(f32) + got[:2].astype(f32) + far.astype(f32)]
    ppermute x36 -> x32, starting transfers between devices: 48.2 us -> 60.3 us  [across(): lax.ppermute(v, 'tensor', [(i, i ^ j) for i in range(lax.axis_size('tenso...]
    ppermute x10 -> x5, starting transfers between devices: 15.5 us -> 6.03 us  [swap_x(): return lax.ppermute(v, 'seq', [(0, 1), (1, 0)])]
    ppermute x8 -> x3, starting transfers between devices: 11.3 us -> 5.18 us  [swap_y(): return lax.ppermute(v, 'dp', [(i, i ^ 2) for i in range(4)])]
    squeeze x3 -> x0, local copies, waits for them, and re-layouts: 4.42 us -> none  [the longest x1 3.61 us: plane_scatter_large(): near[1][..., :half, :]]
  transfers between devices with their start and end apart: 67 -> 46, of which waited for: 23 -> 23; matrix products, arithmetic and copies ran while one was open for 10% -> 4% of each run, Pallas kernels for 12% -> 20%
where the time goes in v2:
time: 339 us; the launch traced here: 338 us
  waiting for transfers between devices  132 us (39%)
  Pallas kernels  92.4 us (27%)
  starting transfers between devices  73.2 us (22%)
  between operations  14.7 us (4%)
  local copies, waits for them, and re-layouts  13.6 us (4%)
  other arithmetic  11.8 us (3%)
    ppermute x32, waiting for transfers between devices, across(): lax.ppermute(v, 'tensor', [(i, i ^ j) for i in range(lax.axis_size('tenso...  79.2 us
    ppermute x32, starting transfers between devices, across(): lax.ppermute(v, 'tensor', [(i, i ^ j) for i in range(lax.axis_size('tenso...  60.3 us
    pallas_call x10, Pallas kernels, whole_call(): pl.pallas_call(body, out_shape=outs, grid_spec=pltpu.PrefetchScalarGridSp...  51.5 us
    ppermute x3, waiting for transfers between devices, swap_y(): return lax.ppermute(v, 'dp', [(i, i ^ 2) for i in range(4)])  27.9 us
    pallas_call x1, Pallas kernels, per_device(): pl.pallas_call(functools.partial(expert_kernel, n), out_shape=tuple([sds(...  24.3 us
    ppermute x5, waiting for transfers between devices, swap_x(): return lax.ppermute(v, 'seq', [(0, 1), (1, 0)])  22.2 us
    pallas_call x1, Pallas kernels, per_device(): pl.pallas_call(functools.partial(expert_back_kernel, n), out_shape=tuple(...  16.7 us
  transfers between devices with their start and end apart: 46, of which 23 were waited for; matrix products, arithmetic and copies ran while one was open for 4% of the time, Pallas kernels for 20%

profile of v2, /device:TPU:0, one launch (start us, length us, event | category | flops | bytes accessed | tf_op | source)
XLA Modules:
  0.0 338.2 jit_solution(1925119687536408515)
XLA Ops:
  23.4 12.2 %collective-permute-done.1 = bf16[2,144,512]{2,1,0:T(8,128)(2,1)S(1)} collective-permute-done((bf16[2,144,512]{2,1,0:T(8,128)(2,1)S(1)}, bf16[2,144,512]{2,1,0:T(8,128)(2,1)S(1)}, u32[]{:S(2)}, u32[]{:S(2)}) %collective-permute-start.1) | collective-permute-done | bytes 294944 | tf_op jit(solution)/shard_map/ppermute | solution.py:419
  39.1 6.3 %collective-permute-start.3 = (bf16[8,576]{1,0:T(8,128)(2,1)S(1)}, bf16[8,576]{1,0:T(8,128)(2,1)S(1)}, u32[]{:S(2)}, u32[]{:S(2)}) collective-permute-start(bf16[8,576]{1,0:T(8,128)(2,1)S(1)} %get-tuple-element.126), channel_id=1, source_target_pairs={{0,1},{1,0},{2,3},{3,2},{4,5},{5,4},{6,7},{7,6},{8,9},{9,8},{10,11... | collective-permute-start | bytes 27656 | tf_op jit(solution)/shard_map/ppermute | solution.py:388
  53.1 4.7 %shard_map.247 = (bf16[512,1024]{1,0:T(8,128)(2,1)}, bf16[512,256]{1,0:T(8,128)(2,1)}, bf16[512,256]{1,0:T(8,128)(2,1)}) custom-call(s32[8]{0:T(128)} %copy-done.41, bf16[128,1280]{1,0:T(8,128)(2,1)} %copy-done.4, bf16[128,1280]{1,0:T(8,128)(2,1)} %copy-done.8, bf16[128,1280]{1,0:T(8,128)(2,1)} %copy-done.9, bf16[128,1280]{1,0:T(8,128)(2,1)} %copy-done.10, ...), custom_call_target="tpu_custom_call" | custom-call | tf_op jit(solution)/shard_map/pallas_call | solution.py:38
  61.4 15.7 %collective-permute-done.10 = bf16[128,1024]{1,0:T(8,128)(2,1)S(1)} collective-permute-done((bf16[128,1024]{1,0:T(8,128)(2,1)S(1)}, bf16[128,1024]{1,0:T(8,128)(2,1)S(1)}, u32[]{:S(2)}, u32[]{:S(2)}) %collective-permute-start.10) | collective-permute-done | bytes 262176 | tf_op jit(solution)/shard_map/ppermute | solution.py:419
  77.1 7.2 %collective-permute-done.9 = bf16[128,1024]{1,0:T(8,128)(2,1)S(1)} collective-permute-done((bf16[128,1024]{1,0:T(8,128)(2,1)S(1)}, bf16[128,1024]{1,0:T(8,128)(2,1)S(1)}, u32[]{:S(2)}, u32[]{:S(2)}) %collective-permute-start.9) | collective-permute-done | bytes 262176 | tf_op jit(solution)/shard_map/ppermute | solution.py:411
  88.5 11.7 %collective-permute-done.13.refs_1_.kv = bf16[512,256]{1,0:T(8,128)(2,1)S(1)} collective-permute-done((bf16[512,256]{1,0:T(8,128)(2,1)S(1)}, bf16[512,256]{1,0:T(8,128)(2,1)S(1)}, u32[]{:S(2)}, u32[]{:S(2)}) %collective-permute-start.13) | collective-permute-done | bytes 262176 | tf_op jit(solution)/shard_map/ppermute | solution.py:411
  100.9 8.8 %shard_map.248 = (bf16[128,256]{1,0:T(8,128)(2,1)}, bf16[128,256]{1,0:T(8,128)(2,1)}, bf16[128,256]{1,0:T(8,128)(2,1)}, bf16[128,256]{1,0:T(8,128)(2,1)}, f32[4,64,512]{2,1,0:T(8,128)}, /*index=5*/f32[4,1,512]{2,1,0:T(1,128)}) custom-call(bf16[512,256]{1,0:T(8,128)(2,1)} %get-tuple-element.65.q, s32[1,512]{1,0:T(1,128)} %max.10.lim, ...), custom_call_target="tpu_custom_call" | custom-call | tf_op jit(solution)/shard_map/pallas_call | solution.py:38
  114.9 12.3 %collective-permute-done.15.refs_2_ = bf16[128,256]{1,0:T(8,128)(2,1)S(1)} collective-permute-done((bf16[128,256]{1,0:T(8,128)(2,1)}, bf16[128,256]{1,0:T(8,128)(2,1)S(1)}, u32[]{:S(2)}, u32[]{:S(2)}) %collective-permute-start.15) | collective-permute-done | bytes 65568 | tf_op jit(solution)/shard_map/ppermute | solution.py:388
  129.9 4.2 %shard_map.249 = (f32[128,1024]{1,0:T(8,128)}, bf16[128,1024]{1,0:T(8,128)(2,1)}) custom-call(s32[8]{0:T(128)} %copy-done.41, bf16[128,1024]{1,0:T(8,128)(2,1)} %bitcast.70, f32[1,1024]{1,0:T(1,128)} %reshape.224.gain, bf16[4,128,1024]{2,1,0:T(8,128)(2,1)} %copy-done, bf16[4,128,1024]{2,1,0:T(8,128)(2,1)} %copy-done.2, ...), custom_call_target="tpu_custom_call" | custom-call | tf_op jit(solution)/shard_map/pallas_call | solution.py:38
  141.7 17.9 %collective-permute-done.18.refs_2_ = bf16[128,1024]{1,0:T(8,128)(2,1)S(1)} collective-permute-done((bf16[128,1024]{1,0:T(8,128)(2,1)}, bf16[128,1024]{1,0:T(8,128)(2,1)S(1)}, u32[]{:S(2)}, u32[]{:S(2)}) %collective-permute-start.18) | collective-permute-done | bytes 262176 | tf_op jit(solution)/shard_map/ppermute | solution.py:388
  160.3 24.3 %shard_map.250 = (bf16[128,1024]{1,0:T(8,128)(2,1)}, bf16[128,1024]{1,0:T(8,128)(2,1)}, bf16[128,1024]{1,0:T(8,128)(2,1)}, bf16[128,1024]{1,0:T(8,128)(2,1)}, bf...) custom-call(f32[512,16]{1,0:T(8,128)} %get-tuple-element.122.chosen, ...), custom_call_target="tpu_custom_call" | custom-call | tf_op jit(solution)/shard_map/pallas_call | solution.py:584
  184.6 5.1 %collective-permute-start.23 = (bf16[128,1024]{1,0:T(8,128)(2,1)}, bf16[128,1024]{1,0:T(8,128)(2,1)S(1)}, u32[]{:S(2)}, u32[]{:S(2)}) collective-permute-start(bf16[128,1024]{1,0:T(8,128)(2,1)} %get-tuple-element.83), channel_id=1, source_target_pairs={{0,1},{1,0},{2,3},{3,2},{4,5},{5,4},{6,7},{7,6},{8,9},{9,8},{10,11... | collective-permute-start | bytes 786440 | tf_op jit(solution)/shard_map/ppermute | solution.py:388
  192.1 16.7 %shard_map.251 = (bf16[128,1024]{1,0:T(8,128)(2,1)}, bf16[128,1024]{1,0:T(8,128)(2,1)}, bf16[128,1024]{1,0:T(8,128)(2,1)}, bf16[128,1024]{1,0:T(8,128)(2,1)}, bf16[8,3,16,128,128]{4,3,2,1,0:T(8,128)(2,1)}) custom-call(bf16[512,2048]{1,0:T(8,128)(2,1)} %get-tuple-element.73.active, bf16[512,2048]{1,0:T(8,128)(2,1)} %get-tuple-element.74.gate, ...), custom_call_target="tpu_custom_call" | custom-call | tf_op jit(solution)/shard_map/pallas_call | solution.py:604
  212.0 4.3 %shard_map.252 = (f32[128,1024]{1,0:T(8,128)}, bf16[128,1024]{1,0:T(8,128)(2,1)}, f32[1,1024]{1,0:T(1,128)}, bf16[128,256]{1,0:T(8,128)(2,1)}, bf16[128,256]{1,0...) custom-call(s32[8]{0:T(128)} %copy-done.41, f32[128,1024]{1,0:T(8,128)} %get-tuple-element.70.middle, ...), custom_call_target="tpu_custom_call" | custom-call | tf_op jit(solution)/shard_map/pallas_call | solution.py:38
  216.3 3.9 %collective-permute-start.26 = (bf16[128,256]{1,0:T(8,128)(2,1)}, bf16[128,256]{1,0:T(8,128)(2,1)S(1)}, u32[]{:S(2)}, u32[]{:S(2)}) collective-permute-start(bf16[128,256]{1,0:T(8,128)(2,1)} %get-tuple-element.87), channel_id=1, source_target_pairs={{0,1},{1,0},{2,3},{3,2},{4,5},{5,4},{6,7},{7,6},{8,9},{9,8},{10,11... | collective-permute-start | bytes 196616 | tf_op jit(solution)/shard_map/ppermute | solution.py:388
  229.6 7.1 %shard_map.253 = (bf16[512,256]{1,0:T(8,128)(2,1)}, f32[4,64,512]{2,1,0:T(8,128)}) custom-call(bf16[512,256]{1,0:T(8,128)(2,1)} %get-tuple-element.65.q, s32[1,512]{1,0:T(1,128)} %max.10.lim, bf16[512,256]{1,0:T(8,128)(2,1)} %copy-done.17, s32[512,1]{1,0:T(8,128)} %broadcast_add_fusion.refs_3_.kpos, f32[4,1,512]{2,1,0:T(1,128)} %get-tuple-element.80.lse, ...), custom_call_target="tpu_custom_call" | custom-call | tf_op jit(solution)/shard_map/pallas_call | solution.py:38
  239.8 7.7 %shard_map.254 = (f32[512,256]{1,0:T(8,128)}, bf16[512,256]{1,0:T(8,128)(2,1)}) custom-call(bf16[512,256]{1,0:T(8,128)(2,1)} %get-tuple-element.65.q, s32[1,512]{1,0:T(1,128)} %max.10.lim, bf16[512,256]{1,0:T(8,128)(2,1)} %get-tuple-element.63.refs_0_.kv, s32[512,1]{1,0:T(8,128)} %copy-done.3, f32[4,1,512]{2,1,0:T(1,128)} %get-tuple-element.80.lse, ...), custom_call_target="tpu_custom_call" | custom-call | tf_op jit(solution)/shard_map/pallas_call | solution.py:38
  248.3 4.9 %shard_map.255 = (bf16[128,1024]{1,0:T(8,128)(2,1)}, bf16[128,1024]{1,0:T(8,128)(2,1)}, bf16[128,1024]{1,0:T(8,128)(2,1)}, bf16[128,1024]{1,0:T(8,128)(2,1)}, bf...) custom-call(s32[8]{0:T(128)} %copy-done.41, bf16[512,256]{1,0:T(8,128)(2,1)} %get-tuple-element.94.dq, ...), custom_call_target="tpu_custom_call" | custom-call | tf_op jit(solution)/shard_map/pallas_call | solution.py:38
  254.0 5.1 %shard_map.258 = (bf16[4,160,768]{2,1,0:T(8,128)(2,1)}, bf16[4,160,768]{2,1,0:T(8,128)(2,1)}) custom-call(s32[8]{0:T(128)} %copy-done.41, bf16[512,1024]{1,0:T(8,128)(2,1)} %get-tuple-element.105.x1, bf16[512,512]{1,0:T(8,128)(2,1)} %get-tuple-element.106.grads, f32[16,1024]{1,0:T(8,128)} %get-tuple-element.107.router_part, ...), custom_call_target="tpu_custom_call" | custom-call | tf_op jit(solution)/shard_map/pallas_call | solution.py:38
  269.0 8.1 %collective-permute-done.32.refs_1_ = bf16[128,1024]{1,0:T(8,128)(2,1)S(1)} collective-permute-done((bf16[128,1024]{1,0:T(8,128)(2,1)S(1)}, bf16[128,1024]{1,0:T(8,128)(2,1)S(1)}, u32[]{:S(2)}, u32[]{:S(2)}) %collective-permute-start.32) | collective-permute-done | bytes 262176 | tf_op jit(solution)/shard_map/ppermute | solution.py:388
  277.1 10.1 %collective-permute-done.33.refs_2_ = bf16[128,1024]{1,0:T(8,128)(2,1)S(1)} collective-permute-done((bf16[128,1024]{1,0:T(8,128)(2,1)S(1)}, bf16[128,1024]{1,0:T(8,128)(2,1)S(1)}, u32[]{:S(2)}, u32[]{:S(2)}) %collective-permute-start.33) | collective-permute-done | bytes 262176 | tf_op jit(solution)/shard_map/ppermute | solution.py:388
  287.2 4.9 %collective-permute-start.35 = (bf16[128,1024]{1,0:T(8,128)(2,1)}, bf16[128,1024]{1,0:T(8,128)(2,1)S(1)}, u32[]{:S(2)}, u32[]{:S(2)}) collective-permute-start(bf16[128,1024]{1,0:T(8,128)(2,1)} %get-tuple-element.101), channel_id=1, source_target_pairs={{0,1},{1,0},{2,3},{3,2},{4,5},{5,4},{6,7},{7,6},{8,9},{9,8},{10,11... | collective-permute-start | bytes 786440 | tf_op jit(solution)/shard_map/ppermute | solution.py:388
  301.4 12.1 %collective-permute-done.36.refs_2_ = bf16[128,1024]{1,0:T(8,128)(2,1)S(1)} collective-permute-done((bf16[128,1024]{1,0:T(8,128)(2,1)}, bf16[128,1024]{1,0:T(8,128)(2,1)S(1)}, u32[]{:S(2)}, u32[]{:S(2)}) %collective-permute-start.36) | collective-permute-done | bytes 262176 | tf_op jit(solution)/shard_map/ppermute | solution.py:388
  316.5 3.8 %collective-permute-start.42 = (f32[18,128]{1,0:T(8,128)S(1)}, f32[18,128]{1,0:T(8,128)S(1)}, u32[]{:S(2)}, u32[]{:S(2)}) collective-permute-start(f32[18,128]{1,0:T(8,128)S(1)} %slice.144), channel_id=1, source_target_pairs={{0,1},{1,0},{2,3},{3,2},{4,5},{5,4},{6,7},{7,6},{8,9},{9,8},{10,11... | collective-permute-start | bytes 27656 | tf_op jit(solution)/shard_map/ppermute | solution.py:388
  (248 shorter events, 104.6 us)
Async XLA Ops:
  7.2 152.4 %all-gather.3.cloned.1.call-start = ((), (), s32[]{:S(2)}) async-start(), calls=%async_computation.2 | async-start | bytes 14155776 | tf_op jit(solution)/shard_map/all_gather | solution.py:579
  10.1 317.7 %reduce-scatter.2.cloned.1.call-start = ((), (), s32[]{:S(2)}) async-start(), calls=%async_computation.1 | async-start | bytes 14155776 | tf_op jit(solution)/shard_map/reduce_scatter | solution.py:624
  10.2 27.8 %collective-permute-start.6 = (bf16[128,1280]{1,0:T(8,128)(2,1)S(1)}, bf16[128,1280]{1,0:T(8,128)(2,1)S(1)}, u32[]{:S(2)}, u32[]{:S(2)}) collective-permute-start(bf16[128,1280]{1,0:T(8,128)(2,1)S(1)} %pad_maximum_fusion.3.refs_0_), channel_id=1, source_target_pairs={{0,1},{1,0},{2,3},{3,2},{4,5},{5,4},{6,7},{7,6},{8,9},{9,8},{10,11... | collective-permute-start | bytes 983048 | tf_op jit(solution)/shard_map/ppermute | solution.py:388
  13.4 25.5 %collective-permute-start.7 = (bf16[128,1280]{1,0:T(8,128)(2,1)S(1)}, bf16[128,1280]{1,0:T(8,128)(2,1)S(1)}, u32[]{:S(2)}, u32[]{:S(2)}) collective-permute-start(bf16[128,1280]{1,0:T(8,128)(2,1)S(1)} %pad_maximum_fusion.3.refs_0_), channel_id=1, source_target_pairs={{0,2},{1,3},{2,0},{3,1},{4,6},{5,7},{6,4},{7,5},{8,10},{9,11},{10,... | collective-permute-start | bytes 983048 | tf_op jit(solution)/shard_map/ppermute | solution.py:388
  15.9 23.0 %collective-permute-start.8 = (bf16[128,1280]{1,0:T(8,128)(2,1)S(1)}, bf16[128,1280]{1,0:T(8,128)(2,1)S(1)}, u32[]{:S(2)}, u32[]{:S(2)}) collective-permute-start(bf16[128,1280]{1,0:T(8,128)(2,1)S(1)} %pad_maximum_fusion.3.refs_0_), channel_id=1, source_target_pairs={{0,3},{1,2},{2,1},{3,0},{4,7},{5,6},{6,5},{7,4},{8,11},{9,10},{10,... | collective-permute-start | bytes 983048 | tf_op jit(solution)/shard_map/ppermute | solution.py:388
  57.8 19.2 %collective-permute-start.10 = (bf16[128,1024]{1,0:T(8,128)(2,1)S(1)}, bf16[128,1024]{1,0:T(8,128)(2,1)S(1)}, u32[]{:S(2)}, u32[]{:S(2)}) collective-permute-start(bf16[128,1024]{1,0:T(8,128)(2,1)S(1)} %pad_maximum_fusion.5), channel_id=1, source_target_pairs={{0,16},{8,24},{16,0},{24,8},{1,17},{9,25},{17,1},{25,9},{2,18},{10... | collective-permute-start | bytes 786440 | tf_op jit(solution)/shard_map/ppermute | solution.py:419
  59.6 17.4 %collective-permute-start.11 = (bf16[128,1024]{1,0:T(8,128)(2,1)S(1)}, bf16[128,1024]{1,0:T(8,128)(2,1)S(1)}, u32[]{:S(2)}, u32[]{:S(2)}) collective-permute-start(bf16[128,1024]{1,0:T(8,128)(2,1)S(1)} %pad_maximum_fusion.5), channel_id=1, source_target_pairs={{0,20},{4,16},{8,28},{12,24},{16,4},{20,0},{24,12},{28,8},{1,21},{... | collective-permute-start | bytes 786440 | tf_op jit(solution)/shard_map/ppermute | solution.py:423
  61.1 23.2 %collective-permute-start.9 = (bf16[128,1024]{1,0:T(8,128)(2,1)S(1)}, bf16[128,1024]{1,0:T(8,128)(2,1)S(1)}, u32[]{:S(2)}, u32[]{:S(2)}) collective-permute-start(bf16[128,1024]{1,0:T(8,128)(2,1)S(1)} %pad_maximum_fusion.5), channel_id=1, source_target_pairs={{0,4},{4,0},{1,5},{5,1},{2,6},{6,2},{3,7},{7,3},{8,12},{12,8},{9,1... | collective-permute-start | bytes 786440 | tf_op jit(solution)/shard_map/ppermute | solution.py:411
  84.4 44.5 %collective-permute-start.12 = (bf16[4,128,1024]{2,1,0:T(8,128)(2,1)S(1)}, bf16[4,128,1024]{2,1,0:T(8,128)(2,1)S(1)}, u32[]{:S(2)}, u32[]{:S(2)}) collective-permute-start(bf16[4,128,1024]{2,1,0:T(8,128)(2,1)S(1)} %pad_maximum_fusion.1.wa), channel_id=1, source_target_pairs={{0,8},{8,0},{16,24},{24,16},{1,9},{9,1},{17,25},{25,17},{2,10},{10... | collective-permute-start | bytes 3145736 | tf_op jit(solution)/shard_map/ppermute | solution.py:415
  87.8 49.0 %collective-permute-start.20 = (bf16[128,1024]{1,0:T(8,128)(2,1)S(1)}, bf16[128,1024]{1,0:T(8,128)(2,1)S(1)}, u32[]{:S(2)}, u32[]{:S(2)}) collective-permute-start(bf16[128,1024]{1,0:T(8,128)(2,1)S(1)} %bitcast.66), channel_id=1, source_target_pairs={{0,1},{1,0},{2,3},{3,2},{4,5},{5,4},{6,7},{7,6},{8,9},{9,8},{10,11... | collective-permute-start | bytes 786440 | tf_op jit(solution)/shard_map/ppermute | solution.py:388
  110.3 16.9 %collective-permute-start.15 = (bf16[128,256]{1,0:T(8,128)(2,1)}, bf16[128,256]{1,0:T(8,128)(2,1)S(1)}, u32[]{:S(2)}, u32[]{:S(2)}) collective-permute-start(bf16[128,256]{1,0:T(8,128)(2,1)} %get-tuple-element.68.refs_6_), channel_id=1, source_target_pairs={{0,2},{1,3},{2,0},{3,1},{4,6},{5,7},{6,4},{7,5},{8,10},{9,11},{10,... | collective-permute-start | bytes 196616 | tf_op jit(solution)/shard_map/ppermute | solution.py:388
  114.9 25.6 %collective-permute-start.21 = (bf16[128,1024]{1,0:T(8,128)(2,1)S(1)}, bf16[128,1024]{1,0:T(8,128)(2,1)S(1)}, u32[]{:S(2)}, u32[]{:S(2)}) collective-permute-start(bf16[128,1024]{1,0:T(8,128)(2,1)S(1)} %bitcast.67), channel_id=1, source_target_pairs={{0,2},{1,3},{2,0},{3,1},{4,6},{5,7},{6,4},{7,5},{8,10},{9,11},{10,... | collective-permute-start | bytes 786440 | tf_op jit(solution)/shard_map/ppermute | solution.py:388
  134.3 25.2 %collective-permute-start.18 = (bf16[128,1024]{1,0:T(8,128)(2,1)}, bf16[128,1024]{1,0:T(8,128)(2,1)S(1)}, u32[]{:S(2)}, u32[]{:S(2)}) collective-permute-start(bf16[128,1024]{1,0:T(8,128)(2,1)} %get-tuple-element.71.refs_0_), channel_id=1, source_target_pairs={{0,2},{1,3},{2,0},{3,1},{4,6},{5,7},{6,4},{7,5},{8,10},{9,11},{10,... | collective-permute-start | bytes 786440 | tf_op jit(solution)/shard_map/ppermute | solution.py:388
  136.8 22.8 %collective-permute-start.19 = (bf16[128,1024]{1,0:T(8,128)(2,1)}, bf16[128,1024]{1,0:T(8,128)(2,1)S(1)}, u32[]{:S(2)}, u32[]{:S(2)}) collective-permute-start(bf16[128,1024]{1,0:T(8,128)(2,1)} %get-tuple-element.71.refs_0_), channel_id=1, source_target_pairs={{0,3},{1,2},{2,1},{3,0},{4,7},{5,6},{6,5},{7,4},{8,11},{9,10},{10,... | collective-permute-start | bytes 786440 | tf_op jit(solution)/shard_map/ppermute | solution.py:388
  184.6 24.2 %collective-permute-start.23 = (bf16[128,1024]{1,0:T(8,128)(2,1)}, bf16[128,1024]{1,0:T(8,128)(2,1)S(1)}, u32[]{:S(2)}, u32[]{:S(2)}) collective-permute-start(bf16[128,1024]{1,0:T(8,128)(2,1)} %get-tuple-element.83), channel_id=1, source_target_pairs={{0,1},{1,0},{2,3},{3,2},{4,5},{5,4},{6,7},{7,6},{8,9},{9,8},{10,11... | collective-permute-start | bytes 786440 | tf_op jit(solution)/shard_map/ppermute | solution.py:388
  189.7 21.5 %collective-permute-start.24 = (bf16[128,1024]{1,0:T(8,128)(2,1)}, bf16[128,1024]{1,0:T(8,128)(2,1)S(1)}, u32[]{:S(2)}, u32[]{:S(2)}) collective-permute-start(bf16[128,1024]{1,0:T(8,128)(2,1)} %get-tuple-element.84), channel_id=1, source_target_pairs={{0,2},{1,3},{2,0},{3,1},{4,6},{5,7},{6,4},{7,5},{8,10},{9,11},{10,... | collective-permute-start | bytes 786440 | tf_op jit(solution)/shard_map/ppermute | solution.py:388
  190.3 21.0 %collective-permute-start.25 = (bf16[128,1024]{1,0:T(8,128)(2,1)}, bf16[128,1024]{1,0:T(8,128)(2,1)S(1)}, u32[]{:S(2)}, u32[]{:S(2)}) collective-permute-start(bf16[128,1024]{1,0:T(8,128)(2,1)} %get-tuple-element.85), channel_id=1, source_target_pairs={{0,3},{1,2},{2,1},{3,0},{4,7},{5,6},{6,5},{7,4},{8,11},{9,10},{10,... | collective-permute-start | bytes 786440 | tf_op jit(solution)/shard_map/ppermute | solution.py:388
  228.3 19.3 %collective-permute-start.30 = (bf16[128,1024]{1,0:T(8,128)(2,1)}, bf16[128,1024]{1,0:T(8,128)(2,1)S(1)}, u32[]{:S(2)}, u32[]{:S(2)}) collective-permute-start(bf16[128,1024]{1,0:T(8,128)(2,1)} %get-tuple-element.93.refs_0_), channel_id=1, source_target_pairs={{0,2},{1,3},{2,0},{3,1},{4,6},{5,7},{6,4},{7,5},{8,10},{9,11},{10,... | collective-permute-start | bytes 786440 | tf_op jit(solution)/shard_map/ppermute | solution.py:388
  263.0 31.4 %collective-permute-start.40 = (bf16[2,160,768]{2,1,0:T(8,128)(2,1)S(1)}, bf16[2,160,768]{2,1,0:T(8,128)(2,1)S(1)}, u32[]{:S(2)}, u32[]{:S(2)}) collective-permute-start(bf16[2,160,768]{2,1,0:T(8,128)(2,1)S(1)} %add_convert_fusion), channel_id=1, source_target_pairs={{0,16},{8,24},{16,0},{24,8},{1,17},{9,25},{17,1},{25,9},{2,18},{10... | collective-permute-start | bytes 1474568 | tf_op jit(solution)/shard_map/ppermute | solution.py:419
  265.9 21.3 %collective-permute-start.33 = (bf16[128,1024]{1,0:T(8,128)(2,1)S(1)}, bf16[128,1024]{1,0:T(8,128)(2,1)S(1)}, u32[]{:S(2)}, u32[]{:S(2)}) collective-permute-start(bf16[128,1024]{1,0:T(8,128)(2,1)S(1)} %copy-done.49), channel_id=1, source_target_pairs={{0,2},{1,3},{2,0},{3,1},{4,6},{5,7},{6,4},{7,5},{8,10},{9,11},{10,... | collective-permute-start | bytes 786440 | tf_op jit(solution)/shard_map/ppermute | solution.py:388
  266.7 20.5 %collective-permute-start.34 = (bf16[128,1024]{1,0:T(8,128)(2,1)S(1)}, bf16[128,1024]{1,0:T(8,128)(2,1)S(1)}, u32[]{:S(2)}, u32[]{:S(2)}) collective-permute-start(bf16[128,1024]{1,0:T(8,128)(2,1)S(1)} %copy-done.48), channel_id=1, source_target_pairs={{0,3},{1,2},{2,1},{3,0},{4,7},{5,6},{6,5},{7,4},{8,11},{9,10},{10,... | collective-permute-start | bytes 786440 | tf_op jit(solution)/shard_map/ppermute | solution.py:388
  292.0 21.5 %collective-permute-start.36 = (bf16[128,1024]{1,0:T(8,128)(2,1)}, bf16[128,1024]{1,0:T(8,128)(2,1)S(1)}, u32[]{:S(2)}, u32[]{:S(2)}) collective-permute-start(bf16[128,1024]{1,0:T(8,128)(2,1)} %get-tuple-element.102), channel_id=1, source_target_pairs={{0,2},{1,3},{2,0},{3,1},{4,6},{5,7},{6,4},{7,5},{8,10},{9,11},{10,... | collective-permute-start | bytes 786440 | tf_op jit(solution)/shard_map/ppermute | solution.py:388
  292.1 21.5 %collective-permute-start.37 = (bf16[128,1024]{1,0:T(8,128)(2,1)S(1)}, bf16[128,1024]{1,0:T(8,128)(2,1)S(1)}, u32[]{:S(2)}, u32[]{:S(2)}) collective-permute-start(bf16[128,1024]{1,0:T(8,128)(2,1)S(1)} %copy-done.47), channel_id=1, source_target_pairs={{0,3},{1,2},{2,1},{3,0},{4,7},{5,6},{6,5},{7,4},{8,11},{9,10},{10,... | collective-permute-start | bytes 786440 | tf_op jit(solution)/shard_map/ppermute | solution.py:388
  295.6 20.8 %collective-permute-start.41 = (bf16[160,768]{1,0:T(8,128)(2,1)S(1)}, bf16[160,768]{1,0:T(8,128)(2,1)S(1)}, u32[]{:S(2)}, u32[]{:S(2)}) collective-permute-start(bf16[160,768]{1,0:T(8,128)(2,1)S(1)} %fusion.5), channel_id=1, source_target_pairs={{0,4},{4,0},{1,5},{5,1},{2,6},{6,2},{3,7},{7,3},{8,12},{12,8},{9,1... | collective-permute-start | bytes 737288 | tf_op jit(solution)/shard_map/ppermute | solution.py:411
  (75 other events, 836.4 us)
Sparse Core Ops, SparseCore 0:
  10.2 96.5 all-gather.2
  211.4 109.0 reduce-scatter.1

commit v3 on v2

--- a/solution.py
+++ b/solution.py
@@ -33,7 +33,7 @@
     return pl.BlockSpec(shape, lambda *_: (0,) * rank)
 
 
-def whole_call(body, outs, args, scratch=(), flops=0, prefetch=0):
+def whole_call(body, outs, args, scratch=(), flops=0, prefetch=0, cost=0):
     moved = sum(math.prod(a.shape) * a.dtype.itemsize for a in (*args, *outs))
     return pl.pallas_call(
         body,
@@ -45,7 +45,7 @@
             out_specs=[full(o.shape) for o in outs],
             scratch_shapes=list(scratch),
         ),
-        cost_estimate=pl.CostEstimate(flops=0, bytes_accessed=0, transcendentals=0),
+        cost_estimate=pl.CostEstimate(flops=int(cost), bytes_accessed=0, transcendentals=0),
     )(*args)
 
 
@@ -427,9 +427,9 @@
     return lax.optimization_barrier((*values, *others))[: len(values)]
 
 
-def plane_gather(v, fancy, near=False):
+def plane_gather(v, fancy, near=False, first=()):
     if fancy and near:
-        near = jnp.stack([v, swap_x(v), swap_y(v), swap_xy(v)])
+        near = after(jnp.stack([v, swap_x(v), swap_y(v), swap_xy(v)]), *first)
         return near, swap_core(near)
     if fancy:
         near = jnp.stack([v, swap_x(v)])
@@ -483,23 +483,23 @@
     where = (place ^ jnp.array(order, jnp.int32)) if fancy else jnp.arange(n_p, dtype=jnp.int32)
 
     own, cot = hidden_in[0], cotangent[0]
-    joined = m == w_out.shape[0]
-    xs = spread(jnp.concatenate([own, w_out], axis=1) if joined else own)
 
     shard = first_gain.shape[0]
     small = jnp.concatenate([router.reshape(-1), first_gain, second_gain])
     size = small.shape[0]
+    smalls = spread(small.reshape(1, size))
+    which = me ^ jnp.arange(n)
+    pick_rows = (which[:, None] == jnp.arange(n)[None, :]).astype(f32)
+    stacked = jnp.concatenate(smalls, axis=0).astype(f32)
+    natural = jnp.sum(pick_rows[:, :, None] * stacked[None], axis=1).astype(bf16)
     qkv_w = jnp.concatenate([w_query, key_projection, value_projection], axis=1)
     cols = qkv_w.shape[1]
-    small = jnp.pad(small, (0, 16 * cols - size)).reshape(16, cols)
-    wa, wb = plane_gather(jnp.concatenate([qkv_w, small], axis=0), fancy)
-    tail = jnp.concatenate([wa[:, rows:], wb[:, rows:]], axis=0).reshape(n_p, -1)[:, :size]
-    stacked = jnp.stack(spread(tail)).astype(f32)
-    which = me ^ jnp.arange(n)
-    pick_rows = (which[:, None] == jnp.arange(n)[None, :]).astype(f32)
+    natural = jnp.pad(natural.reshape(-1), (0, 16 * cols - n * size)).reshape(16, cols)
+    xs = spread(own)
+    wa, wb = plane_gather(jnp.concatenate([qkv_w, natural], axis=0), fancy, near=True)
+    tail = jnp.concatenate([wa[:, rows:], wb[:, rows:]], axis=0).reshape(n_p, -1)[:, : n * size]
     ordered = (where[None, :] == jnp.arange(n_p, dtype=jnp.int32)[:, None]).astype(f32)
-    stacked = jnp.sum(pick_rows[:, :, None, None] * stacked[None], axis=1)
-    tail = jnp.sum(ordered[:, None, :, None] * stacked[None], axis=2)
+    tail = jnp.sum(ordered[:, :, None] * tail.astype(f32)[None], axis=1).reshape(n_p, n, size)
     gain_one = tail[:, :, size - 2 * shard : size - shard].reshape(1, d)
     gain_two = tail[:, :, size - shard :].reshape(1, d)
     router_all = tail[:, :, : size - 2 * shard].reshape(d, E).astype(bf16)
@@ -557,13 +557,15 @@
             pltpu.VMEM((2, HEAD, span), bf16),
             pltpu.VMEM((span, 1), jnp.int32),
         ),
-        flops=4 * count * span * wide * 4,
+        cost=10 ** 10,
     )
     mixed, (mixed_t, lse) = got[:n], got[n:]
 
-    out_w = jnp.concatenate([v[:, d:] for v in xs] if joined else spread(w_out), axis=1)
-    oa, ob = plane_gather(after(out_w, kv), fancy, near=True)
-    mine = collect(mixed)
+    out_w = jnp.concatenate(spread(after(w_out, wa)), axis=1)
+    cots = [cot] + spread(after(cot, kv))[1:]
+    oa, ob = plane_gather(after(out_w, kvs[-1]), fancy, near=True, first=())
+    mine = collect([mixed[0], *after_all(mixed[1:], cots[1:])])
+    oa, ob = (oa, swap_core(after(oa, *mine))) if fancy else (oa, ob)
     middle, second = whole_call(
         functools.partial(middle_kernel, n),
         (sds((m, d), f32), sds((m, d), bf16)),
@@ -574,7 +576,7 @@
     )
 
     seconds = spread(second)
-    cots = [cot] + spread(after(cot, kv))[1:]
+
     packed = jnp.stack([w_gate, w_up, w_down])
     ws = lax.all_gather(packed, ("dp", "seq"), axis=0, tiled=False)
     eb, fe = EXPERTS_PER_STEP, w_gate.shape[2]
@@ -621,7 +623,7 @@
 
     sums = collect(second_parts)
     expert_parts = after(expert_parts, *sums)
-    expert_grads = lax.psum_scatter(expert_parts, ("dp", "seq"), scatter_dimension=0, tiled=False).astype(f32)
+    expert_grads = lax.psum_scatter(expert_parts, ("dp", "seq"), scatter_dimension=0, tiled=False)
     got = whole_call(
         functools.partial(middle_back_kernel, n),
         (sds((m, d), f32), sds((m, d), bf16), sds((1, d), f32)) + tuple([sds((m, wide), bf16)] * n),
@@ -655,7 +657,7 @@
                 pltpu.VMEM((2, one, HEAD), f32),
                 pltpu.VMEM((heads, HEAD, count), f32),
             ),
-            flops=10 * count * one * wide * 4,
+            cost=10 ** 10,
         )
 
     if fancy:
@@ -668,6 +670,7 @@
         dkv = lax.psum_scatter(dkv, "seq", scatter_dimension=0, tiled=True)
         got_kv = (jnp.zeros((count, 256), bf16),)
 
+    out_sums = [out_parts[0]] + collect([out_parts[0], *after_all(out_parts[1:], mixed_grads)])[1:]
     dq_ready = after(dq, *branches[1:3])
     got = whole_call(
         functools.partial(qkv_back_kernel, n, rows),
@@ -678,6 +681,7 @@
         prefetch=1,
     )
     first_parts, (grads, gain_one_part) = got[:n], got[n:]
+    grads = after(grads, *out_sums[:3])
     sums = collect(first_parts)
     weight_shape = sds((half_p, rows + LINES, cols + wide), bf16)
     weight_keep, weight_send = whole_call(
@@ -692,7 +696,6 @@
     (input_grad,) = whole_call(
         functools.partial(input_kernel, n), (sds((m, d), bf16),), (own, gain_one, middle_grad, *sums)
     )
-    out_sums = [out_parts[0]] + collect([sums[0], *after_all(out_parts[1:], sums)])[1:]
     (output,) = whole_call(
         functools.partial(output_kernel, n), (sds((m, d), bf16),), (middle, *out_sums)
     )
@@ -710,9 +713,9 @@
         weights[:, wide : wide + kv_wide],
         weights[:, wide + kv_wide : cols],
         weights[:, cols:],
-        expert_grads[0],
-        expert_grads[1],
-        expert_grads[2],
+        expert_grads[0].astype(f32),
+        expert_grads[1].astype(f32),
+        expert_grads[2].astype(f32),
         total[E],
         total[E + 1],
         total[:E].T,

time: 339 us -> 296 us (0.87)
  waiting for transfers between devices: 132 us -> 87.1 us
    ppermute x3, waiting for transfers between devices: 27.9 us -> 10.9 us  [swap_y(): return lax.ppermute(v, 'dp', [(i, i ^ 2) for i in range(4)])]
    ppermute x5, waiting for transfers between devices: 22.2 us -> 5.4 us  [swap_x(): return lax.ppermute(v, 'seq', [(0, 1), (1, 0)])]
    ppermute x32 -> x35, waiting for transfers between devices: 79.2 us -> 62.6 us  [across(): lax.ppermute(v, 'tensor', [(i, i ^ j) for i in range(lax.axis_size('tenso...]
    ppermute x1 -> x2, waiting for transfers between devices: 0.01 us -> 3.48 us  [swap_xy(): return lax.ppermute(v, ('dp', 'seq'), [(i, i ^ 5) for i in range(8)])]
    ppermute x32 -> x35, starting transfers between devices: 60.3 us -> 63.4 us  [across(): lax.ppermute(v, 'tensor', [(i, i ^ j) for i in range(lax.axis_size('tenso...]
    unnamed x108 -> x116, local copies, waits for them, and re-layouts: 5.67 us -> 7.15 us
  transfers between devices with their start and end apart: 46 -> 50, of which waited for: 23 -> 23; matrix products, arithmetic and copies ran while one was open for 4% -> 5% of each run, Pallas kernels for 20% -> 23%
where the time goes in v3:
time: 296 us; the launch traced here: 295 us
  Pallas kernels  92.1 us (31%)
  waiting for transfers between devices  87.1 us (29%)
  starting transfers between devices  74.8 us (25%)
  between operations  14.7 us (5%)
  local copies, waits for them, and re-layouts  14.1 us (5%)
  other arithmetic  11.9 us (4%)
    ppermute x35, starting transfers between devices, across(): lax.ppermute(v, 'tensor', [(i, i ^ j) for i in range(lax.axis_size('tenso...  63.4 us
    ppermute x35, waiting for transfers between devices, across(): lax.ppermute(v, 'tensor', [(i, i ^ j) for i in range(lax.axis_size('tenso...  62.6 us
    pallas_call x10, Pallas kernels, whole_call(): pl.pallas_call(body, out_shape=outs, grid_spec=pltpu.PrefetchScalarGridSp...  51.1 us
    pallas_call x1, Pallas kernels, per_device(): pl.pallas_call(functools.partial(expert_kernel, n), out_shape=tuple([sds(...  24.2 us
    pallas_call x1, Pallas kernels, per_device(): pl.pallas_call(functools.partial(expert_back_kernel, n), out_shape=tuple(...  16.8 us
    ppermute x3, waiting for transfers between devices, swap_y(): return lax.ppermute(v, 'dp', [(i, i ^ 2) for i in range(4)])  10.9 us
    unnamed x116, local copies, waits for them, and re-layouts  7.15 us
    ppermute x5, starting transfers between devices, swap_x(): return lax.ppermute(v, 'seq', [(0, 1), (1, 0)])  5.99 us
  transfers between devices with their start and end apart: 50, of which 23 were waited for; matrix products, arithmetic and copies ran while one was open for 5% of the time, Pallas kernels for 23%

profile of v3, /device:TPU:0, one launch (start us, length us, event | category | flops | bytes accessed | tf_op | source)
XLA Modules:
  0.0 295.2 jit_solution(90143810546326552)
XLA Ops:
  17.4 3.5 %collective-permute-start.11 = (bf16[128,1024]{1,0:T(8,128)(2,1)S(1)}, bf16[128,1024]{1,0:T(8,128)(2,1)S(1)}, u32[]{:S(2)}, u32[]{:S(2)}) collective-permute-start(bf16[128,1024]{1,0:T(8,128)(2,1)S(1)} %bitcast.74), channel_id=1, source_target_pairs={{0,2},{1,3},{2,0},{3,1},{4,6},{5,7},{6,4},{7,5},{8,10},{9,11},{10,... | collective-permute-start | bytes 786440 | tf_op jit(solution)/shard_map/ppermute | solution.py:388
  26.8 5.4 %collective-permute-done.3 = bf16[144,512]{1,0:T(8,128)(2,1)S(1)} collective-permute-done((bf16[144,512]{1,0:T(8,128)(2,1)S(1)}, bf16[144,512]{1,0:T(8,128)(2,1)S(1)}, u32[]{:S(2)}, u32[]{:S(2)}) %collective-permute-start.3) | collective-permute-done | bytes 147488 | tf_op jit(solution)/shard_map/ppermute | solution.py:411
  34.5 3.5 %collective-permute-done.5 = bf16[144,512]{1,0:T(8,128)(2,1)S(1)} collective-permute-done((bf16[144,512]{1,0:T(8,128)(2,1)S(1)}, bf16[144,512]{1,0:T(8,128)(2,1)S(1)}, u32[]{:S(2)}, u32[]{:S(2)}) %collective-permute-start.5) | collective-permute-done | bytes 147488 | tf_op jit(solution)/shard_map/ppermute | solution.py:423
  43.2 4.5 %shard_map.247 = (bf16[512,1024]{1,0:T(8,128)(2,1)}, bf16[512,256]{1,0:T(8,128)(2,1)}, bf16[512,256]{1,0:T(8,128)(2,1)}) custom-call(s32[8]{0:T(128)} %copy-done.40, bf16[128,1024]{1,0:T(8,128)(2,1)} %bitcast.69, bf16[128,1024]{1,0:T(8,128)(2,1)} %copy-done.12, bf16[128,1024]{1,0:T(8,128)(2,1)} %copy-done.13, bf16[128,1024]{1,0:T(8,128)(2,1)} %copy-done.14, ...), custom_call_target="tpu_custom_call" | custom-call | tf_op jit(solution)/shard_map/pallas_call | solution.py:38
  55.3 7.0 %collective-permute-done.7 = bf16[128,256]{1,0:T(8,128)(2,1)S(1)} collective-permute-done((bf16[128,256]{1,0:T(8,128)(2,1)S(1)}, bf16[128,256]{1,0:T(8,128)(2,1)S(1)}, u32[]{:S(2)}, u32[]{:S(2)}) %collective-permute-start.7) | collective-permute-done | bytes 65568 | tf_op jit(solution)/shard_map/ppermute | solution.py:388
  68.1 8.8 %shard_map.248 = (bf16[128,256]{1,0:T(8,128)(2,1)}, bf16[128,256]{1,0:T(8,128)(2,1)}, bf16[128,256]{1,0:T(8,128)(2,1)}, bf16[128,256]{1,0:T(8,128)(2,1)}, f32[4,64,512]{2,1,0:T(8,128)}, /*index=5*/f32[4,1,512]{2,1,0:T(1,128)}) custom-call(bf16[512,256]{1,0:T(8,128)(2,1)} %get-tuple-element.72.q, s32[1,512]{1,0:T(1,128)} %max.10.lim, ...), custom_call_target="tpu_custom_call" | custom-call | flops 10000000000 | tf_op jit(solution)/shard_map/pallas_call | solution.py:38
  76.9 4.2 %collective-permute-done.18.refs_6_ = bf16[128,1024]{1,0:T(8,128)(2,1)S(1)} collective-permute-done((bf16[128,1024]{1,0:T(8,128)(2,1)S(1)}, bf16[128,1024]{1,0:T(8,128)(2,1)S(1)}, u32[]{:S(2)}, u32[]{:S(2)}) %collective-permute-start.18) | collective-permute-done | bytes 262176 | tf_op jit(solution)/shard_map/ppermute | solution.py:388
  81.1 6.1 %collective-permute-start.20 = (bf16[128,256]{1,0:T(8,128)(2,1)}, bf16[128,256]{1,0:T(8,128)(2,1)S(1)}, u32[]{:S(2)}, u32[]{:S(2)}) collective-permute-start(bf16[128,256]{1,0:T(8,128)(2,1)} %get-tuple-element.78.refs_5_), channel_id=1, source_target_pairs={{0,1},{1,0},{2,3},{3,2},{4,5},{5,4},{6,7},{7,6},{8,9},{9,8},{10,11... | collective-permute-start | bytes 196616 | tf_op jit(solution)/shard_map/ppermute | solution.py:388
  89.9 5.7 %collective-permute-done.21.refs_2_ = bf16[128,256]{1,0:T(8,128)(2,1)S(1)} collective-permute-done((bf16[128,256]{1,0:T(8,128)(2,1)}, bf16[128,256]{1,0:T(8,128)(2,1)S(1)}, u32[]{:S(2)}, u32[]{:S(2)}) %collective-permute-start.21) | collective-permute-done | bytes 65568 | tf_op jit(solution)/shard_map/ppermute | solution.py:388
  99.7 4.2 %shard_map.249 = (f32[128,1024]{1,0:T(8,128)}, bf16[128,1024]{1,0:T(8,128)(2,1)}) custom-call(s32[8]{0:T(128)} %copy-done.40, bf16[128,1024]{1,0:T(8,128)(2,1)} %bitcast.70, f32[1,1024]{1,0:T(1,128)} %reshape.255.gain, bf16[4,128,1024]{2,1,0:T(8,128)(2,1)} %copy-done, bf16[4,128,1024]{2,1,0:T(8,128)(2,1)} %copy-done.2, ...), custom_call_target="tpu_custom_call" | custom-call | tf_op jit(solution)/shard_map/pallas_call | solution.py:38
  110.3 7.0 %collective-permute-done.24.refs_1_ = bf16[128,1024]{1,0:T(8,128)(2,1)S(1)} collective-permute-done((bf16[128,1024]{1,0:T(8,128)(2,1)}, bf16[128,1024]{1,0:T(8,128)(2,1)S(1)}, u32[]{:S(2)}, u32[]{:S(2)}) %collective-permute-start.24) | collective-permute-done | bytes 262176 | tf_op jit(solution)/shard_map/ppermute | solution.py:388
  117.3 9.2 %collective-permute-done.25.refs_2_ = bf16[128,1024]{1,0:T(8,128)(2,1)S(1)} collective-permute-done((bf16[128,1024]{1,0:T(8,128)(2,1)}, bf16[128,1024]{1,0:T(8,128)(2,1)S(1)}, u32[]{:S(2)}, u32[]{:S(2)}) %collective-permute-start.25) | collective-permute-done | bytes 262176 | tf_op jit(solution)/shard_map/ppermute | solution.py:388
  127.2 24.2 %shard_map.250 = (bf16[128,1024]{1,0:T(8,128)(2,1)}, bf16[128,1024]{1,0:T(8,128)(2,1)}, bf16[128,1024]{1,0:T(8,128)(2,1)}, bf16[128,1024]{1,0:T(8,128)(2,1)}, bf...) custom-call(f32[512,16]{1,0:T(8,128)} %get-tuple-element.134.chosen, ...), custom_call_target="tpu_custom_call" | custom-call | tf_op jit(solution)/shard_map/pallas_call | solution.py:586
  151.4 5.1 %collective-permute-start.27 = (bf16[128,1024]{1,0:T(8,128)(2,1)}, bf16[128,1024]{1,0:T(8,128)(2,1)S(1)}, u32[]{:S(2)}, u32[]{:S(2)}) collective-permute-start(bf16[128,1024]{1,0:T(8,128)(2,1)} %get-tuple-element.92), channel_id=1, source_target_pairs={{0,1},{1,0},{2,3},{3,2},{4,5},{5,4},{6,7},{7,6},{8,9},{9,8},{10,11... | collective-permute-start | bytes 786440 | tf_op jit(solution)/shard_map/ppermute | solution.py:388
  159.0 16.8 %shard_map.251 = (bf16[128,1024]{1,0:T(8,128)(2,1)}, bf16[128,1024]{1,0:T(8,128)(2,1)}, bf16[128,1024]{1,0:T(8,128)(2,1)}, bf16[128,1024]{1,0:T(8,128)(2,1)}, bf16[8,3,16,128,128]{4,3,2,1,0:T(8,128)(2,1)}) custom-call(bf16[512,2048]{1,0:T(8,128)(2,1)} %get-tuple-element.84.active, bf16[512,2048]{1,0:T(8,128)(2,1)} %get-tuple-element.85.gate, ...), custom_call_target="tpu_custom_call" | custom-call | tf_op jit(solution)/shard_map/pallas_call | solution.py:606
  178.9 4.3 %shard_map.252 = (f32[128,1024]{1,0:T(8,128)}, bf16[128,1024]{1,0:T(8,128)(2,1)}, f32[1,1024]{1,0:T(1,128)}, bf16[128,256]{1,0:T(8,128)(2,1)}, bf16[128,256]{1,0...) custom-call(s32[8]{0:T(128)} %copy-done.40, f32[128,1024]{1,0:T(8,128)} %get-tuple-element.82.middle, ...), custom_call_target="tpu_custom_call" | custom-call | tf_op jit(solution)/shard_map/pallas_call | solution.py:38
  183.2 3.9 %collective-permute-start.30 = (bf16[128,256]{1,0:T(8,128)(2,1)}, bf16[128,256]{1,0:T(8,128)(2,1)S(1)}, u32[]{:S(2)}, u32[]{:S(2)}) collective-permute-start(bf16[128,256]{1,0:T(8,128)(2,1)} %get-tuple-element.96), channel_id=1, source_target_pairs={{0,1},{1,0},{2,3},{3,2},{4,5},{5,4},{6,7},{7,6},{8,9},{9,8},{10,11... | collective-permute-start | bytes 196616 | tf_op jit(solution)/shard_map/ppermute | solution.py:388
  196.6 6.9 %shard_map.254 = (bf16[512,256]{1,0:T(8,128)(2,1)}, f32[4,64,512]{2,1,0:T(8,128)}) custom-call(bf16[512,256]{1,0:T(8,128)(2,1)} %get-tuple-element.72.q, s32[1,512]{1,0:T(1,128)} %max.10.lim, bf16[512,256]{1,0:T(8,128)(2,1)} %copy-done.46, s32[512,1]{1,0:T(8,128)} %broadcast_add_fusion.refs_3_.kpos, f32[4,1,512]{2,1,0:T(1,128)} %get-tuple-element.103.lse, ...), custom_call_target="tpu_custom_call" | custom-call | flops 10000000000 | tf_op jit(solution)/shard_map/pallas_call | solution.py:38
  209.8 7.8 %shard_map.255 = (f32[512,256]{1,0:T(8,128)}, bf16[512,256]{1,0:T(8,128)(2,1)}) custom-call(bf16[512,256]{1,0:T(8,128)(2,1)} %get-tuple-element.72.q, s32[1,512]{1,0:T(1,128)} %max.10.lim, bf16[512,256]{1,0:T(8,128)(2,1)} %get-tuple-element.70.refs_0_.kv, s32[512,1]{1,0:T(8,128)} %copy-done.15, f32[4,1,512]{2,1,0:T(1,128)} %get-tuple-element.103.lse, ...), custom_call_target="tpu_custom_call" | custom-call | flops 10000000000 | tf_op jit(solution)/shard_map/pallas_call | solution.py:38
  218.4 5.1 %shard_map.256 = (bf16[128,1024]{1,0:T(8,128)(2,1)}, bf16[128,1024]{1,0:T(8,128)(2,1)}, bf16[128,1024]{1,0:T(8,128)(2,1)}, bf16[128,1024]{1,0:T(8,128)(2,1)}, bf...) custom-call(s32[8]{0:T(128)} %copy-done.40, bf16[512,256]{1,0:T(8,128)(2,1)} %get-tuple-element.109.dq, ...), custom_call_target="tpu_custom_call" | custom-call | tf_op jit(solution)/shard_map/pallas_call | solution.py:38
  229.7 4.9 %shard_map.258 = (bf16[4,160,768]{2,1,0:T(8,128)(2,1)}, bf16[4,160,768]{2,1,0:T(8,128)(2,1)}) custom-call(s32[8]{0:T(128)} %copy-done.40, bf16[512,1024]{1,0:T(8,128)(2,1)} %get-tuple-element.116.x1, bf16[512,512]{1,0:T(8,128)(2,1)} %get-tuple-element.118.grads, f32[16,1024]{1,0:T(8,128)} %get-tuple-element.119.router_part, ...), custom_call_target="tpu_custom_call" | custom-call | tf_op jit(solution)/shard_map/pallas_call | solution.py:38
  245.1 8.6 %collective-permute-done.44 = bf16[2,160,768]{2,1,0:T(8,128)(2,1)S(1)} collective-permute-done((bf16[2,160,768]{2,1,0:T(8,128)(2,1)S(1)}, bf16[2,160,768]{2,1,0:T(8,128)(2,1)S(1)}, u32[]{:S(2)}, u32[]{:S(2)}) %collective-permute-start.44) | collective-permute-done | bytes 491552 | tf_op jit(solution)/shard_map/ppermute | solution.py:419
  258.3 10.7 %collective-permute-done.40.refs_2_ = bf16[128,1024]{1,0:T(8,128)(2,1)S(1)} collective-permute-done((bf16[128,1024]{1,0:T(8,128)(2,1)S(1)}, bf16[128,1024]{1,0:T(8,128)(2,1)S(1)}, u32[]{:S(2)}, u32[]{:S(2)}) %collective-permute-start.40) | collective-permute-done | bytes 262176 | tf_op jit(solution)/shard_map/ppermute | solution.py:388
  272.4 5.3 %collective-permute-start.46 = (f32[18,128]{1,0:T(8,128)S(1)}, f32[18,128]{1,0:T(8,128)S(1)}, u32[]{:S(2)}, u32[]{:S(2)}) collective-permute-start(f32[18,128]{1,0:T(8,128)S(1)} %slice.129), channel_id=1, source_target_pairs={{0,1},{1,0},{2,3},{3,2},{4,5},{5,4},{6,7},{7,6},{8,9},{9,8},{10,11... | collective-permute-start | bytes 27656 | tf_op jit(solution)/shard_map/ppermute | solution.py:388
  (262 shorter events, 107.9 us)
Async XLA Ops:
  7.2 119.3 %all-gather.3.cloned.1.call-start = ((), (), s32[]{:S(2)}) async-start(), calls=%async_computation.2 | async-start | bytes 14155776 | tf_op jit(solution)/shard_map/all_gather | solution.py:581
  10.0 275.2 %reduce-scatter.2.cloned.1.call-start = ((), (), s32[]{:S(2)}) async-start(), calls=%async_computation.1 | async-start | bytes 14155776 | tf_op jit(solution)/shard_map/reduce_scatter | solution.py:626
  16.5 25.8 %collective-permute-start.10 = (bf16[128,1024]{1,0:T(8,128)(2,1)S(1)}, bf16[128,1024]{1,0:T(8,128)(2,1)S(1)}, u32[]{:S(2)}, u32[]{:S(2)}) collective-permute-start(bf16[128,1024]{1,0:T(8,128)(2,1)S(1)} %bitcast.73), channel_id=1, source_target_pairs={{0,1},{1,0},{2,3},{3,2},{4,5},{5,4},{6,7},{7,6},{8,9},{9,8},{10,11... | collective-permute-start | bytes 786440 | tf_op jit(solution)/shard_map/ppermute | solution.py:388
  17.4 25.0 %collective-permute-start.11 = (bf16[128,1024]{1,0:T(8,128)(2,1)S(1)}, bf16[128,1024]{1,0:T(8,128)(2,1)S(1)}, u32[]{:S(2)}, u32[]{:S(2)}) collective-permute-start(bf16[128,1024]{1,0:T(8,128)(2,1)S(1)} %bitcast.74), channel_id=1, source_target_pairs={{0,2},{1,3},{2,0},{3,1},{4,6},{5,7},{6,4},{7,5},{8,10},{9,11},{10,... | collective-permute-start | bytes 786440 | tf_op jit(solution)/shard_map/ppermute | solution.py:388
  47.7 16.9 %collective-permute-start.13 = (bf16[512,256]{1,0:T(8,128)(2,1)}, bf16[512,256]{1,0:T(8,128)(2,1)S(1)}, u32[]{:S(2)}, u32[]{:S(2)}) collective-permute-start(bf16[512,256]{1,0:T(8,128)(2,1)} %get-tuple-element.70.refs_0_.kv), channel_id=1, source_target_pairs={{0,4},{4,0},{1,5},{5,1},{2,6},{6,2},{3,7},{7,3},{8,12},{12,8},{9,1... | collective-permute-start | bytes 786440 | tf_op jit(solution)/shard_map/ppermute | solution.py:411
  62.3 18.7 %collective-permute-start.18 = (bf16[128,1024]{1,0:T(8,128)(2,1)S(1)}, bf16[128,1024]{1,0:T(8,128)(2,1)S(1)}, u32[]{:S(2)}, u32[]{:S(2)}) collective-permute-start(bf16[128,1024]{1,0:T(8,128)(2,1)S(1)} %bitcast.80), channel_id=1, source_target_pairs={{0,2},{1,3},{2,0},{3,1},{4,6},{5,7},{6,4},{7,5},{8,10},{9,11},{10,... | collective-permute-start | bytes 786440 | tf_op jit(solution)/shard_map/ppermute | solution.py:388
  62.9 18.2 %collective-permute-start.19 = (bf16[128,1024]{1,0:T(8,128)(2,1)S(1)}, bf16[128,1024]{1,0:T(8,128)(2,1)S(1)}, u32[]{:S(2)}, u32[]{:S(2)}) collective-permute-start(bf16[128,1024]{1,0:T(8,128)(2,1)S(1)} %bitcast.81), channel_id=1, source_target_pairs={{0,3},{1,2},{2,1},{3,0},{4,7},{5,6},{6,5},{7,4},{8,11},{9,10},{10,... | collective-permute-start | bytes 786440 | tf_op jit(solution)/shard_map/ppermute | solution.py:388
  64.6 23.5 %collective-permute-start.14 = (bf16[128,1024]{1,0:T(8,128)(2,1)S(1)}, bf16[128,1024]{1,0:T(8,128)(2,1)S(1)}, u32[]{:S(2)}, u32[]{:S(2)}) collective-permute-start(bf16[128,1024]{1,0:T(8,128)(2,1)S(1)} %pad_maximum_fusion.3), channel_id=1, source_target_pairs={{0,4},{4,0},{1,5},{5,1},{2,6},{6,2},{3,7},{7,3},{8,12},{12,8},{9,1... | collective-permute-start | bytes 786440 | tf_op jit(solution)/shard_map/ppermute | solution.py:411
  64.9 24.7 %collective-permute-start.15 = (bf16[128,1024]{1,0:T(8,128)(2,1)S(1)}, bf16[128,1024]{1,0:T(8,128)(2,1)S(1)}, u32[]{:S(2)}, u32[]{:S(2)}) collective-permute-start(bf16[128,1024]{1,0:T(8,128)(2,1)S(1)} %pad_maximum_fusion.3), channel_id=1, source_target_pairs={{0,16},{8,24},{16,0},{24,8},{1,17},{9,25},{17,1},{25,9},{2,18},{10... | collective-permute-start | bytes 786440 | tf_op jit(solution)/shard_map/ppermute | solution.py:419
  66.0 23.6 %collective-permute-start.16 = (bf16[128,1024]{1,0:T(8,128)(2,1)S(1)}, bf16[128,1024]{1,0:T(8,128)(2,1)S(1)}, u32[]{:S(2)}, u32[]{:S(2)}) collective-permute-start(bf16[128,1024]{1,0:T(8,128)(2,1)S(1)} %pad_maximum_fusion.3), channel_id=1, source_target_pairs={{0,20},{4,16},{8,28},{12,24},{16,4},{20,0},{24,12},{28,8},{1,21},{... | collective-permute-start | bytes 786440 | tf_op jit(solution)/shard_map/ppermute | solution.py:423
  104.9 21.5 %collective-permute-start.25 = (bf16[128,1024]{1,0:T(8,128)(2,1)}, bf16[128,1024]{1,0:T(8,128)(2,1)S(1)}, u32[]{:S(2)}, u32[]{:S(2)}) collective-permute-start(bf16[128,1024]{1,0:T(8,128)(2,1)} %get-tuple-element.83.refs_0_), channel_id=1, source_target_pairs={{0,2},{1,3},{2,0},{3,1},{4,6},{5,7},{6,4},{7,5},{8,10},{9,11},{10,... | collective-permute-start | bytes 786440 | tf_op jit(solution)/shard_map/ppermute | solution.py:388
  106.3 20.2 %collective-permute-start.26 = (bf16[128,1024]{1,0:T(8,128)(2,1)}, bf16[128,1024]{1,0:T(8,128)(2,1)S(1)}, u32[]{:S(2)}, u32[]{:S(2)}) collective-permute-start(bf16[128,1024]{1,0:T(8,128)(2,1)} %get-tuple-element.83.refs_0_), channel_id=1, source_target_pairs={{0,3},{1,2},{2,1},{3,0},{4,7},{5,6},{6,5},{7,4},{8,11},{9,10},{10,... | collective-permute-start | bytes 786440 | tf_op jit(solution)/shard_map/ppermute | solution.py:388
  151.4 24.3 %collective-permute-start.27 = (bf16[128,1024]{1,0:T(8,128)(2,1)}, bf16[128,1024]{1,0:T(8,128)(2,1)S(1)}, u32[]{:S(2)}, u32[]{:S(2)}) collective-permute-start(bf16[128,1024]{1,0:T(8,128)(2,1)} %get-tuple-element.92), channel_id=1, source_target_pairs={{0,1},{1,0},{2,3},{3,2},{4,5},{5,4},{6,7},{7,6},{8,9},{9,8},{10,11... | collective-permute-start | bytes 786440 | tf_op jit(solution)/shard_map/ppermute | solution.py:388
  156.6 21.5 %collective-permute-start.28 = (bf16[128,1024]{1,0:T(8,128)(2,1)}, bf16[128,1024]{1,0:T(8,128)(2,1)S(1)}, u32[]{:S(2)}, u32[]{:S(2)}) collective-permute-start(bf16[128,1024]{1,0:T(8,128)(2,1)} %get-tuple-element.93), channel_id=1, source_target_pairs={{0,2},{1,3},{2,0},{3,1},{4,6},{5,7},{6,4},{7,5},{8,10},{9,11},{10,... | collective-permute-start | bytes 786440 | tf_op jit(solution)/shard_map/ppermute | solution.py:388
  157.3 20.8 %collective-permute-start.29 = (bf16[128,1024]{1,0:T(8,128)(2,1)}, bf16[128,1024]{1,0:T(8,128)(2,1)S(1)}, u32[]{:S(2)}, u32[]{:S(2)}) collective-permute-start(bf16[128,1024]{1,0:T(8,128)(2,1)} %get-tuple-element.94), channel_id=1, source_target_pairs={{0,3},{1,2},{2,1},{3,0},{4,7},{5,6},{6,5},{7,4},{8,11},{9,10},{10,... | collective-permute-start | bytes 786440 | tf_op jit(solution)/shard_map/ppermute | solution.py:388
  195.0 22.7 %collective-permute-start.37 = (bf16[128,1024]{1,0:T(8,128)(2,1)}, bf16[128,1024]{1,0:T(8,128)(2,1)S(1)}, u32[]{:S(2)}, u32[]{:S(2)}) collective-permute-start(bf16[128,1024]{1,0:T(8,128)(2,1)} %get-tuple-element.108.refs_0_), channel_id=1, source_target_pairs={{0,2},{1,3},{2,0},{3,1},{4,6},{5,7},{6,4},{7,5},{8,10},{9,11},{10,... | collective-permute-start | bytes 786440 | tf_op jit(solution)/shard_map/ppermute | solution.py:388
  204.0 19.5 %collective-permute-start.33 = (bf16[128,1024]{1,0:T(8,128)(2,1)S(1)}, bf16[128,1024]{1,0:T(8,128)(2,1)S(1)}, u32[]{:S(2)}, u32[]{:S(2)}) collective-permute-start(bf16[128,1024]{1,0:T(8,128)(2,1)S(1)} %copy-done.49), channel_id=1, source_target_pairs={{0,1},{1,0},{2,3},{3,2},{4,5},{5,4},{6,7},{7,6},{8,9},{9,8},{10,11... | collective-permute-start | bytes 786440 | tf_op jit(solution)/shard_map/ppermute | solution.py:388
  204.9 21.1 %collective-permute-start.34 = (bf16[128,1024]{1,0:T(8,128)(2,1)S(1)}, bf16[128,1024]{1,0:T(8,128)(2,1)S(1)}, u32[]{:S(2)}, u32[]{:S(2)}) collective-permute-start(bf16[128,1024]{1,0:T(8,128)(2,1)S(1)} %copy-done.48), channel_id=1, source_target_pairs={{0,2},{1,3},{2,0},{3,1},{4,6},{5,7},{6,4},{7,5},{8,10},{9,11},{10,... | collective-permute-start | bytes 786440 | tf_op jit(solution)/shard_map/ppermute | solution.py:388
  209.8 19.2 %collective-permute-start.42 = (bf16[128,1024]{1,0:T(8,128)(2,1)S(1)}, bf16[128,1024]{1,0:T(8,128)(2,1)S(1)}, u32[]{:S(2)}, u32[]{:S(2)}) collective-permute-start(bf16[128,1024]{1,0:T(8,128)(2,1)S(1)} %collective-permute-done.36.refs_1_), channel_id=1, source_target_pairs={{0,2},{1,3},{2,0},{3,1},{4,6},{5,7},{6,4},{7,5},{8,10},{9,11},{10,... | collective-permute-start | bytes 786440 | tf_op jit(solution)/shard_map/ppermute | solution.py:388
  238.6 16.8 %collective-permute-start.35 = (bf16[128,1024]{1,0:T(8,128)(2,1)S(1)}, bf16[128,1024]{1,0:T(8,128)(2,1)S(1)}, u32[]{:S(2)}, u32[]{:S(2)}) collective-permute-start(bf16[128,1024]{1,0:T(8,128)(2,1)S(1)} %copy-done.47), channel_id=1, source_target_pairs={{0,3},{1,2},{2,1},{3,0},{4,7},{5,6},{6,5},{7,4},{8,11},{9,10},{10,... | collective-permute-start | bytes 786440 | tf_op jit(solution)/shard_map/ppermute | solution.py:388
  240.7 17.6 %collective-permute-start.39 = (bf16[128,1024]{1,0:T(8,128)(2,1)}, bf16[128,1024]{1,0:T(8,128)(2,1)S(1)}, u32[]{:S(2)}, u32[]{:S(2)}) collective-permute-start(bf16[128,1024]{1,0:T(8,128)(2,1)} %get-tuple-element.113), channel_id=1, source_target_pairs={{0,1},{1,0},{2,3},{3,2},{4,5},{5,4},{6,7},{7,6},{8,9},{9,8},{10,11... | collective-permute-start | bytes 786440 | tf_op jit(solution)/shard_map/ppermute | solution.py:388
  240.7 28.4 %collective-permute-start.40 = (bf16[128,1024]{1,0:T(8,128)(2,1)S(1)}, bf16[128,1024]{1,0:T(8,128)(2,1)S(1)}, u32[]{:S(2)}, u32[]{:S(2)}) collective-permute-start(bf16[128,1024]{1,0:T(8,128)(2,1)S(1)} %copy-done.51), channel_id=1, source_target_pairs={{0,2},{1,3},{2,0},{3,1},{4,6},{5,7},{6,4},{7,5},{8,10},{9,11},{10,... | collective-permute-start | bytes 786440 | tf_op jit(solution)/shard_map/ppermute | solution.py:388
  243.1 26.0 %collective-permute-start.41 = (bf16[128,1024]{1,0:T(8,128)(2,1)S(1)}, bf16[128,1024]{1,0:T(8,128)(2,1)S(1)}, u32[]{:S(2)}, u32[]{:S(2)}) collective-permute-start(bf16[128,1024]{1,0:T(8,128)(2,1)S(1)} %copy-done.50), channel_id=1, source_target_pairs={{0,3},{1,2},{2,1},{3,0},{4,7},{5,6},{6,5},{7,4},{8,11},{9,10},{10,... | collective-permute-start | bytes 786440 | tf_op jit(solution)/shard_map/ppermute | solution.py:388
  253.9 18.5 %collective-permute-start.45 = (bf16[160,768]{1,0:T(8,128)(2,1)S(1)}, bf16[160,768]{1,0:T(8,128)(2,1)S(1)}, u32[]{:S(2)}, u32[]{:S(2)}) collective-permute-start(bf16[160,768]{1,0:T(8,128)(2,1)S(1)} %fusion.8), channel_id=1, source_target_pairs={{0,4},{4,0},{1,5},{5,1},{2,6},{6,2},{3,7},{7,3},{8,12},{12,8},{9,1... | collective-permute-start | bytes 737288 | tf_op jit(solution)/shard_map/ppermute | solution.py:411
  (83 other events, 652.8 us)
Sparse Core Ops, SparseCore 0:
  10.1 93.3 all-gather.2
  178.3 102.0 reduce-scatter.1

commit v4 on v3

--- a/solution.py
+++ b/solution.py
@@ -14,7 +14,7 @@
 CAP = 320
 EPS = 1e-06
 FILL = -1e30
-EXPERTS_PER_STEP = 2
+EXPERTS_PER_STEP = 4
 ROW_TILE = 256
 LINES = 32
 f32 = jnp.float32
@@ -445,9 +445,9 @@
         both = jnp.concatenate([keep, send], axis=0)
         return lax.psum_scatter(both, ("dp", "seq"), scatter_dimension=0, tiled=False).astype(f32)
     got = swap_core(send)
-    far = swap_y((keep[2:].astype(f32) + got[2:].astype(f32)).astype(bf16))
-    mine = keep[:2].astype(f32) + got[:2].astype(f32) + far.astype(f32)
-    return mine[0] + swap_x(mine[1].astype(bf16)).astype(f32)
+    low = [(keep[i].astype(f32) + got[i].astype(f32)).astype(bf16) for i in (1, 2, 3)]
+    far = swap_x(low[0]).astype(f32) + swap_y(low[1]).astype(f32) + swap_xy(low[2]).astype(f32)
+    return keep[0].astype(f32) + got[0].astype(f32) + far
 
 
 def per_device(
@@ -701,8 +701,7 @@
     )
     weights = plane_scatter(weight_keep, weight_send, fancy)
     total = weights[rows : rows + E + 2, :rows]
-    for bit in range(n.bit_length() - 1):
-        total = total + across(total, 1 << bit)
+    total = sum(spread(total)[1:], total)
     total = lax.dynamic_slice_in_dim(total, me * shard, shard, axis=1)
     weights = weights[:rows]
     kv_wide = key_projection.shape[1]

time: 296 us -> 289 us (0.976)
  Pallas kernels: 92.1 us -> 86.6 us
    ppermute x35 -> x36, waiting for transfers between devices: 62.6 us -> 73.3 us  [across(): lax.ppermute(v, 'tensor', [(i, i ^ j) for i in range(lax.axis_size('tenso...]
    ppermute x3, waiting for transfers between devices: 10.9 us -> 2.33 us  [swap_y(): return lax.ppermute(v, 'dp', [(i, i ^ 2) for i in range(4)])]
    pallas_call x1, Pallas kernels: 24.2 us -> 20.4 us  [per_device(): pl.pallas_call(functools.partial(expert_kernel, n), out_shape=tuple([sds(...]
    unnamed x116 -> x110, local copies, waits for them, and re-layouts: 7.15 us -> 6.47 us
    ppermute x35 -> x36, starting transfers between devices: 63.4 us -> 63.2 us  [across(): lax.ppermute(v, 'tensor', [(i, i ^ j) for i in range(lax.axis_size('tenso...]
  transfers between devices with their start and end apart: 50 -> 52, of which waited for: 23 -> 24; matrix products, arithmetic and copies ran while one was open for 5% -> 5% of each run, Pallas kernels for 23% -> 23%
where the time goes in v4:
time: 289 us
  waiting for transfers between devices  86.8 us (30%)
  Pallas kernels  86.6 us (30%)
  starting transfers between devices  73.7 us (26%)
  between operations  14.7 us (5%)
  local copies, waits for them, and re-layouts  13.4 us (5%)
  other arithmetic  13.1 us (5%)
    ppermute x36, waiting for transfers between devices, across(): lax.ppermute(v, 'tensor', [(i, i ^ j) for i in range(lax.axis_size('tenso...  73.3 us
    ppermute x36, starting transfers between devices, across(): lax.ppermute(v, 'tensor', [(i, i ^ j) for i in range(lax.axis_size('tenso...  63.2 us
    pallas_call x10, Pallas kernels, whole_call(): pl.pallas_call(body, out_shape=outs, grid_spec=pltpu.PrefetchScalarGridSp...  50.8 us
    pallas_call x1, Pallas kernels, per_device(): pl.pallas_call(functools.partial(expert_kernel, n), out_shape=tuple([sds(...  20.4 us
    pallas_call x1, Pallas kernels, per_device(): pl.pallas_call(functools.partial(expert_back_kernel, n), out_shape=tuple(...  15.4 us
    unnamed x110, local copies, waits for them, and re-layouts  6.47 us
  transfers between devices with their start and end apart: 52, of which 24 were waited for; matrix products, arithmetic and copies ran while one was open for 5% of the time, Pallas kernels for 23%

profile of v4, /device:TPU:0, one launch (start us, length us, event | category | flops | bytes accessed | tf_op | source)
XLA Modules:
  0.0 288.6 jit_solution(8654581115690902819)
XLA Ops:
  17.4 3.5 %collective-permute-start.11 = (bf16[128,1024]{1,0:T(8,128)(2,1)S(1)}, bf16[128,1024]{1,0:T(8,128)(2,1)S(1)}, u32[]{:S(2)}, u32[]{:S(2)}) collective-permute-start(bf16[128,1024]{1,0:T(8,128)(2,1)S(1)} %bitcast.76), channel_id=1, source_target_pairs={{0,2},{1,3},{2,0},{3,1},{4,6},{5,7},{6,4},{7,5},{8,10},{9,11},{10,... | collective-permute-start | bytes 786440 | tf_op jit(solution)/shard_map/ppermute | solution.py:388
  26.8 5.4 %collective-permute-done.3 = bf16[144,512]{1,0:T(8,128)(2,1)S(1)} collective-permute-done((bf16[144,512]{1,0:T(8,128)(2,1)S(1)}, bf16[144,512]{1,0:T(8,128)(2,1)S(1)}, u32[]{:S(2)}, u32[]{:S(2)}) %collective-permute-start.3) | collective-permute-done | bytes 147488 | tf_op jit(solution)/shard_map/ppermute | solution.py:411
  43.2 4.5 %shard_map.247 = (bf16[512,1024]{1,0:T(8,128)(2,1)}, bf16[512,256]{1,0:T(8,128)(2,1)}, bf16[512,256]{1,0:T(8,128)(2,1)}) custom-call(s32[8]{0:T(128)} %copy-done.39, bf16[128,1024]{1,0:T(8,128)(2,1)} %bitcast.71, bf16[128,1024]{1,0:T(8,128)(2,1)} %copy-done.12, bf16[128,1024]{1,0:T(8,128)(2,1)} %copy-done.13, bf16[128,1024]{1,0:T(8,128)(2,1)} %copy-done.14, ...), custom_call_target="tpu_custom_call" | custom-call | tf_op jit(solution)/shard_map/pallas_call | solution.py:38
  55.3 7.0 %collective-permute-done.7 = bf16[128,256]{1,0:T(8,128)(2,1)S(1)} collective-permute-done((bf16[128,256]{1,0:T(8,128)(2,1)S(1)}, bf16[128,256]{1,0:T(8,128)(2,1)S(1)}, u32[]{:S(2)}, u32[]{:S(2)}) %collective-permute-start.7) | collective-permute-done | bytes 65568 | tf_op jit(solution)/shard_map/ppermute | solution.py:388
  68.1 8.8 %shard_map.248 = (bf16[128,256]{1,0:T(8,128)(2,1)}, bf16[128,256]{1,0:T(8,128)(2,1)}, bf16[128,256]{1,0:T(8,128)(2,1)}, bf16[128,256]{1,0:T(8,128)(2,1)}, f32[4,64,512]{2,1,0:T(8,128)}, /*index=5*/f32[4,1,512]{2,1,0:T(1,128)}) custom-call(bf16[512,256]{1,0:T(8,128)(2,1)} %get-tuple-element.72.q, s32[1,512]{1,0:T(1,128)} %max.10.lim, ...), custom_call_target="tpu_custom_call" | custom-call | flops 10000000000 | tf_op jit(solution)/shard_map/pallas_call | solution.py:38
  76.9 4.2 %collective-permute-done.18.refs_6_ = bf16[128,1024]{1,0:T(8,128)(2,1)S(1)} collective-permute-done((bf16[128,1024]{1,0:T(8,128)(2,1)S(1)}, bf16[128,1024]{1,0:T(8,128)(2,1)S(1)}, u32[]{:S(2)}, u32[]{:S(2)}) %collective-permute-start.18) | collective-permute-done | bytes 262176 | tf_op jit(solution)/shard_map/ppermute | solution.py:388
  81.1 6.1 %collective-permute-start.20 = (bf16[128,256]{1,0:T(8,128)(2,1)}, bf16[128,256]{1,0:T(8,128)(2,1)S(1)}, u32[]{:S(2)}, u32[]{:S(2)}) collective-permute-start(bf16[128,256]{1,0:T(8,128)(2,1)} %get-tuple-element.78.refs_5_), channel_id=1, source_target_pairs={{0,1},{1,0},{2,3},{3,2},{4,5},{5,4},{6,7},{7,6},{8,9},{9,8},{10,11... | collective-permute-start | bytes 196616 | tf_op jit(solution)/shard_map/ppermute | solution.py:388
  89.9 5.7 %collective-permute-done.21.refs_2_ = bf16[128,256]{1,0:T(8,128)(2,1)S(1)} collective-permute-done((bf16[128,256]{1,0:T(8,128)(2,1)}, bf16[128,256]{1,0:T(8,128)(2,1)S(1)}, u32[]{:S(2)}, u32[]{:S(2)}) %collective-permute-start.21) | collective-permute-done | bytes 65568 | tf_op jit(solution)/shard_map/ppermute | solution.py:388
  99.7 4.2 %shard_map.249 = (f32[128,1024]{1,0:T(8,128)}, bf16[128,1024]{1,0:T(8,128)(2,1)}) custom-call(s32[8]{0:T(128)} %copy-done.39, bf16[128,1024]{1,0:T(8,128)(2,1)} %bitcast.72, f32[1,1024]{1,0:T(1,128)} %reshape.269.gain, bf16[4,128,1024]{2,1,0:T(8,128)(2,1)} %copy-done, bf16[4,128,1024]{2,1,0:T(8,128)(2,1)} %copy-done.2, ...), custom_call_target="tpu_custom_call" | custom-call | tf_op jit(solution)/shard_map/pallas_call | solution.py:38
  110.3 7.0 %collective-permute-done.24.refs_1_ = bf16[128,1024]{1,0:T(8,128)(2,1)S(1)} collective-permute-done((bf16[128,1024]{1,0:T(8,128)(2,1)}, bf16[128,1024]{1,0:T(8,128)(2,1)S(1)}, u32[]{:S(2)}, u32[]{:S(2)}) %collective-permute-start.24) | collective-permute-done | bytes 262176 | tf_op jit(solution)/shard_map/ppermute | solution.py:388
  117.3 9.2 %collective-permute-done.25.refs_2_ = bf16[128,1024]{1,0:T(8,128)(2,1)S(1)} collective-permute-done((bf16[128,1024]{1,0:T(8,128)(2,1)}, bf16[128,1024]{1,0:T(8,128)(2,1)S(1)}, u32[]{:S(2)}, u32[]{:S(2)}) %collective-permute-start.25) | collective-permute-done | bytes 262176 | tf_op jit(solution)/shard_map/ppermute | solution.py:388
  127.2 20.4 %shard_map.250 = (bf16[128,1024]{1,0:T(8,128)(2,1)}, bf16[128,1024]{1,0:T(8,128)(2,1)}, bf16[128,1024]{1,0:T(8,128)(2,1)}, bf16[128,1024]{1,0:T(8,128)(2,1)}, bf...) custom-call(f32[512,16]{1,0:T(8,128)} %get-tuple-element.137.chosen, ...), custom_call_target="tpu_custom_call" | custom-call | tf_op jit(solution)/shard_map/pallas_call | solution.py:586
  147.6 5.1 %collective-permute-start.27 = (bf16[128,1024]{1,0:T(8,128)(2,1)}, bf16[128,1024]{1,0:T(8,128)(2,1)S(1)}, u32[]{:S(2)}, u32[]{:S(2)}) collective-permute-start(bf16[128,1024]{1,0:T(8,128)(2,1)} %get-tuple-element.92), channel_id=1, source_target_pairs={{0,1},{1,0},{2,3},{3,2},{4,5},{5,4},{6,7},{7,6},{8,9},{9,8},{10,11... | collective-permute-start | bytes 786440 | tf_op jit(solution)/shard_map/ppermute | solution.py:388
  155.2 15.4 %shard_map.251 = (bf16[128,1024]{1,0:T(8,128)(2,1)}, bf16[128,1024]{1,0:T(8,128)(2,1)}, bf16[128,1024]{1,0:T(8,128)(2,1)}, bf16[128,1024]{1,0:T(8,128)(2,1)}, bf16[8,3,16,128,128]{4,3,2,1,0:T(8,128)(2,1)}) custom-call(bf16[512,2048]{1,0:T(8,128)(2,1)} %get-tuple-element.84.active, bf16[512,2048]{1,0:T(8,128)(2,1)} %get-tuple-element.85.gate, ...), custom_call_target="tpu_custom_call" | custom-call | tf_op jit(solution)/shard_map/pallas_call | solution.py:606
  170.6 3.7 %collective-permute-done.28.refs_2_ = bf16[128,1024]{1,0:T(8,128)(2,1)S(1)} collective-permute-done((bf16[128,1024]{1,0:T(8,128)(2,1)}, bf16[128,1024]{1,0:T(8,128)(2,1)S(1)}, u32[]{:S(2)}, u32[]{:S(2)}) %collective-permute-start.28) | collective-permute-done | bytes 262176 | tf_op jit(solution)/shard_map/ppermute | solution.py:388
  175.1 4.3 %shard_map.252 = (f32[128,1024]{1,0:T(8,128)}, bf16[128,1024]{1,0:T(8,128)(2,1)}, f32[1,1024]{1,0:T(1,128)}, bf16[128,256]{1,0:T(8,128)(2,1)}, bf16[128,256]{1,0...) custom-call(s32[8]{0:T(128)} %copy-done.39, f32[128,1024]{1,0:T(8,128)} %get-tuple-element.82.middle, ...), custom_call_target="tpu_custom_call" | custom-call | tf_op jit(solution)/shard_map/pallas_call | solution.py:38
  179.3 4.0 %collective-permute-start.30 = (bf16[128,256]{1,0:T(8,128)(2,1)}, bf16[128,256]{1,0:T(8,128)(2,1)S(1)}, u32[]{:S(2)}, u32[]{:S(2)}) collective-permute-start(bf16[128,256]{1,0:T(8,128)(2,1)} %get-tuple-element.96), channel_id=1, source_target_pairs={{0,1},{1,0},{2,3},{3,2},{4,5},{5,4},{6,7},{7,6},{8,9},{9,8},{10,11... | collective-permute-start | bytes 196616 | tf_op jit(solution)/shard_map/ppermute | solution.py:388
  192.7 6.9 %shard_map.254 = (bf16[512,256]{1,0:T(8,128)(2,1)}, f32[4,64,512]{2,1,0:T(8,128)}) custom-call(bf16[512,256]{1,0:T(8,128)(2,1)} %get-tuple-element.72.q, s32[1,512]{1,0:T(1,128)} %max.10.lim, bf16[512,256]{1,0:T(8,128)(2,1)} %copy-done.45, s32[512,1]{1,0:T(8,128)} %broadcast_add_fusion.refs_3_.kpos, f32[4,1,512]{2,1,0:T(1,128)} %get-tuple-element.103.lse, ...), custom_call_target="tpu_custom_call" | custom-call | flops 10000000000 | tf_op jit(solution)/shard_map/pallas_call | solution.py:38
  206.0 7.6 %shard_map.255 = (f32[512,256]{1,0:T(8,128)}, bf16[512,256]{1,0:T(8,128)(2,1)}) custom-call(bf16[512,256]{1,0:T(8,128)(2,1)} %get-tuple-element.72.q, s32[1,512]{1,0:T(1,128)} %max.10.lim, bf16[512,256]{1,0:T(8,128)(2,1)} %get-tuple-element.70.refs_0_.kv, s32[512,1]{1,0:T(8,128)} %copy-done.15, f32[4,1,512]{2,1,0:T(1,128)} %get-tuple-element.103.lse, ...), custom_call_target="tpu_custom_call" | custom-call | flops 10000000000 | tf_op jit(solution)/shard_map/pallas_call | solution.py:38
  214.4 5.1 %shard_map.256 = (bf16[128,1024]{1,0:T(8,128)(2,1)}, bf16[128,1024]{1,0:T(8,128)(2,1)}, bf16[128,1024]{1,0:T(8,128)(2,1)}, bf16[128,1024]{1,0:T(8,128)(2,1)}, bf...) custom-call(s32[8]{0:T(128)} %copy-done.39, bf16[512,256]{1,0:T(8,128)(2,1)} %get-tuple-element.109.dq, ...), custom_call_target="tpu_custom_call" | custom-call | tf_op jit(solution)/shard_map/pallas_call | solution.py:38
  225.8 4.8 %shard_map.258 = (bf16[4,160,768]{2,1,0:T(8,128)(2,1)}, bf16[4,160,768]{2,1,0:T(8,128)(2,1)}) custom-call(s32[8]{0:T(128)} %copy-done.39, bf16[512,1024]{1,0:T(8,128)(2,1)} %get-tuple-element.116.x1, bf16[512,512]{1,0:T(8,128)(2,1)} %get-tuple-element.118.grads, f32[16,1024]{1,0:T(8,128)} %get-tuple-element.119.router_part, ...), custom_call_target="tpu_custom_call" | custom-call | tf_op jit(solution)/shard_map/pallas_call | solution.py:38
  241.8 8.3 %collective-permute-done.39.refs_1_ = bf16[128,1024]{1,0:T(8,128)(2,1)S(1)} collective-permute-done((bf16[128,1024]{1,0:T(8,128)(2,1)}, bf16[128,1024]{1,0:T(8,128)(2,1)S(1)}, u32[]{:S(2)}, u32[]{:S(2)}) %collective-permute-start.39) | collective-permute-done | bytes 262176 | tf_op jit(solution)/shard_map/ppermute | solution.py:388
  252.4 8.8 %collective-permute-done.40.refs_2_ = bf16[128,1024]{1,0:T(8,128)(2,1)S(1)} collective-permute-done((bf16[128,1024]{1,0:T(8,128)(2,1)}, bf16[128,1024]{1,0:T(8,128)(2,1)S(1)}, u32[]{:S(2)}, u32[]{:S(2)}) %collective-permute-start.40) | collective-permute-done | bytes 262176 | tf_op jit(solution)/shard_map/ppermute | solution.py:388
  265.9 5.3 %collective-permute-start.47 = (f32[18,128]{1,0:T(8,128)S(1)}, f32[18,128]{1,0:T(8,128)S(1)}, u32[]{:S(2)}, u32[]{:S(2)}) collective-permute-start(f32[18,128]{1,0:T(8,128)S(1)} %slice.136), channel_id=1, source_target_pairs={{0,1},{1,0},{2,3},{3,2},{4,5},{5,4},{6,7},{7,6},{8,9},{9,8},{10,11... | collective-permute-start | bytes 27656 | tf_op jit(solution)/shard_map/ppermute | solution.py:388
  (257 shorter events, 108.9 us)
Async XLA Ops:
  7.2 119.3 %all-gather.3.cloned.1.call-start = ((), (), s32[]{:S(2)}) async-start(), calls=%async_computation.2 | async-start | bytes 14155776 | tf_op jit(solution)/shard_map/all_gather | solution.py:581
  10.0 268.6 %reduce-scatter.2.cloned.1.call-start = ((), (), s32[]{:S(2)}) async-start(), calls=%async_computation.1 | async-start | bytes 14155776 | tf_op jit(solution)/shard_map/reduce_scatter | solution.py:626
  16.5 25.8 %collective-permute-start.10 = (bf16[128,1024]{1,0:T(8,128)(2,1)S(1)}, bf16[128,1024]{1,0:T(8,128)(2,1)S(1)}, u32[]{:S(2)}, u32[]{:S(2)}) collective-permute-start(bf16[128,1024]{1,0:T(8,128)(2,1)S(1)} %bitcast.75), channel_id=1, source_target_pairs={{0,1},{1,0},{2,3},{3,2},{4,5},{5,4},{6,7},{7,6},{8,9},{9,8},{10,11... | collective-permute-start | bytes 786440 | tf_op jit(solution)/shard_map/ppermute | solution.py:388
  17.4 25.0 %collective-permute-start.11 = (bf16[128,1024]{1,0:T(8,128)(2,1)S(1)}, bf16[128,1024]{1,0:T(8,128)(2,1)S(1)}, u32[]{:S(2)}, u32[]{:S(2)}) collective-permute-start(bf16[128,1024]{1,0:T(8,128)(2,1)S(1)} %bitcast.76), channel_id=1, source_target_pairs={{0,2},{1,3},{2,0},{3,1},{4,6},{5,7},{6,4},{7,5},{8,10},{9,11},{10,... | collective-permute-start | bytes 786440 | tf_op jit(solution)/shard_map/ppermute | solution.py:388
  47.7 16.9 %collective-permute-start.13 = (bf16[512,256]{1,0:T(8,128)(2,1)}, bf16[512,256]{1,0:T(8,128)(2,1)S(1)}, u32[]{:S(2)}, u32[]{:S(2)}) collective-permute-start(bf16[512,256]{1,0:T(8,128)(2,1)} %get-tuple-element.70.refs_0_.kv), channel_id=1, source_target_pairs={{0,4},{4,0},{1,5},{5,1},{2,6},{6,2},{3,7},{7,3},{8,12},{12,8},{9,1... | collective-permute-start | bytes 786440 | tf_op jit(solution)/shard_map/ppermute | solution.py:411
  62.3 18.7 %collective-permute-start.18 = (bf16[128,1024]{1,0:T(8,128)(2,1)S(1)}, bf16[128,1024]{1,0:T(8,128)(2,1)S(1)}, u32[]{:S(2)}, u32[]{:S(2)}) collective-permute-start(bf16[128,1024]{1,0:T(8,128)(2,1)S(1)} %bitcast.82), channel_id=1, source_target_pairs={{0,2},{1,3},{2,0},{3,1},{4,6},{5,7},{6,4},{7,5},{8,10},{9,11},{10,... | collective-permute-start | bytes 786440 | tf_op jit(solution)/shard_map/ppermute | solution.py:388
  62.9 18.2 %collective-permute-start.19 = (bf16[128,1024]{1,0:T(8,128)(2,1)S(1)}, bf16[128,1024]{1,0:T(8,128)(2,1)S(1)}, u32[]{:S(2)}, u32[]{:S(2)}) collective-permute-start(bf16[128,1024]{1,0:T(8,128)(2,1)S(1)} %bitcast.83), channel_id=1, source_target_pairs={{0,3},{1,2},{2,1},{3,0},{4,7},{5,6},{6,5},{7,4},{8,11},{9,10},{10,... | collective-permute-start | bytes 786440 | tf_op jit(solution)/shard_map/ppermute | solution.py:388
  64.6 23.5 %collective-permute-start.14 = (bf16[128,1024]{1,0:T(8,128)(2,1)S(1)}, bf16[128,1024]{1,0:T(8,128)(2,1)S(1)}, u32[]{:S(2)}, u32[]{:S(2)}) collective-permute-start(bf16[128,1024]{1,0:T(8,128)(2,1)S(1)} %pad_maximum_fusion.3), channel_id=1, source_target_pairs={{0,4},{4,0},{1,5},{5,1},{2,6},{6,2},{3,7},{7,3},{8,12},{12,8},{9,1... | collective-permute-start | bytes 786440 | tf_op jit(solution)/shard_map/ppermute | solution.py:411
  64.9 24.7 %collective-permute-start.15 = (bf16[128,1024]{1,0:T(8,128)(2,1)S(1)}, bf16[128,1024]{1,0:T(8,128)(2,1)S(1)}, u32[]{:S(2)}, u32[]{:S(2)}) collective-permute-start(bf16[128,1024]{1,0:T(8,128)(2,1)S(1)} %pad_maximum_fusion.3), channel_id=1, source_target_pairs={{0,16},{8,24},{16,0},{24,8},{1,17},{9,25},{17,1},{25,9},{2,18},{10... | collective-permute-start | bytes 786440 | tf_op jit(solution)/shard_map/ppermute | solution.py:419
  66.0 23.6 %collective-permute-start.16 = (bf16[128,1024]{1,0:T(8,128)(2,1)S(1)}, bf16[128,1024]{1,0:T(8,128)(2,1)S(1)}, u32[]{:S(2)}, u32[]{:S(2)}) collective-permute-start(bf16[128,1024]{1,0:T(8,128)(2,1)S(1)} %pad_maximum_fusion.3), channel_id=1, source_target_pairs={{0,20},{4,16},{8,28},{12,24},{16,4},{20,0},{24,12},{28,8},{1,21},{... | collective-permute-start | bytes 786440 | tf_op jit(solution)/shard_map/ppermute | solution.py:423
  104.9 21.5 %collective-permute-start.25 = (bf16[128,1024]{1,0:T(8,128)(2,1)}, bf16[128,1024]{1,0:T(8,128)(2,1)S(1)}, u32[]{:S(2)}, u32[]{:S(2)}) collective-permute-start(bf16[128,1024]{1,0:T(8,128)(2,1)} %get-tuple-element.83.refs_0_), channel_id=1, source_target_pairs={{0,2},{1,3},{2,0},{3,1},{4,6},{5,7},{6,4},{7,5},{8,10},{9,11},{10,... | collective-permute-start | bytes 786440 | tf_op jit(solution)/shard_map/ppermute | solution.py:388
  106.3 20.2 %collective-permute-start.26 = (bf16[128,1024]{1,0:T(8,128)(2,1)}, bf16[128,1024]{1,0:T(8,128)(2,1)S(1)}, u32[]{:S(2)}, u32[]{:S(2)}) collective-permute-start(bf16[128,1024]{1,0:T(8,128)(2,1)} %get-tuple-element.83.refs_0_), channel_id=1, source_target_pairs={{0,3},{1,2},{2,1},{3,0},{4,7},{5,6},{6,5},{7,4},{8,11},{9,10},{10,... | collective-permute-start | bytes 786440 | tf_op jit(solution)/shard_map/ppermute | solution.py:388
  147.6 23.0 %collective-permute-start.27 = (bf16[128,1024]{1,0:T(8,128)(2,1)}, bf16[128,1024]{1,0:T(8,128)(2,1)S(1)}, u32[]{:S(2)}, u32[]{:S(2)}) collective-permute-start(bf16[128,1024]{1,0:T(8,128)(2,1)} %get-tuple-element.92), channel_id=1, source_target_pairs={{0,1},{1,0},{2,3},{3,2},{4,5},{5,4},{6,7},{7,6},{8,9},{9,8},{10,11... | collective-permute-start | bytes 786440 | tf_op jit(solution)/shard_map/ppermute | solution.py:388
  152.7 21.5 %collective-permute-start.28 = (bf16[128,1024]{1,0:T(8,128)(2,1)}, bf16[128,1024]{1,0:T(8,128)(2,1)S(1)}, u32[]{:S(2)}, u32[]{:S(2)}) collective-permute-start(bf16[128,1024]{1,0:T(8,128)(2,1)} %get-tuple-element.93), channel_id=1, source_target_pairs={{0,2},{1,3},{2,0},{3,1},{4,6},{5,7},{6,4},{7,5},{8,10},{9,11},{10,... | collective-permute-start | bytes 786440 | tf_op jit(solution)/shard_map/ppermute | solution.py:388
  153.4 20.8 %collective-permute-start.29 = (bf16[128,1024]{1,0:T(8,128)(2,1)}, bf16[128,1024]{1,0:T(8,128)(2,1)S(1)}, u32[]{:S(2)}, u32[]{:S(2)}) collective-permute-start(bf16[128,1024]{1,0:T(8,128)(2,1)} %get-tuple-element.94), channel_id=1, source_target_pairs={{0,3},{1,2},{2,1},{3,0},{4,7},{5,6},{6,5},{7,4},{8,11},{9,10},{10,... | collective-permute-start | bytes 786440 | tf_op jit(solution)/shard_map/ppermute | solution.py:388
  191.1 22.5 %collective-permute-start.37 = (bf16[128,1024]{1,0:T(8,128)(2,1)}, bf16[128,1024]{1,0:T(8,128)(2,1)S(1)}, u32[]{:S(2)}, u32[]{:S(2)}) collective-permute-start(bf16[128,1024]{1,0:T(8,128)(2,1)} %get-tuple-element.108.refs_0_), channel_id=1, source_target_pairs={{0,2},{1,3},{2,0},{3,1},{4,6},{5,7},{6,4},{7,5},{8,10},{9,11},{10,... | collective-permute-start | bytes 786440 | tf_op jit(solution)/shard_map/ppermute | solution.py:388
  200.2 19.3 %collective-permute-start.33 = (bf16[128,1024]{1,0:T(8,128)(2,1)S(1)}, bf16[128,1024]{1,0:T(8,128)(2,1)S(1)}, u32[]{:S(2)}, u32[]{:S(2)}) collective-permute-start(bf16[128,1024]{1,0:T(8,128)(2,1)S(1)} %copy-done.48), channel_id=1, source_target_pairs={{0,1},{1,0},{2,3},{3,2},{4,5},{5,4},{6,7},{7,6},{8,9},{9,8},{10,11... | collective-permute-start | bytes 786440 | tf_op jit(solution)/shard_map/ppermute | solution.py:388
  201.0 21.1 %collective-permute-start.34 = (bf16[128,1024]{1,0:T(8,128)(2,1)S(1)}, bf16[128,1024]{1,0:T(8,128)(2,1)S(1)}, u32[]{:S(2)}, u32[]{:S(2)}) collective-permute-start(bf16[128,1024]{1,0:T(8,128)(2,1)S(1)} %copy-done.47), channel_id=1, source_target_pairs={{0,2},{1,3},{2,0},{3,1},{4,6},{5,7},{6,4},{7,5},{8,10},{9,11},{10,... | collective-permute-start | bytes 786440 | tf_op jit(solution)/shard_map/ppermute | solution.py:388
  205.9 19.2 %collective-permute-start.42 = (bf16[128,1024]{1,0:T(8,128)(2,1)S(1)}, bf16[128,1024]{1,0:T(8,128)(2,1)S(1)}, u32[]{:S(2)}, u32[]{:S(2)}) collective-permute-start(bf16[128,1024]{1,0:T(8,128)(2,1)S(1)} %collective-permute-done.36.refs_1_), channel_id=1, source_target_pairs={{0,2},{1,3},{2,0},{3,1},{4,6},{5,7},{6,4},{7,5},{8,10},{9,11},{10,... | collective-permute-start | bytes 786440 | tf_op jit(solution)/shard_map/ppermute | solution.py:388
  232.7 17.4 %collective-permute-start.39 = (bf16[128,1024]{1,0:T(8,128)(2,1)}, bf16[128,1024]{1,0:T(8,128)(2,1)S(1)}, u32[]{:S(2)}, u32[]{:S(2)}) collective-permute-start(bf16[128,1024]{1,0:T(8,128)(2,1)} %get-tuple-element.113), channel_id=1, source_target_pairs={{0,1},{1,0},{2,3},{3,2},{4,5},{5,4},{6,7},{7,6},{8,9},{9,8},{10,11... | collective-permute-start | bytes 786440 | tf_op jit(solution)/shard_map/ppermute | solution.py:388
  232.7 28.5 %collective-permute-start.40 = (bf16[128,1024]{1,0:T(8,128)(2,1)}, bf16[128,1024]{1,0:T(8,128)(2,1)S(1)}, u32[]{:S(2)}, u32[]{:S(2)}) collective-permute-start(bf16[128,1024]{1,0:T(8,128)(2,1)} %get-tuple-element.114), channel_id=1, source_target_pairs={{0,2},{1,3},{2,0},{3,1},{4,6},{5,7},{6,4},{7,5},{8,10},{9,11},{10,... | collective-permute-start | bytes 786440 | tf_op jit(solution)/shard_map/ppermute | solution.py:388
  235.1 26.1 %collective-permute-start.41 = (bf16[128,1024]{1,0:T(8,128)(2,1)}, bf16[128,1024]{1,0:T(8,128)(2,1)S(1)}, u32[]{:S(2)}, u32[]{:S(2)}) collective-permute-start(bf16[128,1024]{1,0:T(8,128)(2,1)} %get-tuple-element.115), channel_id=1, source_target_pairs={{0,3},{1,2},{2,1},{3,0},{4,7},{5,6},{6,5},{7,4},{8,11},{9,10},{10,... | collective-permute-start | bytes 786440 | tf_op jit(solution)/shard_map/ppermute | solution.py:388
  238.5 26.0 %collective-permute-start.44 = (bf16[160,768]{1,0:T(8,128)(2,1)S(1)}, bf16[160,768]{1,0:T(8,128)(2,1)S(1)}, u32[]{:S(2)}, u32[]{:S(2)}) collective-permute-start(bf16[160,768]{1,0:T(8,128)(2,1)S(1)} %get-tuple-element.126), channel_id=1, source_target_pairs={{0,4},{4,0},{1,5},{5,1},{2,6},{6,2},{3,7},{7,3},{8,12},{12,8},{9,1... | collective-permute-start | bytes 737288 | tf_op jit(solution)/shard_map/ppermute | solution.py:411
  241.8 22.7 %collective-permute-start.45 = (bf16[160,768]{1,0:T(8,128)(2,1)S(1)}, bf16[160,768]{1,0:T(8,128)(2,1)S(1)}, u32[]{:S(2)}, u32[]{:S(2)}) collective-permute-start(bf16[160,768]{1,0:T(8,128)(2,1)S(1)} %get-tuple-element.128), channel_id=1, source_target_pairs={{0,16},{8,24},{16,0},{24,8},{1,17},{9,25},{17,1},{25,9},{2,18},{10... | collective-permute-start | bytes 737288 | tf_op jit(solution)/shard_map/ppermute | solution.py:419
  (82 other events, 650.3 us)
Sparse Core Ops, SparseCore 0:
  10.1 93.3 all-gather.2
  174.4 100.0 reduce-scatter.1

commit v5 on v4

--- a/solution.py
+++ b/solution.py
@@ -12,6 +12,7 @@
 E = 16
 PIECE = 256
 CAP = 320
+COST = 10**10
 EPS = 1e-06
 FILL = -1e30
 EXPERTS_PER_STEP = 4
@@ -220,8 +221,10 @@
     return jnp.sum(jnp.where(lane == index, table, 0.0), axis=1, keepdims=True)
 
 
-def expert_kernel(n, chosen, kept, router, ws, *refs):
+def expert_kernel(n, second, chosen, kept, router, ws, *refs):
     xs, cs, refs = refs[:n], refs[n : 2 * n], refs[2 * n :]
+    if second:
+        router_before, refs = refs[0], refs[4:]
     outs, (active_out, gate_out, up_out, router_grad) = refs[:n], refs[n : n + 4]
     x, c, w, total, soft, share = refs[n + 4 :]
     step, steps = pl.program_id(0), pl.num_programs(0)
@@ -284,7 +287,8 @@
         for j in range(n):
             outs[j][...] = value[j * m : (j + 1) * m, :].astype(bf16)
         across_rows = (((0,), (0,)), ((), ()))
-        router_grad[...] = dot(high, x[...], across_rows) + dot(low, x[...], across_rows)
+        value = dot(high, x[...], across_rows) + dot(low, x[...], across_rows)
+        router_grad[...] = value + router_before[...] if second else value
 
 
 def expert_back_kernel(n, active, gate, up, ws, *refs):
@@ -583,25 +587,45 @@
     steps = E // eb
     block = pl.BlockSpec((count, eb * fe), lambda s: (0, s))
     wide_out = sds((count, E * fe), bf16)
-    got = pl.pallas_call(
-        functools.partial(expert_kernel, n),
-        out_shape=tuple([sds((m, d), bf16)] * n) + (wide_out, wide_out, wide_out, sds((E, d), f32)),
-        grid=(steps,),
-        in_specs=[full((count, E)), full((count, E)), full((d, E))]
-        + [pl.BlockSpec((n_p, 3, eb, rows, fe), lambda s: (0, 0, s, 0, 0))]
-        + [full((m, d))] * (2 * n),
-        out_specs=[full((m, d))] * n + [block] * 3 + [full((E, d))],
-        scratch_shapes=[
-            pltpu.VMEM((count, d), bf16),
-            pltpu.VMEM((count, d), bf16),
-            pltpu.VMEM((d, 3 * eb * fe), bf16),
-            pltpu.VMEM((count, d), f32),
-            pltpu.VMEM((count, E), f32),
-            pltpu.VMEM((count, E), f32),
-        ],
-        cost_estimate=pl.CostEstimate(flops=0, bytes_accessed=0, transcendentals=0),
-    )(chosen, kept, router_all, ws, *seconds, *cots)
-    second_parts, (active, gate_g, up_g, router_part) = got[:n], got[n:]
+    def expert_call(at, parts, begun):
+        tall = m * parts
+        return pl.pallas_call(
+            functools.partial(expert_kernel, parts, bool(begun)),
+            out_shape=tuple([sds((m, d), bf16)] * parts) + (wide_out, wide_out, wide_out, sds((E, d), f32)),
+            grid=(steps,),
+            in_specs=[full((tall, E)), full((tall, E)), full((d, E))]
+            + [pl.BlockSpec((n_p, 3, eb, rows, fe), lambda s: (0, 0, s, 0, 0))]
+            + [full((m, d))] * (2 * parts)
+            + ([full((E, d))] + [pl.BlockSpec(memory_space=pl.ANY)] * 3 if begun else []),
+            out_specs=[full((m, d))] * parts
+            + [pl.BlockSpec((tall, eb * fe), lambda s: (at // parts, s))] * 3
+            + [full((E, d))],
+            scratch_shapes=[
+                pltpu.VMEM((tall, d), bf16),
+                pltpu.VMEM((tall, d), bf16),
+                pltpu.VMEM((d, 3 * eb * fe), bf16),
+                pltpu.VMEM((tall, d), f32),
+                pltpu.VMEM((tall, E), f32),
+                pltpu.VMEM((tall, E), f32),
+            ],
+            input_output_aliases={5 + 2 * parts + i: parts + i for i in range(3)} if begun else {},
+            cost_estimate=pl.CostEstimate(flops=0 if begun else COST, bytes_accessed=0, transcendentals=0),
+        )(
+            chosen[at * m : at * m + tall],
+            kept[at * m : at * m + tall],
+            router_all,
+            ws,
+            *seconds[at : at + parts],
+            *cots[at : at + parts],
+            *begun,
+        )
+
+    split = n // 2 if n % 2 == 0 else n
+    got = expert_call(0, split, ())
+    second_parts, (active, gate_g, up_g, router_part) = got[:split], got[split:]
+    if split < n:
+        got = expert_call(split, split, (router_part, active, gate_g, up_g))
+        second_parts, (active, gate_g, up_g, router_part) = (*second_parts, *got[:split]), got[split:]
     half_p = n_p // 2
     got = pl.pallas_call(
         functools.partial(expert_back_kernel, n),

time: 289 us -> 282 us (0.976)
  waiting for transfers between devices: 86.8 us -> 73.1 us
  Pallas kernels: 86.6 us -> 91.4 us
    ppermute x36, waiting for transfers between devices: 73.3 us -> 58 us  [across(): lax.ppermute(v, 'tensor', [(i, i ^ j) for i in range(lax.axis_size('tenso...]
    pallas_call x1 -> x2, Pallas kernels: 20.4 us -> 25.6 us  [expert_call(): pl.pallas_call(functools.partial(expert_kernel, parts, bool(begun)), out_...]
    unnamed x110 -> x106, local copies, waits for them, and re-layouts: 6.47 us -> 6.7 us
  transfers between devices with their start and end apart: 52 -> 52, of which waited for: 24 -> 21; matrix products, arithmetic and copies ran while one was open for 5% -> 5% of each run, Pallas kernels for 23% -> 28%
where the time goes in v5:
time: 282 us; the launch traced here: 281 us
  Pallas kernels  91.4 us (32%)
  starting transfers between devices  75.6 us (27%)
  waiting for transfers between devices  73.1 us (26%)
  between operations  14.7 us (5%)
  local copies, waits for them, and re-layouts  13.1 us (5%)
  other arithmetic  13 us (5%)
    ppermute x36, starting transfers between devices, across(): lax.ppermute(v, 'tensor', [(i, i ^ j) for i in range(lax.axis_size('tenso...  64.8 us
    ppermute x36, waiting for transfers between devices, across(): lax.ppermute(v, 'tensor', [(i, i ^ j) for i in range(lax.axis_size('tenso...  58 us
    pallas_call x10, Pallas kernels, whole_call(): pl.pallas_call(body, out_shape=outs, grid_spec=pltpu.PrefetchScalarGridSp...  50.4 us
    pallas_call x2, Pallas kernels, expert_call(): pl.pallas_call(functools.partial(expert_kernel, parts, bool(begun)), out_...  25.6 us
    pallas_call x1, Pallas kernels, per_device(): pl.pallas_call(functools.partial(expert_back_kernel, n), out_shape=tuple(...  15.4 us
    unnamed x106, local copies, waits for them, and re-layouts  6.7 us
    ppermute x3, waiting for transfers between devices, swap_xy(): return lax.ppermute(v, ('dp', 'seq'), [(i, i ^ 5) for i in range(8)])  6.53 us
    ppermute x5, starting transfers between devices, swap_x(): return lax.ppermute(v, 'seq', [(0, 1), (1, 0)])  5.74 us
  transfers between devices with their start and end apart: 52, of which 21 were waited for; matrix products, arithmetic and copies ran while one was open for 5% of the time, Pallas kernels for 28%

profile of v5, /device:TPU:0, one launch (start us, length us, event | category | flops | bytes accessed | tf_op | source)
XLA Modules:
  0.0 281.3 jit_solution(17840458873002841668)
XLA Ops:
  26.3 5.2 %collective-permute-done.3 = bf16[144,512]{1,0:T(8,128)(2,1)S(1)} collective-permute-done((bf16[144,512]{1,0:T(8,128)(2,1)S(1)}, bf16[144,512]{1,0:T(8,128)(2,1)S(1)}, u32[]{:S(2)}, u32[]{:S(2)}) %collective-permute-start.3) | collective-permute-done | bytes 147488 | tf_op jit(solution)/shard_map/ppermute | solution.py:415
  41.8 4.5 %shard_map.247 = (bf16[512,1024]{1,0:T(8,128)(2,1)}, bf16[512,256]{1,0:T(8,128)(2,1)}, bf16[512,256]{1,0:T(8,128)(2,1)}) custom-call(s32[8]{0:T(128)} %copy-done.36, bf16[128,1024]{1,0:T(8,128)(2,1)} %bitcast.72, bf16[128,1024]{1,0:T(8,128)(2,1)} %copy-done.10, bf16[128,1024]{1,0:T(8,128)(2,1)} %copy-done.11, bf16[128,1024]{1,0:T(8,128)(2,1)} %copy-done.12, ...), custom_call_target="tpu_custom_call" | custom-call | tf_op jit(solution)/shard_map/pallas_call | solution.py:39
  54.8 6.1 %collective-permute-done.7 = bf16[128,256]{1,0:T(8,128)(2,1)S(1)} collective-permute-done((bf16[128,256]{1,0:T(8,128)(2,1)S(1)}, bf16[128,256]{1,0:T(8,128)(2,1)S(1)}, u32[]{:S(2)}, u32[]{:S(2)}) %collective-permute-start.7) | collective-permute-done | bytes 65568 | tf_op jit(solution)/shard_map/ppermute | solution.py:392
  66.7 8.8 %shard_map.248 = (bf16[128,256]{1,0:T(8,128)(2,1)}, bf16[128,256]{1,0:T(8,128)(2,1)}, bf16[128,256]{1,0:T(8,128)(2,1)}, bf16[128,256]{1,0:T(8,128)(2,1)}, f32[4,64,512]{2,1,0:T(8,128)}, /*index=5*/f32[4,1,512]{2,1,0:T(1,128)}) custom-call(bf16[512,256]{1,0:T(8,128)(2,1)} %get-tuple-element.76.q, s32[1,512]{1,0:T(1,128)} %max.10.lim, ...), custom_call_target="tpu_custom_call" | custom-call | flops 10000000000 | tf_op jit(solution)/shard_map/pallas_call | solution.py:39
  79.1 6.1 %collective-permute-start.20 = (bf16[128,256]{1,0:T(8,128)(2,1)}, bf16[128,256]{1,0:T(8,128)(2,1)S(1)}, u32[]{:S(2)}, u32[]{:S(2)}) collective-permute-start(bf16[128,256]{1,0:T(8,128)(2,1)} %get-tuple-element.82.refs_5_), channel_id=1, source_target_pairs={{0,1},{1,0},{2,3},{3,2},{4,5},{5,4},{6,7},{7,6},{8,9},{9,8},{10,11... | collective-permute-start | bytes 196616 | tf_op jit(solution)/shard_map/ppermute | solution.py:392
  89.4 4.2 %collective-permute-done.21.refs_2_ = bf16[128,256]{1,0:T(8,128)(2,1)S(1)} collective-permute-done((bf16[128,256]{1,0:T(8,128)(2,1)}, bf16[128,256]{1,0:T(8,128)(2,1)S(1)}, u32[]{:S(2)}, u32[]{:S(2)}) %collective-permute-start.21) | collective-permute-done | bytes 65568 | tf_op jit(solution)/shard_map/ppermute | solution.py:392
  97.3 4.1 %shard_map.249 = (f32[128,1024]{1,0:T(8,128)}, bf16[128,1024]{1,0:T(8,128)(2,1)}) custom-call(s32[8]{0:T(128)} %copy-done.36, bf16[128,1024]{1,0:T(8,128)(2,1)} %bitcast.73, f32[1,1024]{1,0:T(1,128)} %reshape.269.gain, bf16[4,128,1024]{2,1,0:T(8,128)(2,1)} %copy-done, bf16[4,128,1024]{2,1,0:T(8,128)(2,1)} %copy-done.2, ...), custom_call_target="tpu_custom_call" | custom-call | tf_op jit(solution)/shard_map/pallas_call | solution.py:39
  108.0 5.4 %collective-permute-done.26.refs_1_ = bf16[128,1024]{1,0:T(8,128)(2,1)S(1)} collective-permute-done((bf16[128,1024]{1,0:T(8,128)(2,1)}, bf16[128,1024]{1,0:T(8,128)(2,1)S(1)}, u32[]{:S(2)}, u32[]{:S(2)}) %collective-permute-start.26) | collective-permute-done | bytes 262176 | tf_op jit(solution)/shard_map/ppermute | solution.py:392
  114.1 12.8 %shard_map.250 = (bf16[128,1024]{1,0:T(8,128)(2,1)}, bf16[128,1024]{1,0:T(8,128)(2,1)}, bf16[512,2048]{1,0:T(8,128)(2,1)}, bf16[512,2048]{1,0:T(8,128)(2,1)}, bf...) custom-call(f32[256,16]{1,0:T(8,128)} %get-tuple-element.145.chosen, f32[256,16]{1,0:T(8,128)} %get-tuple-element.144.kept, ...), custom_call_target="tpu_custom_call" | custom-call | flops 10000000000 | tf_op jit(solution)/shard_map/pallas_call | solution.py:592
  127.6 12.8 %shard_map.251 = (bf16[128,1024]{1,0:T(8,128)(2,1)}, bf16[128,1024]{1,0:T(8,128)(2,1)}, bf16[512,2048]{1,0:T(8,128)(2,1)}, bf16[512,2048]{1,0:T(8,128)(2,1)}, bf...) custom-call(f32[256,16]{1,0:T(8,128)} %get-tuple-element.147.chosen, ...), custom_call_target="tpu_custom_call", output_to_operand_aliasing={{2}: (9, {}), {3}: (10, {}), {4}: (11, {})} | custom-call | tf_op jit(solution)/shard_map/pallas_call | solution.py:592
  140.5 5.4 %collective-permute-start.28 = (bf16[128,1024]{1,0:T(8,128)(2,1)}, bf16[128,1024]{1,0:T(8,128)(2,1)S(1)}, u32[]{:S(2)}, u32[]{:S(2)}) collective-permute-start(bf16[128,1024]{1,0:T(8,128)(2,1)} %get-tuple-element.101), channel_id=1, source_target_pairs={{0,2},{1,3},{2,0},{3,1},{4,6},{5,7},{6,4},{7,5},{8,10},{9,11},{10,... | collective-permute-start | bytes 786440 | tf_op jit(solution)/shard_map/ppermute | solution.py:392
  147.4 15.4 %shard_map.252 = (bf16[128,1024]{1,0:T(8,128)(2,1)}, bf16[128,1024]{1,0:T(8,128)(2,1)}, bf16[128,1024]{1,0:T(8,128)(2,1)}, bf16[128,1024]{1,0:T(8,128)(2,1)}, bf16[8,3,16,128,128]{4,3,2,1,0:T(8,128)(2,1)}) custom-call(bf16[512,2048]{1,0:T(8,128)(2,1)} %get-tuple-element.92.active, bf16[512,2048]{1,0:T(8,128)(2,1)} %get-tuple-element.93.gate, ...), custom_call_target="tpu_custom_call" | custom-call | tf_op jit(solution)/shard_map/pallas_call | solution.py:630
  165.1 4.2 %shard_map.253 = (f32[128,1024]{1,0:T(8,128)}, bf16[128,1024]{1,0:T(8,128)(2,1)}, f32[1,1024]{1,0:T(1,128)}, bf16[128,256]{1,0:T(8,128)(2,1)}, bf16[128,256]{1,0...) custom-call(s32[8]{0:T(128)} %copy-done.36, f32[128,1024]{1,0:T(8,128)} %get-tuple-element.86.middle, ...), custom_call_target="tpu_custom_call" | custom-call | tf_op jit(solution)/shard_map/pallas_call | solution.py:39
  169.4 4.8 %collective-permute-start.30 = (bf16[128,256]{1,0:T(8,128)(2,1)}, bf16[128,256]{1,0:T(8,128)(2,1)S(1)}, u32[]{:S(2)}, u32[]{:S(2)}) collective-permute-start(bf16[128,256]{1,0:T(8,128)(2,1)} %get-tuple-element.104), channel_id=1, source_target_pairs={{0,1},{1,0},{2,3},{3,2},{4,5},{5,4},{6,7},{7,6},{8,9},{9,8},{10,11... | collective-permute-start | bytes 196616 | tf_op jit(solution)/shard_map/ppermute | solution.py:392
  176.9 4.2 %collective-permute-done.31.refs_2_ = bf16[128,256]{1,0:T(8,128)(2,1)S(1)} collective-permute-done((bf16[128,256]{1,0:T(8,128)(2,1)}, bf16[128,256]{1,0:T(8,128)(2,1)S(1)}, u32[]{:S(2)}, u32[]{:S(2)}) %collective-permute-start.31) | collective-permute-done | bytes 65568 | tf_op jit(solution)/shard_map/ppermute | solution.py:392
  183.5 6.9 %shard_map.255 = (bf16[512,256]{1,0:T(8,128)(2,1)}, f32[4,64,512]{2,1,0:T(8,128)}) custom-call(bf16[512,256]{1,0:T(8,128)(2,1)} %get-tuple-element.76.q, s32[1,512]{1,0:T(1,128)} %max.10.lim, bf16[512,256]{1,0:T(8,128)(2,1)} %copy-done.42, s32[512,1]{1,0:T(8,128)} %broadcast_add_fusion.refs_3_.kpos, f32[4,1,512]{2,1,0:T(1,128)} %get-tuple-element.111.lse, ...), custom_call_target="tpu_custom_call" | custom-call | flops 10000000000 | tf_op jit(solution)/shard_map/pallas_call | solution.py:39
  195.5 7.5 %shard_map.256 = (f32[512,256]{1,0:T(8,128)}, bf16[512,256]{1,0:T(8,128)(2,1)}) custom-call(bf16[512,256]{1,0:T(8,128)(2,1)} %get-tuple-element.76.q, s32[1,512]{1,0:T(1,128)} %max.10.lim, bf16[512,256]{1,0:T(8,128)(2,1)} %get-tuple-element.74.refs_0_.kv, s32[512,1]{1,0:T(8,128)} %copy-done.13, f32[4,1,512]{2,1,0:T(1,128)} %get-tuple-element.111.lse, ...), custom_call_target="tpu_custom_call" | custom-call | flops 10000000000 | tf_op jit(solution)/shard_map/pallas_call | solution.py:39
  203.8 4.7 %shard_map.257 = (bf16[128,1024]{1,0:T(8,128)(2,1)}, bf16[128,1024]{1,0:T(8,128)(2,1)}, bf16[128,1024]{1,0:T(8,128)(2,1)}, bf16[128,1024]{1,0:T(8,128)(2,1)}, bf...) custom-call(s32[8]{0:T(128)} %copy-done.36, bf16[512,256]{1,0:T(8,128)(2,1)} %get-tuple-element.117.dq, ...), custom_call_target="tpu_custom_call" | custom-call | tf_op jit(solution)/shard_map/pallas_call | solution.py:39
  208.5 5.2 %collective-permute-done.34.refs_2_ = bf16[128,1024]{1,0:T(8,128)(2,1)S(1)} collective-permute-done((bf16[128,1024]{1,0:T(8,128)(2,1)S(1)}, bf16[128,1024]{1,0:T(8,128)(2,1)S(1)}, u32[]{:S(2)}, u32[]{:S(2)}) %collective-permute-start.34) | collective-permute-done | bytes 262176 | tf_op jit(solution)/shard_map/ppermute | solution.py:392
  213.7 4.6 %collective-permute-done.42.refs_3_ = bf16[128,1024]{1,0:T(8,128)(2,1)S(1)} collective-permute-done((bf16[128,1024]{1,0:T(8,128)(2,1)S(1)}, bf16[128,1024]{1,0:T(8,128)(2,1)S(1)}, u32[]{:S(2)}, u32[]{:S(2)}) %collective-permute-start.42) | collective-permute-done | bytes 262176 | tf_op jit(solution)/shard_map/ppermute | solution.py:392
  219.0 4.8 %shard_map.259 = (bf16[4,160,768]{2,1,0:T(8,128)(2,1)}, bf16[4,160,768]{2,1,0:T(8,128)(2,1)}) custom-call(s32[8]{0:T(128)} %copy-done.36, bf16[512,1024]{1,0:T(8,128)(2,1)} %get-tuple-element.124.x1, bf16[512,512]{1,0:T(8,128)(2,1)} %get-tuple-element.126.grads, f32[16,1024]{1,0:T(8,128)} %get-tuple-element.127.router_part, ...), custom_call_target="tpu_custom_call" | custom-call | tf_op jit(solution)/shard_map/pallas_call | solution.py:39
  234.9 8.5 %collective-permute-done.39.refs_1_ = bf16[128,1024]{1,0:T(8,128)(2,1)S(1)} collective-permute-done((bf16[128,1024]{1,0:T(8,128)(2,1)}, bf16[128,1024]{1,0:T(8,128)(2,1)S(1)}, u32[]{:S(2)}, u32[]{:S(2)}) %collective-permute-start.39) | collective-permute-done | bytes 262176 | tf_op jit(solution)/shard_map/ppermute | solution.py:392
  245.6 8.0 %collective-permute-done.40.refs_2_ = bf16[128,1024]{1,0:T(8,128)(2,1)S(1)} collective-permute-done((bf16[128,1024]{1,0:T(8,128)(2,1)}, bf16[128,1024]{1,0:T(8,128)(2,1)S(1)}, u32[]{:S(2)}, u32[]{:S(2)}) %collective-permute-start.40) | collective-permute-done | bytes 262176 | tf_op jit(solution)/shard_map/ppermute | solution.py:392
  259.1 4.6 %collective-permute-start.47 = (f32[18,128]{1,0:T(8,128)S(1)}, f32[18,128]{1,0:T(8,128)S(1)}, u32[]{:S(2)}, u32[]{:S(2)}) collective-permute-start(f32[18,128]{1,0:T(8,128)S(1)} %slice.152), channel_id=1, source_target_pairs={{0,1},{1,0},{2,3},{3,2},{4,5},{5,4},{6,7},{7,6},{8,9},{9,8},{10,11... | collective-permute-start | bytes 27656 | tf_op jit(solution)/shard_map/ppermute | solution.py:392
  (254 shorter events, 107.9 us)
Async XLA Ops:
  7.2 106.2 %all-gather.3.cloned.1.call-start = ((), (), s32[]{:S(2)}) async-start(), calls=%async_computation.2 | async-start | bytes 14155776 | tf_op jit(solution)/shard_map/all_gather | solution.py:585
  10.0 261.3 %reduce-scatter.2.cloned.1.call-start = ((), (), s32[]{:S(2)}) async-start(), calls=%async_computation.1 | async-start | bytes 14155776 | tf_op jit(solution)/shard_map/reduce_scatter | solution.py:650
  16.0 24.9 %collective-permute-start.10 = (bf16[128,1024]{1,0:T(8,128)(2,1)S(1)}, bf16[128,1024]{1,0:T(8,128)(2,1)S(1)}, u32[]{:S(2)}, u32[]{:S(2)}) collective-permute-start(bf16[128,1024]{1,0:T(8,128)(2,1)S(1)} %bitcast.76), channel_id=1, source_target_pairs={{0,1},{1,0},{2,3},{3,2},{4,5},{5,4},{6,7},{7,6},{8,9},{9,8},{10,11... | collective-permute-start | bytes 786440 | tf_op jit(solution)/shard_map/ppermute | solution.py:392
  16.9 24.0 %collective-permute-start.11 = (bf16[128,1024]{1,0:T(8,128)(2,1)S(1)}, bf16[128,1024]{1,0:T(8,128)(2,1)S(1)}, u32[]{:S(2)}, u32[]{:S(2)}) collective-permute-start(bf16[128,1024]{1,0:T(8,128)(2,1)S(1)} %bitcast.77), channel_id=1, source_target_pairs={{0,2},{1,3},{2,0},{3,1},{4,6},{5,7},{6,4},{7,5},{8,10},{9,11},{10,... | collective-permute-start | bytes 786440 | tf_op jit(solution)/shard_map/ppermute | solution.py:392
  46.3 16.9 %collective-permute-start.13 = (bf16[512,256]{1,0:T(8,128)(2,1)}, bf16[512,256]{1,0:T(8,128)(2,1)S(1)}, u32[]{:S(2)}, u32[]{:S(2)}) collective-permute-start(bf16[512,256]{1,0:T(8,128)(2,1)} %get-tuple-element.74.refs_0_.kv), channel_id=1, source_target_pairs={{0,4},{4,0},{1,5},{5,1},{2,6},{6,2},{3,7},{7,3},{8,12},{12,8},{9,1... | collective-permute-start | bytes 786440 | tf_op jit(solution)/shard_map/ppermute | solution.py:415
  48.3 17.0 %collective-permute-start.17 = (bf16[128,1024]{1,0:T(8,128)(2,1)S(1)}, bf16[128,1024]{1,0:T(8,128)(2,1)S(1)}, u32[]{:S(2)}, u32[]{:S(2)}) collective-permute-start(bf16[128,1024]{1,0:T(8,128)(2,1)S(1)} %bitcast.83), channel_id=1, source_target_pairs={{0,1},{1,0},{2,3},{3,2},{4,5},{5,4},{6,7},{7,6},{8,9},{9,8},{10,11... | collective-permute-start | bytes 786440 | tf_op jit(solution)/shard_map/ppermute | solution.py:392
  60.9 18.1 %collective-permute-start.18 = (bf16[128,1024]{1,0:T(8,128)(2,1)S(1)}, bf16[128,1024]{1,0:T(8,128)(2,1)S(1)}, u32[]{:S(2)}, u32[]{:S(2)}) collective-permute-start(bf16[128,1024]{1,0:T(8,128)(2,1)S(1)} %bitcast.84), channel_id=1, source_target_pairs={{0,2},{1,3},{2,0},{3,1},{4,6},{5,7},{6,4},{7,5},{8,10},{9,11},{10,... | collective-permute-start | bytes 786440 | tf_op jit(solution)/shard_map/ppermute | solution.py:392
  61.5 17.6 %collective-permute-start.19 = (bf16[128,1024]{1,0:T(8,128)(2,1)S(1)}, bf16[128,1024]{1,0:T(8,128)(2,1)S(1)}, u32[]{:S(2)}, u32[]{:S(2)}) collective-permute-start(bf16[128,1024]{1,0:T(8,128)(2,1)S(1)} %bitcast.85), channel_id=1, source_target_pairs={{0,3},{1,2},{2,1},{3,0},{4,7},{5,6},{6,5},{7,4},{8,11},{9,10},{10,... | collective-permute-start | bytes 786440 | tf_op jit(solution)/shard_map/ppermute | solution.py:392
  63.2 22.8 %collective-permute-start.14 = (bf16[128,1024]{1,0:T(8,128)(2,1)S(1)}, bf16[128,1024]{1,0:T(8,128)(2,1)S(1)}, u32[]{:S(2)}, u32[]{:S(2)}) collective-permute-start(bf16[128,1024]{1,0:T(8,128)(2,1)S(1)} %pad_maximum_fusion.3), channel_id=1, source_target_pairs={{0,4},{4,0},{1,5},{5,1},{2,6},{6,2},{3,7},{7,3},{8,12},{12,8},{9,1... | collective-permute-start | bytes 786440 | tf_op jit(solution)/shard_map/ppermute | solution.py:415
  63.8 23.7 %collective-permute-start.15 = (bf16[128,1024]{1,0:T(8,128)(2,1)S(1)}, bf16[128,1024]{1,0:T(8,128)(2,1)S(1)}, u32[]{:S(2)}, u32[]{:S(2)}) collective-permute-start(bf16[128,1024]{1,0:T(8,128)(2,1)S(1)} %pad_maximum_fusion.3), channel_id=1, source_target_pairs={{0,16},{8,24},{16,0},{24,8},{1,17},{9,25},{17,1},{25,9},{2,18},{10... | collective-permute-start | bytes 786440 | tf_op jit(solution)/shard_map/ppermute | solution.py:423
  65.3 23.9 %collective-permute-start.16 = (bf16[128,1024]{1,0:T(8,128)(2,1)S(1)}, bf16[128,1024]{1,0:T(8,128)(2,1)S(1)}, u32[]{:S(2)}, u32[]{:S(2)}) collective-permute-start(bf16[128,1024]{1,0:T(8,128)(2,1)S(1)} %pad_maximum_fusion.3), channel_id=1, source_target_pairs={{0,20},{4,16},{8,28},{12,24},{16,4},{20,0},{24,12},{28,8},{1,21},{... | collective-permute-start | bytes 786440 | tf_op jit(solution)/shard_map/ppermute | solution.py:427
  104.8 22.0 %collective-permute-start.24 = (bf16[128,1024]{1,0:T(8,128)(2,1)}, bf16[128,1024]{1,0:T(8,128)(2,1)S(1)}, u32[]{:S(2)}, u32[]{:S(2)}) collective-permute-start(bf16[128,1024]{1,0:T(8,128)(2,1)} %get-tuple-element.87.refs_0_), channel_id=1, source_target_pairs={{0,2},{1,3},{2,0},{3,1},{4,6},{5,7},{6,4},{7,5},{8,10},{9,11},{10,... | collective-permute-start | bytes 786440 | tf_op jit(solution)/shard_map/ppermute | solution.py:392
  106.4 20.5 %collective-permute-start.25 = (bf16[128,1024]{1,0:T(8,128)(2,1)}, bf16[128,1024]{1,0:T(8,128)(2,1)S(1)}, u32[]{:S(2)}, u32[]{:S(2)}) collective-permute-start(bf16[128,1024]{1,0:T(8,128)(2,1)} %get-tuple-element.87.refs_0_), channel_id=1, source_target_pairs={{0,3},{1,2},{2,1},{3,0},{4,7},{5,6},{6,5},{7,4},{8,11},{9,10},{10,... | collective-permute-start | bytes 786440 | tf_op jit(solution)/shard_map/ppermute | solution.py:392
  140.5 23.8 %collective-permute-start.28 = (bf16[128,1024]{1,0:T(8,128)(2,1)}, bf16[128,1024]{1,0:T(8,128)(2,1)S(1)}, u32[]{:S(2)}, u32[]{:S(2)}) collective-permute-start(bf16[128,1024]{1,0:T(8,128)(2,1)} %get-tuple-element.101), channel_id=1, source_target_pairs={{0,2},{1,3},{2,0},{3,1},{4,6},{5,7},{6,4},{7,5},{8,10},{9,11},{10,... | collective-permute-start | bytes 786440 | tf_op jit(solution)/shard_map/ppermute | solution.py:392
  145.8 18.4 %collective-permute-start.29 = (bf16[128,1024]{1,0:T(8,128)(2,1)}, bf16[128,1024]{1,0:T(8,128)(2,1)S(1)}, u32[]{:S(2)}, u32[]{:S(2)}) collective-permute-start(bf16[128,1024]{1,0:T(8,128)(2,1)} %get-tuple-element.102), channel_id=1, source_target_pairs={{0,3},{1,2},{2,1},{3,0},{4,7},{5,6},{6,5},{7,4},{8,11},{9,10},{10,... | collective-permute-start | bytes 786440 | tf_op jit(solution)/shard_map/ppermute | solution.py:392
  182.4 20.6 %collective-permute-start.37 = (bf16[128,1024]{1,0:T(8,128)(2,1)}, bf16[128,1024]{1,0:T(8,128)(2,1)S(1)}, u32[]{:S(2)}, u32[]{:S(2)}) collective-permute-start(bf16[128,1024]{1,0:T(8,128)(2,1)} %get-tuple-element.116.refs_0_), channel_id=1, source_target_pairs={{0,2},{1,3},{2,0},{3,1},{4,6},{5,7},{6,4},{7,5},{8,10},{9,11},{10,... | collective-permute-start | bytes 786440 | tf_op jit(solution)/shard_map/ppermute | solution.py:392
  191.3 17.2 %collective-permute-start.33 = (bf16[128,1024]{1,0:T(8,128)(2,1)S(1)}, bf16[128,1024]{1,0:T(8,128)(2,1)S(1)}, u32[]{:S(2)}, u32[]{:S(2)}) collective-permute-start(bf16[128,1024]{1,0:T(8,128)(2,1)S(1)} %copy-done.45), channel_id=1, source_target_pairs={{0,1},{1,0},{2,3},{3,2},{4,5},{5,4},{6,7},{7,6},{8,9},{9,8},{10,11... | collective-permute-start | bytes 786440 | tf_op jit(solution)/shard_map/ppermute | solution.py:392
  192.5 21.2 %collective-permute-start.34 = (bf16[128,1024]{1,0:T(8,128)(2,1)S(1)}, bf16[128,1024]{1,0:T(8,128)(2,1)S(1)}, u32[]{:S(2)}, u32[]{:S(2)}) collective-permute-start(bf16[128,1024]{1,0:T(8,128)(2,1)S(1)} %copy-done.44), channel_id=1, source_target_pairs={{0,2},{1,3},{2,0},{3,1},{4,6},{5,7},{6,4},{7,5},{8,10},{9,11},{10,... | collective-permute-start | bytes 786440 | tf_op jit(solution)/shard_map/ppermute | solution.py:392
  193.9 24.3 %collective-permute-start.42 = (bf16[128,1024]{1,0:T(8,128)(2,1)S(1)}, bf16[128,1024]{1,0:T(8,128)(2,1)S(1)}, u32[]{:S(2)}, u32[]{:S(2)}) collective-permute-start(bf16[128,1024]{1,0:T(8,128)(2,1)S(1)} %collective-permute-done.36.refs_1_), channel_id=1, source_target_pairs={{0,2},{1,3},{2,0},{3,1},{4,6},{5,7},{6,4},{7,5},{8,10},{9,11},{10,... | collective-permute-start | bytes 786440 | tf_op jit(solution)/shard_map/ppermute | solution.py:392
  225.4 18.0 %collective-permute-start.39 = (bf16[128,1024]{1,0:T(8,128)(2,1)}, bf16[128,1024]{1,0:T(8,128)(2,1)S(1)}, u32[]{:S(2)}, u32[]{:S(2)}) collective-permute-start(bf16[128,1024]{1,0:T(8,128)(2,1)} %get-tuple-element.121), channel_id=1, source_target_pairs={{0,1},{1,0},{2,3},{3,2},{4,5},{5,4},{6,7},{7,6},{8,9},{9,8},{10,11... | collective-permute-start | bytes 786440 | tf_op jit(solution)/shard_map/ppermute | solution.py:392
  225.4 28.3 %collective-permute-start.40 = (bf16[128,1024]{1,0:T(8,128)(2,1)}, bf16[128,1024]{1,0:T(8,128)(2,1)S(1)}, u32[]{:S(2)}, u32[]{:S(2)}) collective-permute-start(bf16[128,1024]{1,0:T(8,128)(2,1)} %get-tuple-element.122), channel_id=1, source_target_pairs={{0,2},{1,3},{2,0},{3,1},{4,6},{5,7},{6,4},{7,5},{8,10},{9,11},{10,... | collective-permute-start | bytes 786440 | tf_op jit(solution)/shard_map/ppermute | solution.py:392
  228.2 25.5 %collective-permute-start.41 = (bf16[128,1024]{1,0:T(8,128)(2,1)}, bf16[128,1024]{1,0:T(8,128)(2,1)S(1)}, u32[]{:S(2)}, u32[]{:S(2)}) collective-permute-start(bf16[128,1024]{1,0:T(8,128)(2,1)} %get-tuple-element.123), channel_id=1, source_target_pairs={{0,3},{1,2},{2,1},{3,0},{4,7},{5,6},{6,5},{7,4},{8,11},{9,10},{10,... | collective-permute-start | bytes 786440 | tf_op jit(solution)/shard_map/ppermute | solution.py:392
  231.1 25.9 %collective-permute-start.44 = (bf16[160,768]{1,0:T(8,128)(2,1)S(1)}, bf16[160,768]{1,0:T(8,128)(2,1)S(1)}, u32[]{:S(2)}, u32[]{:S(2)}) collective-permute-start(bf16[160,768]{1,0:T(8,128)(2,1)S(1)} %get-tuple-element.134), channel_id=1, source_target_pairs={{0,4},{4,0},{1,5},{5,1},{2,6},{6,2},{3,7},{7,3},{8,12},{12,8},{9,1... | collective-permute-start | bytes 737288 | tf_op jit(solution)/shard_map/ppermute | solution.py:415
  234.9 22.2 %collective-permute-start.45 = (bf16[160,768]{1,0:T(8,128)(2,1)S(1)}, bf16[160,768]{1,0:T(8,128)(2,1)S(1)}, u32[]{:S(2)}, u32[]{:S(2)}) collective-permute-start(bf16[160,768]{1,0:T(8,128)(2,1)S(1)} %get-tuple-element.136), channel_id=1, source_target_pairs={{0,16},{8,24},{16,0},{24,8},{1,17},{9,25},{17,1},{25,9},{2,18},{10... | collective-permute-start | bytes 737288 | tf_op jit(solution)/shard_map/ppermute | solution.py:423
  (80 other events, 657.3 us)
Sparse Core Ops, SparseCore 0:
  10.2 91.9 all-gather.2
  164.4 101.2 reduce-scatter.1

commit v6 on v5

--- a/solution.py
+++ b/solution.py
@@ -568,7 +568,7 @@
     out_w = jnp.concatenate(spread(after(w_out, wa)), axis=1)
     cots = [cot] + spread(after(cot, kv))[1:]
     oa, ob = plane_gather(after(out_w, kvs[-1]), fancy, near=True, first=())
-    mine = collect([mixed[0], *after_all(mixed[1:], cots[1:])])
+    mine = collect([mixed[0], *after_all(mixed[1:], cots[1:3])])
     oa, ob = (oa, swap_core(after(oa, *mine))) if fancy else (oa, ob)
     middle, second = whole_call(
         functools.partial(middle_kernel, n),

time: 282 us -> 287 us (1.018)
    ppermute x36, waiting for transfers between devices: 58 us -> 49.5 us  [across(): lax.ppermute(v, 'tensor', [(i, i ^ j) for i in range(lax.axis_size('tenso...]
    ppermute x36, starting transfers between devices: 64.8 us -> 60 us  [across(): lax.ppermute(v, 'tensor', [(i, i ^ j) for i in range(lax.axis_size('tenso...]
    ppermute x5, starting transfers between devices: 5.74 us -> 9.34 us  [swap_x(): return lax.ppermute(v, 'seq', [(0, 1), (1, 0)])]
    ppermute x3, waiting for transfers between devices: 6.53 us -> 9.77 us  [swap_xy(): return lax.ppermute(v, ('dp', 'seq'), [(i, i ^ 5) for i in range(8)])]
    ppermute x3, starting transfers between devices: 1.84 us -> 4.89 us  [swap_xy(): return lax.ppermute(v, ('dp', 'seq'), [(i, i ^ 5) for i in range(8)])]
    ppermute x3, waiting for transfers between devices: 1.85 us -> 4.74 us  [swap_y(): return lax.ppermute(v, 'dp', [(i, i ^ 2) for i in range(4)])]
    unnamed x106 -> x110, local copies, waits for them, and re-layouts: 6.7 us -> 8.06 us
  transfers between devices with their start and end apart: 52 -> 52, of which waited for: 21 -> 24; matrix products, arithmetic and copies ran while one was open for 5% -> 5% of each run, Pallas kernels for 28% -> 28%
where the time goes in v6:
time: 287 us; the launch traced here: 286 us
  Pallas kernels  92.2 us (32%)
  starting transfers between devices  77.5 us (27%)
  waiting for transfers between devices  72.3 us (25%)
  local copies, waits for them, and re-layouts  15.7 us (5%)
  between operations  14.7 us (5%)
  other arithmetic  13.1 us (5%)
    ppermute x36, starting transfers between devices, across(): lax.ppermute(v, 'tensor', [(i, i ^ j) for i in range(lax.axis_size('tenso...  60 us
    pallas_call x10, Pallas kernels, whole_call(): pl.pallas_call(body, out_shape=outs, grid_spec=pltpu.PrefetchScalarGridSp...  51.2 us
    ppermute x36, waiting for transfers between devices, across(): lax.ppermute(v, 'tensor', [(i, i ^ j) for i in range(lax.axis_size('tenso...  49.5 us
    pallas_call x2, Pallas kernels, expert_call(): pl.pallas_call(functools.partial(expert_kernel, parts, bool(begun)), out_...  25.6 us
    pallas_call x1, Pallas kernels, per_device(): pl.pallas_call(functools.partial(expert_back_kernel, n), out_shape=tuple(...  15.4 us
    ppermute x3, waiting for transfers between devices, swap_xy(): return lax.ppermute(v, ('dp', 'seq'), [(i, i ^ 5) for i in range(8)])  9.77 us
    ppermute x5, starting transfers between devices, swap_x(): return lax.ppermute(v, 'seq', [(0, 1), (1, 0)])  9.34 us
    unnamed x110, local copies, waits for them, and re-layouts  8.06 us
  transfers between devices with their start and end apart: 52, of which 24 were waited for; matrix products, arithmetic and copies ran while one was open for 5% of the time, Pallas kernels for 28%

profile of v6, /device:TPU:0, one launch (start us, length us, event | category | flops | bytes accessed | tf_op | source)
XLA Modules:
  0.0 285.9 jit_solution(14640220062588299035)
XLA Ops:
  16.9 3.5 %collective-permute-start.11 = (bf16[128,1024]{1,0:T(8,128)(2,1)S(1)}, bf16[128,1024]{1,0:T(8,128)(2,1)S(1)}, u32[]{:S(2)}, u32[]{:S(2)}) collective-permute-start(bf16[128,1024]{1,0:T(8,128)(2,1)S(1)} %bitcast.77), channel_id=1, source_target_pairs={{0,2},{1,3},{2,0},{3,1},{4,6},{5,7},{6,4},{7,5},{8,10},{9,11},{10,... | collective-permute-start | bytes 786440 | tf_op jit(solution)/shard_map/ppermute | solution.py:392
  26.3 5.2 %collective-permute-done.3 = bf16[144,512]{1,0:T(8,128)(2,1)S(1)} collective-permute-done((bf16[144,512]{1,0:T(8,128)(2,1)S(1)}, bf16[144,512]{1,0:T(8,128)(2,1)S(1)}, u32[]{:S(2)}, u32[]{:S(2)}) %collective-permute-start.3) | collective-permute-done | bytes 147488 | tf_op jit(solution)/shard_map/ppermute | solution.py:415
  33.4 3.9 %collective-permute-done.5 = bf16[144,512]{1,0:T(8,128)(2,1)S(1)} collective-permute-done((bf16[144,512]{1,0:T(8,128)(2,1)S(1)}, bf16[144,512]{1,0:T(8,128)(2,1)S(1)}, u32[]{:S(2)}, u32[]{:S(2)}) %collective-permute-start.5) | collective-permute-done | bytes 147488 | tf_op jit(solution)/shard_map/ppermute | solution.py:427
  42.5 4.5 %shard_map.247 = (bf16[512,1024]{1,0:T(8,128)(2,1)}, bf16[512,256]{1,0:T(8,128)(2,1)}, bf16[512,256]{1,0:T(8,128)(2,1)}) custom-call(s32[8]{0:T(128)} %copy-done.38, bf16[128,1024]{1,0:T(8,128)(2,1)} %bitcast.72, bf16[128,1024]{1,0:T(8,128)(2,1)} %copy-done.10, bf16[128,1024]{1,0:T(8,128)(2,1)} %copy-done.11, bf16[128,1024]{1,0:T(8,128)(2,1)} %copy-done.12, ...), custom_call_target="tpu_custom_call" | custom-call | tf_op jit(solution)/shard_map/pallas_call | solution.py:39
  54.1 3.6 %collective-permute-done.8 = bf16[128,256]{1,0:T(8,128)(2,1)S(1)} collective-permute-done((bf16[128,256]{1,0:T(8,128)(2,1)S(1)}, bf16[128,256]{1,0:T(8,128)(2,1)S(1)}, u32[]{:S(2)}, u32[]{:S(2)}) %collective-permute-start.8) | collective-permute-done | bytes 65568 | tf_op jit(solution)/shard_map/ppermute | solution.py:392
  65.0 9.0 %shard_map.248 = (bf16[128,256]{1,0:T(8,128)(2,1)}, bf16[128,256]{1,0:T(8,128)(2,1)}, bf16[128,256]{1,0:T(8,128)(2,1)}, bf16[128,256]{1,0:T(8,128)(2,1)}, f32[4,64,512]{2,1,0:T(8,128)}, /*index=5*/f32[4,1,512]{2,1,0:T(1,128)}) custom-call(bf16[512,256]{1,0:T(8,128)(2,1)} %get-tuple-element.76.q, s32[1,512]{1,0:T(1,128)} %max.10.lim, ...), custom_call_target="tpu_custom_call" | custom-call | flops 10000000000 | tf_op jit(solution)/shard_map/pallas_call | solution.py:39
  81.4 5.4 %collective-permute-done.16 = bf16[128,1024]{1,0:T(8,128)(2,1)S(1)} collective-permute-done((bf16[128,1024]{1,0:T(8,128)(2,1)S(1)}, bf16[128,1024]{1,0:T(8,128)(2,1)S(1)}, u32[]{:S(2)}, u32[]{:S(2)}) %collective-permute-start.16) | collective-permute-done | bytes 262176 | tf_op jit(solution)/shard_map/ppermute | solution.py:427
  92.2 4.3 %shard_map.249 = (f32[128,1024]{1,0:T(8,128)}, bf16[128,1024]{1,0:T(8,128)(2,1)}) custom-call(s32[8]{0:T(128)} %copy-done.38, bf16[128,1024]{1,0:T(8,128)(2,1)} %bitcast.73, f32[1,1024]{1,0:T(1,128)} %reshape.269.gain, bf16[4,128,1024]{2,1,0:T(8,128)(2,1)} %copy-done, bf16[4,128,1024]{2,1,0:T(8,128)(2,1)} %copy-done.2, ...), custom_call_target="tpu_custom_call" | custom-call | tf_op jit(solution)/shard_map/pallas_call | solution.py:39
  106.2 12.8 %shard_map.250 = (bf16[128,1024]{1,0:T(8,128)(2,1)}, bf16[128,1024]{1,0:T(8,128)(2,1)}, bf16[512,2048]{1,0:T(8,128)(2,1)}, bf16[512,2048]{1,0:T(8,128)(2,1)}, bf...) custom-call(f32[256,16]{1,0:T(8,128)} %get-tuple-element.145.chosen, f32[256,16]{1,0:T(8,128)} %get-tuple-element.144.kept, ...), custom_call_target="tpu_custom_call" | custom-call | flops 10000000000 | tf_op jit(solution)/shard_map/pallas_call | solution.py:592
  119.0 11.9 %collective-permute-done.23.refs_0_.refs_2_ = bf16[128,1024]{1,0:T(8,128)(2,1)S(1)} collective-permute-done((bf16[128,1024]{1,0:T(8,128)(2,1)}, bf16[128,1024]{1,0:T(8,128)(2,1)S(1)}, u32[]{:S(2)}, u32[]{:S(2)}) %collective-permute-start.23) | collective-permute-done | bytes 262176 | tf_op jit(solution)/shard_map/ppermute | solution.py:392
  131.7 12.8 %shard_map.251 = (bf16[128,1024]{1,0:T(8,128)(2,1)}, bf16[128,1024]{1,0:T(8,128)(2,1)}, bf16[512,2048]{1,0:T(8,128)(2,1)}, bf16[512,2048]{1,0:T(8,128)(2,1)}, bf...) custom-call(f32[256,16]{1,0:T(8,128)} %get-tuple-element.147.chosen, ...), custom_call_target="tpu_custom_call", output_to_operand_aliasing={{2}: (9, {}), {3}: (10, {}), {4}: (11, {})} | custom-call | tf_op jit(solution)/shard_map/pallas_call | solution.py:592
  144.5 4.8 %collective-permute-start.28 = (bf16[128,1024]{1,0:T(8,128)(2,1)}, bf16[128,1024]{1,0:T(8,128)(2,1)S(1)}, u32[]{:S(2)}, u32[]{:S(2)}) collective-permute-start(bf16[128,1024]{1,0:T(8,128)(2,1)} %get-tuple-element.101), channel_id=1, source_target_pairs={{0,2},{1,3},{2,0},{3,1},{4,6},{5,7},{6,4},{7,5},{8,10},{9,11},{10,... | collective-permute-start | bytes 786440 | tf_op jit(solution)/shard_map/ppermute | solution.py:392
  151.9 15.4 %shard_map.252 = (bf16[128,1024]{1,0:T(8,128)(2,1)}, bf16[128,1024]{1,0:T(8,128)(2,1)}, bf16[128,1024]{1,0:T(8,128)(2,1)}, bf16[128,1024]{1,0:T(8,128)(2,1)}, bf16[8,3,16,128,128]{4,3,2,1,0:T(8,128)(2,1)}) custom-call(bf16[512,2048]{1,0:T(8,128)(2,1)} %get-tuple-element.92.active, bf16[512,2048]{1,0:T(8,128)(2,1)} %get-tuple-element.93.gate, ...), custom_call_target="tpu_custom_call" | custom-call | tf_op jit(solution)/shard_map/pallas_call | solution.py:630
  168.8 4.2 %shard_map.253 = (f32[128,1024]{1,0:T(8,128)}, bf16[128,1024]{1,0:T(8,128)(2,1)}, f32[1,1024]{1,0:T(1,128)}, bf16[128,256]{1,0:T(8,128)(2,1)}, bf16[128,256]{1,0...) custom-call(s32[8]{0:T(128)} %copy-done.38, f32[128,1024]{1,0:T(8,128)} %get-tuple-element.86.middle, ...), custom_call_target="tpu_custom_call" | custom-call | tf_op jit(solution)/shard_map/pallas_call | solution.py:39
  173.0 4.8 %collective-permute-start.30 = (bf16[128,256]{1,0:T(8,128)(2,1)}, bf16[128,256]{1,0:T(8,128)(2,1)S(1)}, u32[]{:S(2)}, u32[]{:S(2)}) collective-permute-start(bf16[128,256]{1,0:T(8,128)(2,1)} %get-tuple-element.104), channel_id=1, source_target_pairs={{0,1},{1,0},{2,3},{3,2},{4,5},{5,4},{6,7},{7,6},{8,9},{9,8},{10,11... | collective-permute-start | bytes 196616 | tf_op jit(solution)/shard_map/ppermute | solution.py:392
  180.8 3.5 %collective-permute-done.31.refs_2_ = bf16[128,256]{1,0:T(8,128)(2,1)S(1)} collective-permute-done((bf16[128,256]{1,0:T(8,128)(2,1)}, bf16[128,256]{1,0:T(8,128)(2,1)S(1)}, u32[]{:S(2)}, u32[]{:S(2)}) %collective-permute-start.31) | collective-permute-done | bytes 65568 | tf_op jit(solution)/shard_map/ppermute | solution.py:392
  187.8 7.0 %shard_map.255 = (bf16[512,256]{1,0:T(8,128)(2,1)}, f32[4,64,512]{2,1,0:T(8,128)}) custom-call(bf16[512,256]{1,0:T(8,128)(2,1)} %get-tuple-element.76.q, s32[1,512]{1,0:T(1,128)} %max.10.lim, bf16[512,256]{1,0:T(8,128)(2,1)} %copy-done.44, s32[512,1]{1,0:T(8,128)} %broadcast_add_fusion.refs_3_.kpos, f32[4,1,512]{2,1,0:T(1,128)} %get-tuple-element.111.lse, ...), custom_call_target="tpu_custom_call" | custom-call | flops 10000000000 | tf_op jit(solution)/shard_map/pallas_call | solution.py:39
  200.7 8.1 %shard_map.256 = (f32[512,256]{1,0:T(8,128)}, bf16[512,256]{1,0:T(8,128)(2,1)}) custom-call(bf16[512,256]{1,0:T(8,128)(2,1)} %get-tuple-element.76.q, s32[1,512]{1,0:T(1,128)} %max.10.lim, bf16[512,256]{1,0:T(8,128)(2,1)} %get-tuple-element.74.refs_0_.kv, s32[512,1]{1,0:T(8,128)} %copy-done.13, f32[4,1,512]{2,1,0:T(1,128)} %get-tuple-element.111.lse, ...), custom_call_target="tpu_custom_call" | custom-call | flops 10000000000 | tf_op jit(solution)/shard_map/pallas_call | solution.py:39
  209.5 4.7 %shard_map.257 = (bf16[128,1024]{1,0:T(8,128)(2,1)}, bf16[128,1024]{1,0:T(8,128)(2,1)}, bf16[128,1024]{1,0:T(8,128)(2,1)}, bf16[128,1024]{1,0:T(8,128)(2,1)}, bf...) custom-call(s32[8]{0:T(128)} %copy-done.38, bf16[512,256]{1,0:T(8,128)(2,1)} %get-tuple-element.117.dq, ...), custom_call_target="tpu_custom_call" | custom-call | tf_op jit(solution)/shard_map/pallas_call | solution.py:39
  214.2 4.9 %collective-permute-done.34.refs_2_ = bf16[128,1024]{1,0:T(8,128)(2,1)S(1)} collective-permute-done((bf16[128,1024]{1,0:T(8,128)(2,1)S(1)}, bf16[128,1024]{1,0:T(8,128)(2,1)S(1)}, u32[]{:S(2)}, u32[]{:S(2)}) %collective-permute-start.34) | collective-permute-done | bytes 262176 | tf_op jit(solution)/shard_map/ppermute | solution.py:392
  223.2 4.8 %shard_map.259 = (bf16[4,160,768]{2,1,0:T(8,128)(2,1)}, bf16[4,160,768]{2,1,0:T(8,128)(2,1)}) custom-call(s32[8]{0:T(128)} %copy-done.38, bf16[512,1024]{1,0:T(8,128)(2,1)} %get-tuple-element.124.x1, bf16[512,512]{1,0:T(8,128)(2,1)} %get-tuple-element.126.grads, f32[16,1024]{1,0:T(8,128)} %get-tuple-element.127.router_part, ...), custom_call_target="tpu_custom_call" | custom-call | tf_op jit(solution)/shard_map/pallas_call | solution.py:39
  240.7 6.6 %collective-permute-done.39.refs_1_ = bf16[128,1024]{1,0:T(8,128)(2,1)S(1)} collective-permute-done((bf16[128,1024]{1,0:T(8,128)(2,1)}, bf16[128,1024]{1,0:T(8,128)(2,1)S(1)}, u32[]{:S(2)}, u32[]{:S(2)}) %collective-permute-start.39) | collective-permute-done | bytes 262176 | tf_op jit(solution)/shard_map/ppermute | solution.py:392
  252.5 5.9 %collective-permute-done.40.refs_2_ = bf16[128,1024]{1,0:T(8,128)(2,1)S(1)} collective-permute-done((bf16[128,1024]{1,0:T(8,128)(2,1)}, bf16[128,1024]{1,0:T(8,128)(2,1)S(1)}, u32[]{:S(2)}, u32[]{:S(2)}) %collective-permute-start.40) | collective-permute-done | bytes 262176 | tf_op jit(solution)/shard_map/ppermute | solution.py:392
  263.3 5.1 %collective-permute-start.47 = (f32[18,128]{1,0:T(8,128)S(1)}, f32[18,128]{1,0:T(8,128)S(1)}, u32[]{:S(2)}, u32[]{:S(2)}) collective-permute-start(f32[18,128]{1,0:T(8,128)S(1)} %slice.152), channel_id=1, source_target_pairs={{0,1},{1,0},{2,3},{3,2},{4,5},{5,4},{6,7},{7,6},{8,9},{9,8},{10,11... | collective-permute-start | bytes 27656 | tf_op jit(solution)/shard_map/ppermute | solution.py:392
  (258 shorter events, 114.6 us)
Async XLA Ops:
  7.2 98.3 %all-gather.3.cloned.1.call-start = ((), (), s32[]{:S(2)}) async-start(), calls=%async_computation.2 | async-start | bytes 14155776 | tf_op jit(solution)/shard_map/all_gather | solution.py:585
  10.0 265.9 %reduce-scatter.2.cloned.1.call-start = ((), (), s32[]{:S(2)}) async-start(), calls=%async_computation.1 | async-start | bytes 14155776 | tf_op jit(solution)/shard_map/reduce_scatter | solution.py:650
  16.0 25.5 %collective-permute-start.10 = (bf16[128,1024]{1,0:T(8,128)(2,1)S(1)}, bf16[128,1024]{1,0:T(8,128)(2,1)S(1)}, u32[]{:S(2)}, u32[]{:S(2)}) collective-permute-start(bf16[128,1024]{1,0:T(8,128)(2,1)S(1)} %bitcast.76), channel_id=1, source_target_pairs={{0,1},{1,0},{2,3},{3,2},{4,5},{5,4},{6,7},{7,6},{8,9},{9,8},{10,11... | collective-permute-start | bytes 786440 | tf_op jit(solution)/shard_map/ppermute | solution.py:392
  16.9 24.7 %collective-permute-start.11 = (bf16[128,1024]{1,0:T(8,128)(2,1)S(1)}, bf16[128,1024]{1,0:T(8,128)(2,1)S(1)}, u32[]{:S(2)}, u32[]{:S(2)}) collective-permute-start(bf16[128,1024]{1,0:T(8,128)(2,1)S(1)} %bitcast.77), channel_id=1, source_target_pairs={{0,2},{1,3},{2,0},{3,1},{4,6},{5,7},{6,4},{7,5},{8,10},{9,11},{10,... | collective-permute-start | bytes 786440 | tf_op jit(solution)/shard_map/ppermute | solution.py:392
  57.7 16.3 %collective-permute-start.17 = (bf16[128,1024]{1,0:T(8,128)(2,1)S(1)}, bf16[128,1024]{1,0:T(8,128)(2,1)S(1)}, u32[]{:S(2)}, u32[]{:S(2)}) collective-permute-start(bf16[128,1024]{1,0:T(8,128)(2,1)S(1)} %bitcast.83), channel_id=1, source_target_pairs={{0,1},{1,0},{2,3},{3,2},{4,5},{5,4},{6,7},{7,6},{8,9},{9,8},{10,11... | collective-permute-start | bytes 786440 | tf_op jit(solution)/shard_map/ppermute | solution.py:392
  59.1 15.0 %collective-permute-start.18 = (bf16[128,1024]{1,0:T(8,128)(2,1)S(1)}, bf16[128,1024]{1,0:T(8,128)(2,1)S(1)}, u32[]{:S(2)}, u32[]{:S(2)}) collective-permute-start(bf16[128,1024]{1,0:T(8,128)(2,1)S(1)} %bitcast.84), channel_id=1, source_target_pairs={{0,2},{1,3},{2,0},{3,1},{4,6},{5,7},{6,4},{7,5},{8,10},{9,11},{10,... | collective-permute-start | bytes 786440 | tf_op jit(solution)/shard_map/ppermute | solution.py:392
  61.2 15.1 %collective-permute-start.14 = (bf16[128,1024]{1,0:T(8,128)(2,1)S(1)}, bf16[128,1024]{1,0:T(8,128)(2,1)S(1)}, u32[]{:S(2)}, u32[]{:S(2)}) collective-permute-start(bf16[128,1024]{1,0:T(8,128)(2,1)S(1)} %pad_maximum_fusion.3), channel_id=1, source_target_pairs={{0,4},{4,0},{1,5},{5,1},{2,6},{6,2},{3,7},{7,3},{8,12},{12,8},{9,1... | collective-permute-start | bytes 786440 | tf_op jit(solution)/shard_map/ppermute | solution.py:415
  63.6 17.9 %collective-permute-start.15 = (bf16[128,1024]{1,0:T(8,128)(2,1)S(1)}, bf16[128,1024]{1,0:T(8,128)(2,1)S(1)}, u32[]{:S(2)}, u32[]{:S(2)}) collective-permute-start(bf16[128,1024]{1,0:T(8,128)(2,1)S(1)} %pad_maximum_fusion.3), channel_id=1, source_target_pairs={{0,16},{8,24},{16,0},{24,8},{1,17},{9,25},{17,1},{25,9},{2,18},{10... | collective-permute-start | bytes 786440 | tf_op jit(solution)/shard_map/ppermute | solution.py:423
  63.6 23.3 %collective-permute-start.16 = (bf16[128,1024]{1,0:T(8,128)(2,1)S(1)}, bf16[128,1024]{1,0:T(8,128)(2,1)S(1)}, u32[]{:S(2)}, u32[]{:S(2)}) collective-permute-start(bf16[128,1024]{1,0:T(8,128)(2,1)S(1)} %pad_maximum_fusion.3), channel_id=1, source_target_pairs={{0,20},{4,16},{8,28},{12,24},{16,4},{20,0},{24,12},{28,8},{1,21},{... | collective-permute-start | bytes 786440 | tf_op jit(solution)/shard_map/ppermute | solution.py:427
  98.1 20.9 %collective-permute-start.25 = (bf16[128,1024]{1,0:T(8,128)(2,1)S(1)}, bf16[128,1024]{1,0:T(8,128)(2,1)S(1)}, u32[]{:S(2)}, u32[]{:S(2)}) collective-permute-start(bf16[128,1024]{1,0:T(8,128)(2,1)S(1)} %bitcast.85), channel_id=1, source_target_pairs={{0,3},{1,2},{2,1},{3,0},{4,7},{5,6},{6,5},{7,4},{8,11},{9,10},{10,... | collective-permute-start | bytes 786440 | tf_op jit(solution)/shard_map/ppermute | solution.py:392
  101.3 29.5 %collective-permute-start.23 = (bf16[128,1024]{1,0:T(8,128)(2,1)}, bf16[128,1024]{1,0:T(8,128)(2,1)S(1)}, u32[]{:S(2)}, u32[]{:S(2)}) collective-permute-start(bf16[128,1024]{1,0:T(8,128)(2,1)} %get-tuple-element.87.refs_0_), channel_id=1, source_target_pairs={{0,2},{1,3},{2,0},{3,1},{4,6},{5,7},{6,4},{7,5},{8,10},{9,11},{10,... | collective-permute-start | bytes 786440 | tf_op jit(solution)/shard_map/ppermute | solution.py:392
  102.2 28.7 %collective-permute-start.24 = (bf16[128,1024]{1,0:T(8,128)(2,1)}, bf16[128,1024]{1,0:T(8,128)(2,1)S(1)}, u32[]{:S(2)}, u32[]{:S(2)}) collective-permute-start(bf16[128,1024]{1,0:T(8,128)(2,1)} %get-tuple-element.87.refs_0_), channel_id=1, source_target_pairs={{0,3},{1,2},{2,1},{3,0},{4,7},{5,6},{6,5},{7,4},{8,11},{9,10},{10,... | collective-permute-start | bytes 786440 | tf_op jit(solution)/shard_map/ppermute | solution.py:392
  144.5 23.5 %collective-permute-start.28 = (bf16[128,1024]{1,0:T(8,128)(2,1)}, bf16[128,1024]{1,0:T(8,128)(2,1)S(1)}, u32[]{:S(2)}, u32[]{:S(2)}) collective-permute-start(bf16[128,1024]{1,0:T(8,128)(2,1)} %get-tuple-element.101), channel_id=1, source_target_pairs={{0,2},{1,3},{2,0},{3,1},{4,6},{5,7},{6,4},{7,5},{8,10},{9,11},{10,... | collective-permute-start | bytes 786440 | tf_op jit(solution)/shard_map/ppermute | solution.py:392
  149.3 18.7 %collective-permute-start.29 = (bf16[128,1024]{1,0:T(8,128)(2,1)}, bf16[128,1024]{1,0:T(8,128)(2,1)S(1)}, u32[]{:S(2)}, u32[]{:S(2)}) collective-permute-start(bf16[128,1024]{1,0:T(8,128)(2,1)} %get-tuple-element.102), channel_id=1, source_target_pairs={{0,3},{1,2},{2,1},{3,0},{4,7},{5,6},{6,5},{7,4},{8,11},{9,10},{10,... | collective-permute-start | bytes 786440 | tf_op jit(solution)/shard_map/ppermute | solution.py:392
  151.9 16.0 %collective-permute-start.27 = (bf16[128,1024]{1,0:T(8,128)(2,1)S(1)}, bf16[128,1024]{1,0:T(8,128)(2,1)S(1)}, u32[]{:S(2)}, u32[]{:S(2)}) collective-permute-start(bf16[128,1024]{1,0:T(8,128)(2,1)S(1)} %copy-done.48), channel_id=1, source_target_pairs={{0,1},{1,0},{2,3},{3,2},{4,5},{5,4},{6,7},{7,6},{8,9},{9,8},{10,11... | collective-permute-start | bytes 786440 | tf_op jit(solution)/shard_map/ppermute | solution.py:392
  186.3 22.5 %collective-permute-start.37 = (bf16[128,1024]{1,0:T(8,128)(2,1)}, bf16[128,1024]{1,0:T(8,128)(2,1)S(1)}, u32[]{:S(2)}, u32[]{:S(2)}) collective-permute-start(bf16[128,1024]{1,0:T(8,128)(2,1)} %get-tuple-element.116.refs_0_), channel_id=1, source_target_pairs={{0,2},{1,3},{2,0},{3,1},{4,6},{5,7},{6,4},{7,5},{8,10},{9,11},{10,... | collective-permute-start | bytes 786440 | tf_op jit(solution)/shard_map/ppermute | solution.py:392
  196.6 17.7 %collective-permute-start.33 = (bf16[128,1024]{1,0:T(8,128)(2,1)S(1)}, bf16[128,1024]{1,0:T(8,128)(2,1)S(1)}, u32[]{:S(2)}, u32[]{:S(2)}) collective-permute-start(bf16[128,1024]{1,0:T(8,128)(2,1)S(1)} %copy-done.47), channel_id=1, source_target_pairs={{0,1},{1,0},{2,3},{3,2},{4,5},{5,4},{6,7},{7,6},{8,9},{9,8},{10,11... | collective-permute-start | bytes 786440 | tf_op jit(solution)/shard_map/ppermute | solution.py:392
  197.7 21.4 %collective-permute-start.34 = (bf16[128,1024]{1,0:T(8,128)(2,1)S(1)}, bf16[128,1024]{1,0:T(8,128)(2,1)S(1)}, u32[]{:S(2)}, u32[]{:S(2)}) collective-permute-start(bf16[128,1024]{1,0:T(8,128)(2,1)S(1)} %copy-done.46), channel_id=1, source_target_pairs={{0,2},{1,3},{2,0},{3,1},{4,6},{5,7},{6,4},{7,5},{8,10},{9,11},{10,... | collective-permute-start | bytes 786440 | tf_op jit(solution)/shard_map/ppermute | solution.py:392
  198.8 23.8 %collective-permute-start.42 = (bf16[128,1024]{1,0:T(8,128)(2,1)S(1)}, bf16[128,1024]{1,0:T(8,128)(2,1)S(1)}, u32[]{:S(2)}, u32[]{:S(2)}) collective-permute-start(bf16[128,1024]{1,0:T(8,128)(2,1)S(1)} %collective-permute-done.36.refs_1_), channel_id=1, source_target_pairs={{0,2},{1,3},{2,0},{3,1},{4,6},{5,7},{6,4},{7,5},{8,10},{9,11},{10,... | collective-permute-start | bytes 786440 | tf_op jit(solution)/shard_map/ppermute | solution.py:392
  229.8 17.5 %collective-permute-start.39 = (bf16[128,1024]{1,0:T(8,128)(2,1)}, bf16[128,1024]{1,0:T(8,128)(2,1)S(1)}, u32[]{:S(2)}, u32[]{:S(2)}) collective-permute-start(bf16[128,1024]{1,0:T(8,128)(2,1)} %get-tuple-element.121), channel_id=1, source_target_pairs={{0,1},{1,0},{2,3},{3,2},{4,5},{5,4},{6,7},{7,6},{8,9},{9,8},{10,11... | collective-permute-start | bytes 786440 | tf_op jit(solution)/shard_map/ppermute | solution.py:392
  229.8 28.6 %collective-permute-start.40 = (bf16[128,1024]{1,0:T(8,128)(2,1)}, bf16[128,1024]{1,0:T(8,128)(2,1)S(1)}, u32[]{:S(2)}, u32[]{:S(2)}) collective-permute-start(bf16[128,1024]{1,0:T(8,128)(2,1)} %get-tuple-element.122), channel_id=1, source_target_pairs={{0,2},{1,3},{2,0},{3,1},{4,6},{5,7},{6,4},{7,5},{8,10},{9,11},{10,... | collective-permute-start | bytes 786440 | tf_op jit(solution)/shard_map/ppermute | solution.py:392
  232.5 25.9 %collective-permute-start.41 = (bf16[128,1024]{1,0:T(8,128)(2,1)}, bf16[128,1024]{1,0:T(8,128)(2,1)S(1)}, u32[]{:S(2)}, u32[]{:S(2)}) collective-permute-start(bf16[128,1024]{1,0:T(8,128)(2,1)} %get-tuple-element.123), channel_id=1, source_target_pairs={{0,3},{1,2},{2,1},{3,0},{4,7},{5,6},{6,5},{7,4},{8,11},{9,10},{10,... | collective-permute-start | bytes 786440 | tf_op jit(solution)/shard_map/ppermute | solution.py:392
  235.6 26.1 %collective-permute-start.44 = (bf16[160,768]{1,0:T(8,128)(2,1)S(1)}, bf16[160,768]{1,0:T(8,128)(2,1)S(1)}, u32[]{:S(2)}, u32[]{:S(2)}) collective-permute-start(bf16[160,768]{1,0:T(8,128)(2,1)S(1)} %get-tuple-element.134), channel_id=1, source_target_pairs={{0,4},{4,0},{1,5},{5,1},{2,6},{6,2},{3,7},{7,3},{8,12},{12,8},{9,1... | collective-permute-start | bytes 737288 | tf_op jit(solution)/shard_map/ppermute | solution.py:415
  239.1 22.6 %collective-permute-start.45 = (bf16[160,768]{1,0:T(8,128)(2,1)S(1)}, bf16[160,768]{1,0:T(8,128)(2,1)S(1)}, u32[]{:S(2)}, u32[]{:S(2)}) collective-permute-start(bf16[160,768]{1,0:T(8,128)(2,1)S(1)} %get-tuple-element.136), channel_id=1, source_target_pairs={{0,16},{8,24},{16,0},{24,8},{1,17},{9,25},{17,1},{25,9},{2,18},{10... | collective-permute-start | bytes 737288 | tf_op jit(solution)/shard_map/ppermute | solution.py:423
  (82 other events, 665.2 us)
Sparse Core Ops, SparseCore 0:
  10.2 92.5 all-gather.2
  168.1 101.8 reduce-scatter.1
